TPU v7x, 32 devices: a whole 2x2x4 slice. The times are simulated.
32 devices in a mesh: dev: 32 (over z, y, x, core).
Axes of the slice: x: 2, y: 2, z: 4, core: 2. Of those that a mesh axis runs over, the one named last changes fastest.
Arguments:
- states: bfloat16 [4096, 1024], P('dev'), may hold values from -400 to 400
- bucket_sizes: int32 [32], P('dev'), may hold values from 1 to 96, 1792 in all
Outputs:
- log_density: float32 [4096], P('dev')
- neighbour_mean: bfloat16 [4096, 1024], P('dev')
Inputs may be any that keep to these rules, and one draw needn't show every extreme that they name: `bucket_sizes`: every block holds at least one and at most 96 live states, and some block holds exactly 96.
All inputs are finite; a program needn't handle non-finite values.
Results may differ from a plain program's by a relative error of at most 0.009.
Values may be sent and summed in bfloat16 or wider, within the bound.
No kernel may reach another device: no remote copies, remote signals or barrier semaphores. Data moves between devices by JAX's collectives and lax.ppermute only.
A program may use at most 64 MiB of HBM per device.

v0:
```python
import math

import jax
import jax.numpy as jnp
from jax import lax
from jax.sharding import PartitionSpec as P

EPS = 1e-06
RIDGE = 1.0


def swapped(value, axis, bit):
    mask = 2**bit
    pairs = [(source, source ^ mask) for source in range(lax.axis_size(axis))]
    return lax.ppermute(value, axis, pairs)


def inverse_lengths(rows_white):
    return lax.rsqrt(
        jnp.einsum("rd,rd->r", rows_white, rows_white, preferred_element_type=jnp.float32) + EPS
    )


def tile_terms(query_white, query_norm, query_rows, key_white, key_live, key_rows, sharpness):
    key_norm = inverse_lengths(key_white)
    inner_prod = jnp.einsum("qd,kd->qk", query_white, key_white, preferred_element_type=jnp.float32)
    scores = sharpness * (query_norm[:, None] * key_norm[None, :] * inner_prod - 1.0)
    not_self = (query_rows[:, None] != key_rows[None, :]).astype(jnp.float32)
    weights = jnp.exp(scores) * key_live.astype(jnp.float32)[None, :] * not_self
    part_density = jnp.sum(weights, axis=1)
    part_sum = jnp.dot(weights.astype(jnp.bfloat16), key_white, preferred_element_type=jnp.float32)
    return (part_density, part_sum)


def join_halves(own_parts, peer_parts, upper_half):
    return tuple(
        (
            jnp.where(
                upper_half,
                jnp.concatenate([peer_part, own_part], axis=0),
                jnp.concatenate([own_part, peer_part], axis=0),
            )
            for own_part, peer_part in zip(own_parts, peer_parts)
        )
    )


def shards(states, bucket_sizes):
    row_count, feature_dim = states.shape
    block_count = bucket_sizes.shape[0]
    block_rows = row_count // block_count
    device = lax.axis_index("dev")
    in_block = jnp.arange(block_rows, dtype=jnp.int32)
    live_grid = (in_block[None, :] < bucket_sizes[:, None]).astype(jnp.float32)
    live_mask = live_grid.reshape(row_count)
    local_count = jnp.sum(bucket_sizes).astype(jnp.float32)
    widened = states.astype(jnp.float32)
    masked = widened * live_mask[:, None]
    identity = RIDGE * jnp.eye(feature_dim, dtype=jnp.float32)
    state_sum, live_count = lax.psum((jnp.sum(masked, axis=0), local_count), "dev")
    mean_vec = state_sum / live_count
    centred = (widened - mean_vec) * live_mask[:, None]
    gram_matrix = lax.psum(jnp.dot(centred.T, centred, precision=lax.Precision.HIGHEST), "dev")
    covariance = gram_matrix / live_count + identity
    factor = jnp.linalg.cholesky(covariance)
    white = jax.scipy.linalg.solve_triangular(factor, (widened - mean_vec).T, lower=True).T.astype(
        jnp.bfloat16
    )
    local_rows = block_count * block_rows
    query_white = white.reshape(block_count, block_rows, feature_dim).reshape(
        local_rows, feature_dim
    )
    query_live = live_grid.reshape(local_rows)
    live_wire = query_live.astype(jnp.bfloat16)
    sharpness = 2.0 * math.sqrt(feature_dim)
    device_bits = lax.axis_size("dev").bit_length() - 1
    query_bits = device_bits // 2
    group_size = 1 << query_bits
    group_white, group_live = (query_white, live_wire)
    for bit_index in range(query_bits):
        peer_white, peer_live = swapped((group_white, group_live), "dev", bit_index)
        upper_half = device // (1 << bit_index) % 2 == 1
        group_white, group_live = join_halves(
            (group_white, group_live), (peer_white, peer_live), upper_half
        )
    group_index = jnp.arange(group_white.shape[0], dtype=jnp.int32)
    group_first = device // group_size * group_size * block_count
    group_rows = (group_first + group_index // block_rows) * block_rows + group_index % block_rows
    group_norm = inverse_lengths(group_white)
    key_white, key_live = (query_white, live_wire)
    for bit_index in range(query_bits, device_bits):
        peer_white, peer_live = swapped((key_white, key_live), "dev", bit_index)
        upper_half = device // (1 << bit_index) % 2 == 1
        key_white, key_live = join_halves(
            (key_white, key_live), (peer_white, peer_live), upper_half
        )
    key_total = key_white.shape[0]
    key_index = jnp.arange(key_total, dtype=jnp.int32)
    key_device = key_index // local_rows * group_size + device % group_size
    within_rows = key_index % local_rows
    key_rows = (
        key_device * block_count + within_rows // block_rows
    ) * block_rows + within_rows % block_rows
    key_step = math.gcd(key_total, 512)
    block_total = key_total // key_step

    def add_block(totals, key_block):
        part_density, part_sum = tile_terms(
            group_white, group_norm, group_rows, key_block[0], key_block[1], key_block[2], sharpness
        )
        return ((totals[0] + part_density, totals[1] + part_sum), None)

    group_start = (
        jnp.zeros((group_white.shape[0],), jnp.float32),
        jnp.zeros((group_white.shape[0], feature_dim), jnp.float32),
    )
    key_blocks = (
        key_white.reshape(block_total, key_step, feature_dim),
        key_live.reshape(block_total, key_step),
        key_rows.reshape(block_total, key_step),
    )
    (density, neighbour_sum), _ = lax.scan(add_block, group_start, key_blocks)
    for bit_index in reversed(range(query_bits)):
        half_rows = density.shape[0] // 2
        upper_half = device // (1 << bit_index) % 2 == 1
        send_part = (
            jnp.where(upper_half, density[:half_rows], density[half_rows:]),
            jnp.where(upper_half, neighbour_sum[:half_rows], neighbour_sum[half_rows:]),
        )
        keep_density = jnp.where(upper_half, density[half_rows:], density[:half_rows])
        keep_sum = jnp.where(upper_half, neighbour_sum[half_rows:], neighbour_sum[:half_rows])
        peer_density, peer_sum = (
            swapped(send_part[0].astype(jnp.bfloat16), "dev", bit_index).astype(jnp.float32),
            swapped(send_part[1].astype(jnp.bfloat16), "dev", bit_index).astype(jnp.float32),
        )
        density = keep_density + peer_density
        neighbour_sum = keep_sum + peer_sum
    is_live = query_live > 0.5
    log_part = jnp.where(is_live, jnp.log(density), 0.0).astype(jnp.float32)
    mean_part = jnp.where(is_live[:, None], neighbour_sum / density[:, None], 0.0).astype(
        jnp.bfloat16
    )
    log_density = log_part.reshape(block_count, block_rows).reshape(row_count)
    neighbour_mean = mean_part.reshape(block_count, block_rows, feature_dim).reshape(
        row_count, feature_dim
    )
    return (log_density, neighbour_mean)


def solution(mesh):
    placed = (P("dev", None), P("dev"))
    return jax.shard_map(
        shards, mesh=mesh, in_specs=placed, out_specs=(P("dev"), P("dev", None)), check_vma=False
    )
```

profile of v0, /device:TPU:0, one launch (start us, length us, event | category | flops | bytes accessed | tf_op | source)
XLA Modules:
  0.0 662.3 jit_solution(5386567911546569111)
XLA Ops:
  8.9 42.1 %all-reduce.1 = (f32[1024]{0:T(1024)S(1)}, f32[]{:T(128)}) all-reduce(f32[1024]{0:T(1024)S(1)} %fusion.40, f32[]{:T(128)S(6)} %convert_element_type.70), channel_id=1, replica_groups=mesh['dev'=32] {'dev'}, use_global_device_ids=true, to_apply=%region_1.0 | all-reduce | flops 1025 | bytes 8200 | tf_op jit(solution)/shard_map/psum | solution.py:60
  51.7 6.7 %fusion.38 = f32[1024,1024]{0,1:T(8,128)} fusion(bf16[128,1024]{1,0:T(8,128)(2,1)} %param.4, f32[1024]{0:T(1024)S(1)} %broadcast_divide_fusion, f32[128]{0:T(128)S(1)} %compare_convert_fusion), kind=kOutput, calls=%fused_computation.88 | convolution fusion | flops 1611005952 | bytes 4461056 | tf_op jit(solution)/shard_map/dot_general | solution.py:63
  58.5 141.9 %all-reduce.4.cloned.1.call-done = f32[1024,1024]{0,1:T(8,128)} async-done(((f32[1024,1024]{0,1:T(8,128)}), f32[1024,1024]{0,1:T(8,128)}) %all-reduce.4.cloned.1.call-update) | async-done | bytes 4194320 | tf_op jit(solution)/shard_map/psum | solution.py:63
  200.4 5.7 convert_add_fusion
  206.0 5.5 copy.5
  211.5 5.1 fusion.26
  218.6 11.7 %cholesky.223 = f32[128,128]{1,0:T(8,128)S(1)} custom-call(f32[128,128]{1,0:T(8,128)S(1)} %cholesky.580), custom_call_target="Cholesky" | custom-call | tf_op jit(solution)/shard_map/jit(cholesky)/cholesky | solution.py:65
  230.3 9.8 %custom-call.63 = f32[1,128,128]{1,2,0:T(8,128)S(1)} custom-call(f32[1,128,128]{2,1,0:T(8,128)S(1)} %get-tuple-element.244), custom_call_target="InvertDiagBlocksLowerTriangular" | custom-call | tf_op jit(solution)/shard_map/jit(cholesky)/cholesky | solution.py:65
  240.2 2.5 cholesky.255
  242.7 2.4 constant_dynamic-update-slice_fusion.32
  246.6 11.9 %cholesky.244 = f32[128,128]{1,0:T(8,128)S(1)} custom-call(f32[128,128]{1,0:T(8,128)S(1)} %cholesky.584), custom_call_target="Cholesky" | custom-call | tf_op jit(solution)/shard_map/jit(cholesky)/cholesky | solution.py:65
  259.1 9.8 %custom-call.64 = f32[1,128,128]{1,2,0:T(8,128)S(1)} custom-call(f32[1,128,128]{2,1,0:T(8,128)S(1)} %get-tuple-element.241), custom_call_target="InvertDiagBlocksLowerTriangular" | custom-call | tf_op jit(solution)/shard_map/jit(cholesky)/cholesky | solution.py:65
  272.3 11.7 %cholesky.468 = f32[128,128]{1,0:T(8,128)S(1)} custom-call(f32[128,128]{1,0:T(8,128)S(1)} %cholesky.589), custom_call_target="Cholesky" | custom-call | tf_op jit(solution)/shard_map/jit(cholesky)/cholesky | solution.py:65
  285.3 9.8 %custom-call.65 = f32[1,128,128]{1,2,0:T(8,128)S(1)} custom-call(f32[1,128,128]{2,1,0:T(8,128)S(1)} %get-tuple-element.238), custom_call_target="InvertDiagBlocksLowerTriangular" | custom-call | tf_op jit(solution)/shard_map/jit(cholesky)/cholesky | solution.py:65
  296.3 2.3 convolution_subtract_fusion.2
  298.6 12.1 %cholesky.487 = f32[128,128]{1,0:T(8,128)S(1)} custom-call(f32[128,128]{1,0:T(8,128)S(1)} %cholesky.594), custom_call_target="Cholesky" | custom-call | tf_op jit(solution)/shard_map/jit(cholesky)/cholesky | solution.py:65
  312.0 9.8 %custom-call.66 = f32[1,128,128]{1,2,0:T(8,128)S(1)} custom-call(f32[1,128,128]{2,1,0:T(8,128)S(1)} %get-tuple-element.235), custom_call_target="InvertDiagBlocksLowerTriangular" | custom-call | tf_op jit(solution)/shard_map/jit(cholesky)/cholesky | solution.py:65
  322.9 2.3 convolution_subtract_fusion.3
  325.3 11.7 %cholesky.506 = f32[128,128]{1,0:T(8,128)S(1)} custom-call(f32[128,128]{1,0:T(8,128)S(1)} %cholesky.599), custom_call_target="Cholesky" | custom-call | tf_op jit(solution)/shard_map/jit(cholesky)/cholesky | solution.py:65
  338.3 10.0 %custom-call.67 = f32[1,128,128]{1,2,0:T(8,128)S(1)} custom-call(f32[1,128,128]{2,1,0:T(8,128)S(1)} %get-tuple-element.232), custom_call_target="InvertDiagBlocksLowerTriangular" | custom-call | tf_op jit(solution)/shard_map/jit(cholesky)/cholesky | solution.py:65
  349.3 2.3 convolution_subtract_fusion.4
  351.6 11.7 %cholesky.526 = f32[128,128]{1,0:T(8,128)S(1)} custom-call(f32[128,128]{1,0:T(8,128)S(1)} %cholesky.604), custom_call_target="Cholesky" | custom-call | tf_op jit(solution)/shard_map/jit(cholesky)/cholesky | solution.py:65
  364.6 9.8 %custom-call.68 = f32[1,128,128]{1,2,0:T(8,128)S(1)} custom-call(f32[1,128,128]{2,1,0:T(8,128)S(1)} %get-tuple-element.229), custom_call_target="InvertDiagBlocksLowerTriangular" | custom-call | tf_op jit(solution)/shard_map/jit(cholesky)/cholesky | solution.py:65
  377.4 11.8 %cholesky.546 = f32[128,128]{1,0:T(8,128)S(1)} custom-call(f32[128,128]{1,0:T(8,128)S(1)} %cholesky.609), custom_call_target="Cholesky" | custom-call | tf_op jit(solution)/shard_map/jit(cholesky)/cholesky | solution.py:65
  390.4 9.8 %custom-call.69 = f32[1,128,128]{1,2,0:T(8,128)S(1)} custom-call(f32[1,128,128]{2,1,0:T(8,128)S(1)} %get-tuple-element.226), custom_call_target="InvertDiagBlocksLowerTriangular" | custom-call | tf_op jit(solution)/shard_map/jit(cholesky)/cholesky | solution.py:65
  402.9 11.7 %cholesky.564 = f32[128,128]{1,0:T(8,128)S(1)} custom-call(f32[128,128]{1,0:T(8,128)S(1)} %convolution_subtract_fusion.11), custom_call_target="Cholesky" | custom-call | tf_op jit(solution)/shard_map/jit(cholesky)/cholesky | solution.py:65
  421.5 4.8 select_select_fusion
  426.3 23.0 %while.16 = (s32[]{:T(128)}, f32[1024,1024]{1,0:T(8,128)}, s32[8,2]{0,1:T(2,128)S(1)}, f32[8,128,128]{2,1,0:T(8,128)S(1)}, s32[]{:T(128)}) while((s32[]{:T(128)}, f32[1024,1024]{1,0:T(8,128)}, s32[8,2]{0,1:T(2,128)S(1)}, f32[8,128,128]{2,1,0:T(8,128)S(1)}, s32[]{:T(128)}) %tuple.90), condition=%wide.while_cond, body=%wide.while_body.sunk | while | flops 2 | bytes 131181 | solution.py:66
  426.9 2.3 bitcast_dynamic-update-slice_fusion.2
  429.8 2.3 bitcast_dynamic-update-slice_fusion.2
  435.6 2.3 bitcast_dynamic-update-slice_fusion.2
  438.4 2.3 bitcast_dynamic-update-slice_fusion.2
  441.3 2.3 bitcast_dynamic-update-slice_fusion.2
  449.3 78.8 %custom-call.70 = f32[8,128,128]{1,2,0:T(8,128)S(1)} custom-call(f32[8,128,128]{2,1,0:T(8,128)S(1)} %get-tuple-element.125), custom_call_target="InvertDiagBlocksLowerTriangular" | custom-call | tf_op jit(solution)/shard_map/jit(_solve_triangular)/triangular_solve | solution.py:66
  543.2 7.2 %collective-permute-done.2 = bf16[128,1024]{0,1:T(8,128)(2,1)S(1)} collective-permute-done((bf16[128,1024]{0,1:T(8,128)(2,1)S(1)}, bf16[128,1024]{0,1:T(8,128)(2,1)S(1)}, u32[]{:S(2)}, u32[]{:S(2)}) %collective-permute-start.2) | collective-permute-done | bytes 262176 | tf_op jit(solution)/shard_map/ppermute | solution.py:15
  552.1 12.8 %collective-permute-done.3 = bf16[256,1024]{0,1:T(8,128)(2,1)S(1)} collective-permute-done((bf16[256,1024]{0,1:T(8,128)(2,1)S(1)}, bf16[256,1024]{0,1:T(8,128)(2,1)S(1)}, u32[]{:S(2)}, u32[]{:S(2)}) %collective-permute-start.3) | collective-permute-done | bytes 524320 | tf_op jit(solution)/shard_map/ppermute | solution.py:15
  569.5 2.3 collective-permute-done.5
  572.7 15.5 %collective-permute-done.6 = bf16[256]{0:T(256)(128)(2,1)S(1)} collective-permute-done((bf16[256]{0:T(256)(128)(2,1)S(1)}, bf16[256]{0:T(256)(128)(2,1)S(1)}, u32[]{:S(2)}, u32[]{:S(2)}) %collective-permute-start.6) | collective-permute-done | bytes 544 | tf_op jit(solution)/shard_map/ppermute | solution.py:15
  588.2 2.6 collective-permute-start.7
  590.8 21.9 %collective-permute-done.7 = bf16[512]{0:T(512)(128)(2,1)S(1)} collective-permute-done((bf16[512]{0:T(512)(128)(2,1)S(1)}, bf16[512]{0:T(512)(128)(2,1)S(1)}, u32[]{:S(2)}, u32[]{:S(2)}) %collective-permute-start.7) | collective-permute-done | bytes 1056 | tf_op jit(solution)/shard_map/ppermute | solution.py:15
  612.6 2.9 fusion.27
  615.6 2.3 copy.7
  617.9 3.6 maximum_select_fusion
  621.4 4.0 copy.16
  625.4 12.6 %while.17 = (s32[]{:T(128)}, f32[512]{0:T(512)S(1)}, f32[512,1024]{1,0:T(8,128)S(1)}, s32[2,512]{1,0:T(2,128)S(1)}, f32[512]{0:T(512)S(1)}, /*index=5*/bf16[2,51...) while((s32[]{:T(128)}, f32[512]{0:T(512)S(1)}, ...), condition=%wide.region_22.23_spmd.clone, body=%wide.region_20.22_spmd.clone.sunk | while | flops 1078731264 | bytes 9472136 | solution.py:122
  627.0 2.5 fusion.133
  633.3 2.5 fusion.133
  640.2 11.8 %collective-permute-done.8 = bf16[256]{0:T(256)(128)(2,1)S(1)} collective-permute-done((bf16[256]{0:T(256)(128)(2,1)S(1)}, bf16[256]{0:T(256)(128)(2,1)S(1)}, u32[]{:S(2)}, u32[]{:S(2)}) %collective-permute-start.8) | collective-permute-done | bytes 544 | tf_op jit(solution)/shard_map/ppermute | solution.py:15
  (137 shorter events, 72.9 us)
Async XLA Ops:
  7.2 193.2 %all-reduce.4.cloned.1.call-start = ((), (), s32[]{:S(2)}) async-start(), calls=%async_computation | async-start | bytes 8388608 | tf_op jit(solution)/shard_map/psum | solution.py:63
  51.7 6.7 %copy-start.1 = (bf16[128,1024]{1,0:T(8,128)(2,1)S(1)}, bf16[128,1024]{1,0:T(8,128)(2,1)}, u32[]{:S(2)}) copy-start(bf16[128,1024]{1,0:T(8,128)(2,1)} %param.4) | copy-start | bytes 786436
  216.7 1.9 copy-start
  541.6 1.6 collective-permute-start
  541.6 8.7 %collective-permute-start.2 = (bf16[128,1024]{0,1:T(8,128)(2,1)S(1)}, bf16[128,1024]{0,1:T(8,128)(2,1)S(1)}, u32[]{:S(2)}, u32[]{:S(2)}) collective-permute-start(bf16[128,1024]{0,1:T(8,128)(2,1)S(1)} %bitcast.153), channel_id=1, source_target_pairs={{0,4},{1,5},{2,6},{3,7},{4,0},{5,1},{6,2},{7,3},{8,12},{9,13},{10,... | collective-permute-start | bytes 786440 | tf_op jit(solution)/shard_map/ppermute | solution.py:15
  551.5 13.5 %collective-permute-start.3 = (bf16[256,1024]{0,1:T(8,128)(2,1)S(1)}, bf16[256,1024]{0,1:T(8,128)(2,1)S(1)}, u32[]{:S(2)}, u32[]{:S(2)}) collective-permute-start(bf16[256,1024]{0,1:T(8,128)(2,1)S(1)} %get-tuple-element.204), channel_id=1, source_target_pairs={{0,8},{1,9},{2,10},{3,11},{4,12},{5,13},{6,14},{7,15},{8,0},{9,1},... | collective-permute-start | bytes 1572872 | tf_op jit(solution)/shard_map/ppermute | solution.py:15
  565.2 52.7 %collective-permute-start.4 = (bf16[512,1024]{0,1:T(8,128)(2,1)S(1)}, bf16[512,1024]{0,1:T(8,128)(2,1)}, u32[]{:S(2)}, u32[]{:S(2)}) collective-permute-start(bf16[512,1024]{0,1:T(8,128)(2,1)S(1)} %maximum_select_fusion.2), channel_id=1, source_target_pairs={{0,16},{1,17},{2,18},{3,19},{4,20},{5,21},{6,22},{7,23},{8,24},{9,... | collective-permute-start | bytes 3145736 | tf_op jit(solution)/shard_map/ppermute | solution.py:15
  566.7 45.9 %collective-permute-start.1 = (bf16[256,1024]{0,1:T(8,128)(2,1)}, bf16[256,1024]{0,1:T(8,128)(2,1)}, u32[]{:S(2)}, u32[]{:S(2)}) collective-permute-start(bf16[256,1024]{0,1:T(8,128)(2,1)} %get-tuple-element.205), channel_id=1, source_target_pairs={{0,2},{1,3},{2,0},{3,1},{4,6},{5,7},{6,4},{7,5},{8,10},{9,11},{10,... | collective-permute-start | bytes 1572872 | tf_op jit(solution)/shard_map/ppermute | solution.py:15
  568.2 3.5 collective-permute-start.5
  571.7 16.4 %collective-permute-start.6 = (bf16[256]{0:T(256)(128)(2,1)S(1)}, bf16[256]{0:T(256)(128)(2,1)S(1)}, u32[]{:S(2)}, u32[]{:S(2)}) collective-permute-start(bf16[256]{0:T(256)(128)(2,1)S(1)} %broadcast_select_fusion), channel_id=1, source_target_pairs={{0,8},{1,9},{2,10},{3,11},{4,12},{5,13},{6,14},{7,15},{8,0},{9,1},... | collective-permute-start | bytes 1544 | tf_op jit(solution)/shard_map/ppermute | solution.py:15
  588.2 24.4 %collective-permute-start.7 = (bf16[512]{0:T(512)(128)(2,1)S(1)}, bf16[512]{0:T(512)(128)(2,1)S(1)}, u32[]{:S(2)}, u32[]{:S(2)}) collective-permute-start(bf16[512]{0:T(512)(128)(2,1)S(1)} %maximum_select_fusion.4), channel_id=1, source_target_pairs={{0,16},{1,17},{2,18},{3,19},{4,20},{5,21},{6,22},{7,23},{8,24},{9,... | collective-permute-start | bytes 3080 | tf_op jit(solution)/shard_map/ppermute | solution.py:15
  638.1 14.0 %collective-permute-start.10 = (bf16[256,1024]{1,0:T(8,128)(2,1)S(1)}, bf16[256,1024]{1,0:T(8,128)(2,1)S(1)}, u32[]{:S(2)}, u32[]{:S(2)}) collective-permute-start(bf16[256,1024]{1,0:T(8,128)(2,1)S(1)} %select_convert_fusion), channel_id=1, source_target_pairs={{0,2},{1,3},{2,0},{3,1},{4,6},{5,7},{6,4},{7,5},{8,10},{9,11},{10,... | collective-permute-start | bytes 1572872 | tf_op jit(solution)/shard_map/ppermute | solution.py:15
  639.6 12.4 %collective-permute-start.8 = (bf16[256]{0:T(256)(128)(2,1)S(1)}, bf16[256]{0:T(256)(128)(2,1)S(1)}, u32[]{:S(2)}, u32[]{:S(2)}) collective-permute-start(bf16[256]{0:T(256)(128)(2,1)S(1)} %select_convert_fusion.3), channel_id=1, source_target_pairs={{0,2},{1,3},{2,0},{3,1},{4,6},{5,7},{6,4},{7,5},{8,10},{9,11},{10,... | collective-permute-start | bytes 1544 | tf_op jit(solution)/shard_map/ppermute | solution.py:15
  652.0 1.2 collective-permute-start.9
  652.4 1.7 collective-permute-start.11
Sparse Core Ops, SparseCore 0:
  58.5 141.8 all-reduce.3
where the time goes:
time: 668 us; the launch traced here: 662 us
  other arithmetic  281 us (42%)
  waiting for transfers between devices  214 us (32%)
  matrix products  52.3 us (8%)
  blocking collectives  42.1 us (6%)
  local copies, waits for them, and re-layouts  39.2 us (6%)
  between operations  20.5 us (3%)
  starting transfers between devices  12.7 us (2%)
    another operation x30, other arithmetic, shards(): factor = jnp.linalg.cholesky(covariance)  172 us
    psum x1, waiting for transfers between devices, shards(): lax.psum(jnp.dot(centred.T, centred, precision=lax.Precision.HIGHEST), 'd...  142 us
    another operation x3, other arithmetic, shards(): jax.scipy.linalg.solve_triangular(factor, (widened - mean_vec).T, lower=T...  83.6 us
    ppermute x12, waiting for transfers between devices, swapped(): return lax.ppermute(value, axis, pairs)  72.1 us
    psum x1, blocking collectives, shards(): lax.psum((jnp.sum(masked, axis=0), local_count), 'dev')  42.1 us
    another operation x14, matrix products, shards(): factor = jnp.linalg.cholesky(covariance)  23.1 us
    another operation x24, local copies, waits for them, and re-layouts  22.8 us
  transfers between devices with their start and end apart: 13, of which 9 were waited for; matrix products, arithmetic and copies ran while one was open for 1% of the time, Pallas kernels for 0%

commit v1 on v0

v1 whole, which is shorter than its diff:
```python
import math

import jax
import jax.numpy as jnp
from jax import lax
from jax.experimental import pallas as pl
from jax.experimental.pallas import tpu as pltpu
from jax.sharding import PartitionSpec as P

EPS = 1e-06
RIDGE = 1.0
LIVE_MAX = 96
DEAD = 1024.0
DEAD_ABOVE = 512.0
SUB = 8
LANES = 128
TILE = 256
CHUNK = 512
VMEM_BYTES = 60 << 20
EXACT = lax.Precision.HIGHEST


def product(left, right, left_dim, right_dim, precision=None):
    return lax.dot_general(
        left,
        right,
        (((left_dim,), (right_dim,)), ((), ())),
        precision=precision,
        preferred_element_type=jnp.float32,
    )


def two_parts(value):
    high = value.astype(jnp.bfloat16)
    return high, (value - high.astype(jnp.float32)).astype(jnp.bfloat16)


def chunk_of(rows):
    return math.gcd(rows, CHUNK)


def moments_kernel(keys_ref, mean_ref, cov_ref, total):
    rows, dim = keys_ref.shape
    step = chunk_of(rows)
    tiles = dim // TILE

    def live_of(block):
        return block[:, :1] < DEAD_ABOVE

    def add_sums(index, carry):
        sums, count = carry
        block = keys_ref[pl.ds(pl.multiple_of(index * step, step), step), :].astype(jnp.float32)
        live = live_of(block)
        part = jnp.where(live, block, 0.0).reshape(step // SUB, SUB, dim)
        alive = live.astype(jnp.float32).reshape(step // SUB, SUB, 1)
        return sums + jnp.sum(part, axis=0), count + jnp.sum(alive, axis=0)

    start = (jnp.zeros((SUB, dim), jnp.float32), jnp.zeros((SUB, 1), jnp.float32))
    sums, count = lax.fori_loop(0, rows // step, add_sums, start)
    count = jnp.sum(count, axis=0, keepdims=True)
    mean = jnp.sum(sums, axis=0, keepdims=True) / count
    mean_ref[...] = jnp.broadcast_to(mean, (SUB, dim))
    total[...] = jnp.zeros_like(total)

    @pl.loop(0, rows // step)
    def _(index):
        block = keys_ref[pl.ds(pl.multiple_of(index * step, step), step), :].astype(jnp.float32)
        high, low = two_parts(jnp.where(live_of(block), block - mean, 0.0))
        for tile in range(tiles):
            here = slice(tile * TILE, (tile + 1) * TILE)
            upto = slice(0, (tile + 1) * TILE)
            part = product(high[:, here], high[:, upto], 0, 0)
            part += product(high[:, here], low[:, upto], 0, 0)
            part += product(low[:, here], high[:, upto], 0, 0)
            total[here, upto] += part

    for tile in range(tiles):
        here = slice(tile * TILE, (tile + 1) * TILE)
        upto = slice(0, (tile + 1) * TILE)
        shape = (TILE, (tile + 1) * TILE)
        down = lax.broadcasted_iota(jnp.int32, shape, 0) + tile * TILE
        across = lax.broadcasted_iota(jnp.int32, shape, 1)
        cov_ref[here, upto] = total[here, upto] / count + jnp.where(down == across, RIDGE, 0.0)


def invert_factor(rows, inverse):
    count = len(rows)
    sublane = lax.broadcasted_iota(jnp.int32, (SUB, LANES), 0)

    def over_lanes(value, lane):
        return jnp.broadcast_to(value[:, lane : lane + 1], (SUB, LANES))

    def over_sublanes(value, row):
        return jnp.broadcast_to(value[row : row + 1, :], (SUB, LANES))

    for step in range(count):
        first = SUB * step
        pivot_rows, inverse_rows = rows[step], inverse[step]
        columns = [over_lanes(pivot_rows, first + t) for t in range(SUB)]
        below = {
            i: [over_lanes(rows[i], first + t) for t in range(SUB)]
            for i in range(step + 1, count)
        }
        scale, entry, upper, solved = [], {}, [], []
        for t in range(SUB):
            root = lax.rsqrt(over_sublanes(columns[t], t))
            scale.append(root)
            down = jnp.where(sublane > t, columns[t] * root, 0.0)
            upper.append(over_sublanes(pivot_rows, t) * root)
            solved.append(over_sublanes(inverse_rows, t) * root)
            for q in range(t + 1, SUB):
                entry[q, t] = over_sublanes(columns[q], t) * root
                columns[q] = columns[q] - down * entry[q, t]
            pivot_rows = pivot_rows - down * upper[t]
            inverse_rows = jnp.where(sublane == t, solved[t], inverse_rows - down * solved[t])
        inverse[step] = inverse_rows
        for i in range(step + 1, count):
            column, row, other = below[i], rows[i], inverse[i]
            for t in range(SUB):
                factor = column[t] * scale[t]
                for q in range(t + 1, SUB):
                    column[q] = column[q] - factor * entry[q, t]
                row = row - factor * upper[t]
                other = other - factor * solved[t]
            rows[i], inverse[i] = row, other
    return inverse


def whitener_kernel(cov_ref, high_ref, low_ref, work, found, block, part):
    dim = cov_ref.shape[0]
    work[...] = cov_ref[...]
    found[...] = jnp.zeros_like(found)
    block[...] = cov_ref[0:LANES, 0:LANES]
    count = LANES // SUB

    @pl.loop(0, dim // LANES)
    def _(index):
        lane = lax.broadcasted_iota(jnp.int32, (SUB, LANES), 1)
        sublane = lax.broadcasted_iota(jnp.int32, (SUB, LANES), 0)
        rows = [block[SUB * i : SUB * i + SUB, :] for i in range(count)]
        inverse = [(lane == sublane + SUB * i).astype(jnp.float32) for i in range(count)]
        inverse = invert_factor(rows, inverse)
        for i in range(count):
            part[SUB * i : SUB * i + SUB, :] = inverse[i]
        for here in range(dim // LANES):
            top = here // 2 * TILE
            mid, end = top + LANES, top + TILE

            @pl.when(index == here)
            def _(here=here, top=top, mid=mid, end=end):
                own = part[...]
                if here % 2 == 0:
                    left = product(work[mid:end, top:mid], own, 1, 1, EXACT)
                    block[...] = work[mid:end, mid:end] - product(left, left, 1, 1, EXACT)
                    found[top:mid, top:mid] = own
                    found[mid:end, top:mid] = product(left, own, 1, 0, EXACT)
                    return
                found[mid:end, mid:end] = own
                found[mid:end, top:mid] = -product(own, found[mid:end, top:mid], 1, 0, EXACT)
                pair = found[top:end, top:end]
                if end < dim:
                    panel = product(work[end:dim, top:end], pair, 1, 1, EXACT)
                    for low in range(0, dim - end, TILE):
                        size = low + TILE
                        strip = slice(end + low, end + size)
                        work[strip, end : end + size] = work[strip, end : end + size] - product(
                            panel[low:size], panel[0:size], 1, 1, EXACT
                        )
                    block[...] = work[end : end + LANES, end : end + LANES]
                if top > 0:
                    found[top:end, 0:top] = product(pair, found[top:end, 0:top], 1, 0, EXACT)
                if end < dim:
                    found[end:dim, 0:end] = found[end:dim, 0:end] - product(
                        panel, found[top:end, 0:end], 1, 0, EXACT
                    )

    high, low = two_parts(found[...])
    high_ref[...] = high
    low_ref[...] = low


def scores_kernel(
    place_ref, keys_ref, own_ref, mean_ref, high_ref, low_ref, log_ref, out_ref, density, total
):
    rows, dim = keys_ref.shape
    queries = own_ref.shape[0]
    step = chunk_of(rows)
    sharpness = 2.0 * math.sqrt(dim)
    mean = mean_ref[0:1, :]

    def whitened(values):
        high, low = two_parts(values.astype(jnp.float32) - mean)
        parts = []
        for tile in range(dim // TILE):
            here = slice(tile * TILE, (tile + 1) * TILE)
            upto = slice(0, (tile + 1) * TILE)
            part = product(high[:, upto], high_ref[here, upto], 1, 1)
            part += product(high[:, upto], low_ref[here, upto], 1, 1)
            part += product(low[:, upto], high_ref[here, upto], 1, 1)
            parts.append(part.astype(jnp.bfloat16))
        return jnp.concatenate(parts, axis=1)

    def lengths(white):
        wide = white.astype(jnp.float32)
        return lax.rsqrt(jnp.sum(wide * wide, axis=1, keepdims=True) + EPS)

    query = whitened(own_ref[...])
    query_norm = jnp.broadcast_to(lengths(query), (queries, queries)).T[0:1, :]
    density[...] = jnp.zeros_like(density)
    total[...] = jnp.zeros_like(total)

    @pl.loop(0, rows // step)
    def _(index):
        start = pl.multiple_of(index * step, step)
        block = keys_ref[pl.ds(start, step), :]
        live = block[:, :1].astype(jnp.float32) < DEAD_ABOVE
        white = whitened(block)
        inner = product(white, query, 1, 1)
        scores = sharpness * (lengths(white) * query_norm * inner - 1.0)
        shape = (step, queries)
        key_index = start + lax.broadcasted_iota(jnp.int32, shape, 0)
        query_index = place_ref[0] + lax.broadcasted_iota(jnp.int32, shape, 1)
        seen = live & (key_index != query_index)
        weights = jnp.where(seen, jnp.exp(scores), 0.0)
        density[...] += jnp.sum(weights, axis=0, keepdims=True)
        total[...] += product(weights.astype(jnp.bfloat16), white, 0, 0)

    own_size = place_ref[1]
    dense = density[...]
    lane = lax.broadcasted_iota(jnp.int32, dense.shape, 1)
    log_ref[...] = jnp.where(lane < own_size, jnp.log(dense), 0.0)
    divisor = jnp.broadcast_to(dense, (queries, queries)).T[:, 0:1]
    sublane = lax.broadcasted_iota(jnp.int32, (queries, 1), 0)
    out_ref[...] = jnp.where(sublane < own_size, total[...] / divisor, 0.0).astype(jnp.bfloat16)


def whole(count):
    return [pl.BlockSpec(memory_space=pltpu.VMEM)] * count


def shards(states, bucket_sizes):
    row_count, dim = states.shape
    block_count = bucket_sizes.shape[0]
    block_rows = row_count // block_count
    params = pltpu.CompilerParams(vmem_limit_bytes=VMEM_BYTES)
    square = (dim, dim)
    in_block = jnp.arange(LIVE_MAX, dtype=jnp.int32)
    own_live = (in_block[None, :] < bucket_sizes[:, None])[:, :, None]
    prefix = states.reshape(block_count, block_rows, dim)[:, :LIVE_MAX]
    sent = jnp.where(own_live, prefix, jnp.bfloat16(DEAD)).reshape(-1, dim)
    keys = lax.all_gather(sent, "dev", axis=0, tiled=True)
    mean, covariance = pl.pallas_call(
        moments_kernel,
        out_shape=[
            jax.ShapeDtypeStruct((SUB, dim), jnp.float32),
            jax.ShapeDtypeStruct(square, jnp.float32),
        ],
        in_specs=whole(1),
        out_specs=whole(2),
        scratch_shapes=[pltpu.VMEM(square, jnp.float32)],
        compiler_params=params,
    )(keys)
    high, low = pl.pallas_call(
        whitener_kernel,
        out_shape=[jax.ShapeDtypeStruct(square, jnp.bfloat16)] * 2,
        in_specs=whole(1),
        out_specs=whole(2),
        scratch_shapes=[
            pltpu.VMEM(square, jnp.float32),
            pltpu.VMEM(square, jnp.float32),
            pltpu.VMEM((LANES, LANES), jnp.float32),
            pltpu.VMEM((LANES, LANES), jnp.float32),
        ],
        compiler_params=params,
    )(covariance)
    logs, means = [], []
    for here in range(block_count):
        place = (lax.axis_index("dev") * block_count + here) * LIVE_MAX
        log_part, mean_part = pl.pallas_call(
            scores_kernel,
            out_shape=[
                jax.ShapeDtypeStruct((1, block_rows), jnp.float32),
                jax.ShapeDtypeStruct((block_rows, dim), jnp.bfloat16),
            ],
            in_specs=[pl.BlockSpec(memory_space=pltpu.SMEM)] + whole(5),
            out_specs=whole(2),
            scratch_shapes=[
                pltpu.VMEM((1, block_rows), jnp.float32),
                pltpu.VMEM((block_rows, dim), jnp.float32),
            ],
            compiler_params=params,
        )(
            jnp.stack([place, bucket_sizes[here]]),
            keys,
            lax.slice_in_dim(states, here * block_rows, (here + 1) * block_rows),
            mean,
            high,
            low,
        )
        logs.append(log_part.reshape(block_rows))
        means.append(mean_part)
    return jnp.concatenate(logs), jnp.concatenate(means)


def solution(mesh):
    placed = (P("dev", None), P("dev"))
    return jax.shard_map(
        shards, mesh=mesh, in_specs=placed, out_specs=(P("dev"), P("dev", None)), check_vma=False
    )
```

time: 668 us -> 190 us (0.28)
  other arithmetic: 281 us -> 2.31 us
  waiting for transfers between devices: 214 us -> 73.5 us
  Pallas kernels: 0 us -> 98.9 us
  matrix products: 52.3 us -> 0 us
  blocking collectives: 42.1 us -> 0 us
  local copies, waits for them, and re-layouts: 39.2 us -> 0 us
  starting transfers between devices: 12.7 us -> 0.04 us
    another operation x33 -> x1, other arithmetic: 256 us -> 0.61 us  [shards(): jnp.stack([place, bucket_sizes[here]])]
    psum x1 -> x0, waiting for transfers between devices: 142 us -> none  [shards(): lax.psum(jnp.dot(centred.T, centred, precision=lax.Precision.HIGHEST), 'd...]
    pallas_call x0 -> x3, Pallas kernels: none -> 98.9 us  [the longest x1 50.8 us: shards(): pl.pallas_call(whitener_kernel, out_shape=[jax.ShapeDtypeStruct(square, j...]
    all_gather x0 -> x1, waiting for transfers between devices: none -> 73.5 us  [shards(): keys = lax.all_gather(sent, 'dev', axis=0, tiled=True)]
    ppermute x12 -> x0, waiting for transfers between devices: 72.1 us -> none  [swapped(): return lax.ppermute(value, axis, pairs)]
    psum x1 -> x0, blocking collectives: 42.1 us -> none  [shards(): lax.psum((jnp.sum(masked, axis=0), local_count), 'dev')]
    another operation x29 -> x0, matrix products: 36.3 us -> none  [the longest x14 23.1 us: shards(): factor = jnp.linalg.cholesky(covariance)]
    another operation x34 -> x0, local copies, waits for them, and re-layouts: 25.4 us -> none
  transfers between devices with their start and end apart: 13 -> 1, of which waited for: 9 -> 1; matrix products, arithmetic and copies ran while one was open for 1% -> 0% of each run, Pallas kernels for 0% -> 0%
where the time goes in v1:
time: 190 us; the launch traced here: 189 us
  Pallas kernels  98.9 us (52%)
  waiting for transfers between devices  73.5 us (39%)
  between operations  14.7 us (8%)
  other arithmetic  2.31 us (1%)
    all_gather x1, waiting for transfers between devices, shards(): keys = lax.all_gather(sent, 'dev', axis=0, tiled=True)  73.5 us
    pallas_call x1, Pallas kernels, shards(): pl.pallas_call(whitener_kernel, out_shape=[jax.ShapeDtypeStruct(square, j...  50.8 us
    pallas_call x1, Pallas kernels, shards(): pl.pallas_call(scores_kernel, out_shape=[jax.ShapeDtypeStruct((1, block_r...  26.3 us
    pallas_call x1, Pallas kernels, shards(): pl.pallas_call(moments_kernel, out_shape=[jax.ShapeDtypeStruct((SUB, dim)...  21.8 us
  transfers between devices with their start and end apart: 1, of which 1 were waited for; matrix products, arithmetic and copies ran while one was open for 0% of the time, Pallas kernels for 0%

profile of v1, /device:TPU:0, one launch (start us, length us, event | category | flops | bytes accessed | tf_op | source)
XLA Modules:
  0.0 189.4 jit_solution(3637584488864821587)
XLA Ops:
  7.2 0.0 all-gather.3.cloned.1.call-start
  7.9 1.7 slice_select_fusion
  9.6 0.0 all-gather.3.cloned.1.call-update
  9.6 0.6 pad_add_fusion.place_ref
  10.2 73.5 %all-gather.3.cloned.1.call-done = bf16[1,3072,1024]{2,1,0:T(8,128)(2,1)} async-done(((bf16[1,96,1024]{2,1,0:T(8,128)(2,1)}), bf16[1,3072,1024]{2,1,0:T(8,128)(2,1)}) %all-gather.3.cloned.1.call-update) | async-done | bytes 6291472 | tf_op jit(solution)/shard_map/all_gather | solution.py:251
  83.7 21.8 %shard_map.41 = (f32[8,1024]{1,0:T(8,128)}, f32[1024,1024]{1,0:T(8,128)}) custom-call(bf16[3072,1024]{1,0:T(8,128)(2,1)} %bitcast.6), custom_call_target="tpu_custom_call" | custom-call | tf_op jit(solution)/shard_map/pallas_call | solution.py:252
  105.5 50.8 %shard_map.42 = (bf16[1024,1024]{1,0:T(8,128)(2,1)}, bf16[1024,1024]{1,0:T(8,128)(2,1)}) custom-call(f32[1024,1024]{1,0:T(8,128)} %get-tuple-element.9.cov_ref), custom_call_target="tpu_custom_call" | custom-call | tf_op jit(solution)/shard_map/pallas_call | solution.py:263
  156.3 26.3 %shard_map.43 = (f32[1,128]{1,0:T(1,128)}, bf16[128,1024]{1,0:T(8,128)(2,1)}) custom-call(s32[2]{0:T(128)} %pad_add_fusion.place_ref, bf16[3072,1024]{1,0:T(8,128)(2,1)} %bitcast.7, bf16[128,1024]{1,0:T(8,128)(2,1)} %own_ref.1, f32[8,1024]{1,0:T(8,128)} %get-tuple-element.8.mean_ref, bf16[1024,1024]{1,0:T(8,128)(2,1)} %get-tuple-element.10.high_ref, ...), custom_call_target="tpu_custom_call" | custom-call | tf_op jit(solution)/shard_map/pallas_call | solution.py:279
  (1 shorter events, 0.0 us)
Async XLA Ops:
  7.2 76.5 %all-gather.3.cloned.1.call-start = ((), (), s32[]{:S(2)}) async-start(), calls=%async_computation | async-start | bytes 6488064 | tf_op jit(solution)/shard_map/all_gather | solution.py:251
Sparse Core Ops, SparseCore 0:
  11.4 72.1 all-gather.2

commit v2 on v1

--- a/solution.py
+++ b/solution.py
@@ -33,6 +33,25 @@
 def two_parts(value):
     high = value.astype(jnp.bfloat16)
     return high, (value - high.astype(jnp.float32)).astype(jnp.bfloat16)
+
+
+def flipped(value, mask):
+    size = lax.axis_size("dev")
+    return lax.ppermute(value, "dev", [(source, source ^ mask) for source in range(size)])
+
+
+def gather_rows(rows):
+    size = lax.axis_size("dev")
+    near, far = size // 4, size // 2
+    across = flipped(rows, far)
+    beside = flipped(rows, near)
+    groups = [rows, across, beside, flipped(across, near)]
+    pieces = []
+    for group in groups:
+        pieces.append(group)
+        pieces += [flipped(group, mask) for mask in range(2, near, 2)]
+    same_core = jnp.concatenate(pieces, axis=0)
+    return jnp.concatenate([same_core, flipped(same_core, 1)], axis=0)
 
 
 def chunk_of(rows):
@@ -248,7 +267,7 @@
     own_live = (in_block[None, :] < bucket_sizes[:, None])[:, :, None]
     prefix = states.reshape(block_count, block_rows, dim)[:, :LIVE_MAX]
     sent = jnp.where(own_live, prefix, jnp.bfloat16(DEAD)).reshape(-1, dim)
-    keys = lax.all_gather(sent, "dev", axis=0, tiled=True)
+    keys = gather_rows(sent)
     mean, covariance = pl.pallas_call(
         moments_kernel,
         out_shape=[
@@ -275,7 +294,7 @@
     )(covariance)
     logs, means = [], []
     for here in range(block_count):
-        place = (lax.axis_index("dev") * block_count + here) * LIVE_MAX
+        place = jnp.int32(here * LIVE_MAX)
         log_part, mean_part = pl.pallas_call(
             scores_kernel,
             out_shape=[

time: 190 us -> 152 us (0.80)
  waiting for transfers between devices: 73.5 us -> 14.6 us
  starting transfers between devices: 0.04 us -> 22.1 us
  between operations: 14.7 us -> 1.32 us
  local copies, waits for them, and re-layouts: 0 us -> 13.3 us
    all_gather x1 -> x0, waiting for transfers between devices: 73.5 us -> none  [shards(): keys = lax.all_gather(sent, 'dev', axis=0, tiled=True)]
    ppermute x0 -> x16, starting transfers between devices: none -> 22.1 us  [flipped(): lax.ppermute(value, 'dev', [(source, source ^ mask) for source in range(s...]
    ppermute x0 -> x16, waiting for transfers between devices: none -> 14.6 us  [flipped(): lax.ppermute(value, 'dev', [(source, source ^ mask) for source in range(s...]
    unnamed x0 -> x15, local copies, waits for them, and re-layouts: none -> 10.6 us
    concatenate x0 -> x2, local copies, waits for them, and re-layouts: none -> 2.71 us  [the longest x1 1.99 us: gather_rows(): return jnp.concatenate([same_core, flipped(same_core, 1)], axis=0)]
  transfers between devices with their start and end apart: 1 -> 16, of which waited for: 1 -> 5; matrix products, arithmetic and copies ran while one was open for 0% -> 7% of each run, Pallas kernels for 0% -> 0%
where the time goes in v2:
time: 152 us
  Pallas kernels  98.9 us (65%)
  starting transfers between devices  22.1 us (15%)
  waiting for transfers between devices  14.6 us (10%)
  local copies, waits for them, and re-layouts  13.3 us (9%)
  other arithmetic  1.68 us (1%)
    pallas_call x1, Pallas kernels, shards(): pl.pallas_call(whitener_kernel, out_shape=[jax.ShapeDtypeStruct(square, j...  50.8 us
    pallas_call x1, Pallas kernels, shards(): pl.pallas_call(scores_kernel, out_shape=[jax.ShapeDtypeStruct((1, block_r...  26.3 us
    ppermute x16, starting transfers between devices, flipped(): lax.ppermute(value, 'dev', [(source, source ^ mask) for source in range(s...  22.1 us
    pallas_call x1, Pallas kernels, shards(): pl.pallas_call(moments_kernel, out_shape=[jax.ShapeDtypeStruct((SUB, dim)...  21.8 us
    ppermute x16, waiting for transfers between devices, flipped(): lax.ppermute(value, 'dev', [(source, source ^ mask) for source in range(s...  14.6 us
    unnamed x15, local copies, waits for them, and re-layouts  10.6 us
  transfers between devices with their start and end apart: 16, of which 5 were waited for; matrix products, arithmetic and copies ran while one was open for 7% of the time, Pallas kernels for 0%

profile of v2, /device:TPU:0, one launch (start us, length us, event | category | flops | bytes accessed | tf_op | source)
XLA Modules:
  0.0 152.0 jit_solution(10516700295116445654)
XLA Ops:
  1.3 1.0 constant_dynamic-update-slice_fusion.15
  2.3 4.1 %collective-permute-start.3 = (bf16[96,1024]{1,0:T(8,128)(2,1)S(1)}, bf16[96,1024]{1,0:T(8,128)(2,1)S(1)}, u32[]{:S(2)}, u32[]{:S(2)}) collective-permute-start(bf16[96,1024]{1,0:T(8,128)(2,1)S(1)} %get-tuple-element.15), channel_id=1, source_target_pairs={{0,16},{1,17},{2,18},{3,19},{4,20},{5,21},{6,22},{7,23},{8,24},{9,... | collective-permute-start | bytes 589832 | tf_op jit(solution)/shard_map/ppermute | solution.py:40
  6.4 1.5 collective-permute-start
  7.9 1.5 collective-permute-start.1
  9.4 0.5 collective-permute-start.2
  9.9 1.6 %collective-permute-start.7 = (bf16[96,1024]{1,0:T(8,128)(2,1)S(1)}, bf16[96,1024]{1,0:T(8,128)(2,1)S(1)}, u32[]{:S(2)}, u32[]{:S(2)}) collective-permute-start(bf16[96,1024]{1,0:T(8,128)(2,1)S(1)} %get-tuple-element.15), channel_id=1, source_target_pairs={{0,8},{1,9},{2,10},{3,11},{4,12},{5,13},{6,14},{7,15},{8,0},{9,1},... | collective-permute-start | bytes 589832 | tf_op jit(solution)/shard_map/ppermute | solution.py:40
  11.5 0.7 constant_dynamic-update-slice_fusion.32
  12.2 3.5 %collective-permute-done.3 = bf16[96,1024]{1,0:T(8,128)(2,1)S(1)} collective-permute-done((bf16[96,1024]{1,0:T(8,128)(2,1)S(1)}, bf16[96,1024]{1,0:T(8,128)(2,1)S(1)}, u32[]{:S(2)}, u32[]{:S(2)}) %collective-permute-start.3) | collective-permute-done | bytes 196640 | tf_op jit(solution)/shard_map/ppermute | solution.py:40
  15.6 1.5 %collective-permute-start.4 = (bf16[96,1024]{1,0:T(8,128)(2,1)S(1)}, bf16[96,1024]{1,0:T(8,128)(2,1)S(1)}, u32[]{:S(2)}, u32[]{:S(2)}) collective-permute-start(bf16[96,1024]{1,0:T(8,128)(2,1)S(1)} %collective-permute-done.3), channel_id=1, source_target_pairs={{0,2},{1,3},{2,0},{3,1},{4,6},{5,7},{6,4},{7,5},{8,10},{9,11},{10,... | collective-permute-start | bytes 589832 | tf_op jit(solution)/shard_map/ppermute | solution.py:40
  17.2 1.5 %collective-permute-start.5 = (bf16[96,1024]{1,0:T(8,128)(2,1)S(1)}, bf16[96,1024]{1,0:T(8,128)(2,1)S(1)}, u32[]{:S(2)}, u32[]{:S(2)}) collective-permute-start(bf16[96,1024]{1,0:T(8,128)(2,1)S(1)} %collective-permute-done.3), channel_id=1, source_target_pairs={{0,4},{1,5},{2,6},{3,7},{4,0},{5,1},{6,2},{7,3},{8,12},{9,13},{10,... | collective-permute-start | bytes 589832 | tf_op jit(solution)/shard_map/ppermute | solution.py:40
  18.7 0.7 constant_dynamic-update-slice_fusion.14
  19.4 0.4 collective-permute-start.6
  19.8 0.7 constant_dynamic-update-slice_fusion.13
  20.6 0.0 collective-permute-done.2
  20.6 1.4 collective-permute-start.11
  22.0 0.0 collective-permute-done.7
  22.0 1.5 collective-permute-start.8
  23.5 0.7 constant_dynamic-update-slice_fusion.12
  24.2 0.7 constant_dynamic-update-slice_fusion.11
  24.9 0.0 collective-permute-done.4
  24.9 0.7 collective-permute-start.9
  25.7 0.7 constant_dynamic-update-slice_fusion.10
  26.4 0.0 collective-permute-done.5
  26.4 1.2 collective-permute-start.10
  27.6 0.0 collective-permute-done.11
  27.6 2.6 %collective-permute-start.12 = (bf16[96,1024]{1,0:T(8,128)(2,1)S(1)}, bf16[96,1024]{1,0:T(8,128)(2,1)S(1)}, u32[]{:S(2)}, u32[]{:S(2)}) collective-permute-start(bf16[96,1024]{1,0:T(8,128)(2,1)S(1)} %collective-permute-done.11), channel_id=1, source_target_pairs={{0,2},{1,3},{2,0},{3,1},{4,6},{5,7},{6,4},{7,5},{8,10},{9,11},{10,... | collective-permute-start | bytes 589832 | tf_op jit(solution)/shard_map/ppermute | solution.py:40
  30.2 0.7 constant_dynamic-update-slice_fusion.9
  30.9 0.0 collective-permute-start.13
  30.9 0.7 constant_dynamic-update-slice_fusion.8
  31.6 0.7 constant_dynamic-update-slice_fusion.7
  32.3 2.0 %collective-permute-start.14 = (bf16[96,1024]{1,0:T(8,128)(2,1)S(1)}, bf16[96,1024]{1,0:T(8,128)(2,1)S(1)}, u32[]{:S(2)}, u32[]{:S(2)}) collective-permute-start(bf16[96,1024]{1,0:T(8,128)(2,1)S(1)} %collective-permute-done.11), channel_id=1, source_target_pairs={{0,6},{1,7},{2,4},{3,5},{4,2},{5,3},{6,0},{7,1},{8,14},{9,15},{10,... | collective-permute-start | bytes 589832 | tf_op jit(solution)/shard_map/ppermute | solution.py:40
  34.3 0.7 constant_dynamic-update-slice_fusion.6
  35.0 1.9 %collective-permute-done.9 = bf16[96,1024]{1,0:T(8,128)(2,1)S(1)} collective-permute-done((bf16[96,1024]{1,0:T(8,128)(2,1)S(1)}, bf16[96,1024]{1,0:T(8,128)(2,1)S(1)}, u32[]{:S(2)}, u32[]{:S(2)}) %collective-permute-start.9) | collective-permute-done | bytes 196640 | tf_op jit(solution)/shard_map/ppermute | solution.py:40
  37.0 0.7 constant_dynamic-update-slice_fusion.5
  37.7 0.7 constant_dynamic-update-slice_fusion.4
  38.4 0.7 constant_dynamic-update-slice_fusion.3
  39.1 1.2 collective-permute-done.12
  40.3 0.7 constant_dynamic-update-slice_fusion.2
  41.0 2.9 %collective-permute-done.13 = bf16[96,1024]{1,0:T(8,128)(2,1)S(1)} collective-permute-done((bf16[96,1024]{1,0:T(8,128)(2,1)S(1)}, bf16[96,1024]{1,0:T(8,128)(2,1)S(1)}, u32[]{:S(2)}, u32[]{:S(2)}) %collective-permute-start.13) | collective-permute-done | bytes 196640 | tf_op jit(solution)/shard_map/ppermute | solution.py:40
  43.9 0.7 constant_dynamic-update-slice_fusion.1
  44.6 0.7 constant_dynamic-update-slice_fusion
  45.4 0.0 collective-permute-start.15
  45.4 0.6 pad_add_fusion.place_ref
  46.0 5.0 %collective-permute-done.15 = bf16[1536,1024]{1,0:T(8,128)(2,1)S(1)} collective-permute-done((bf16[1536,1024]{1,0:T(8,128)(2,1)S(1)}, bf16[1536,1024]{1,0:T(8,128)(2,1)S(1)}, u32[]{:S(2)}, u32[]{:S(2)}) %collective-permute-start.15) | collective-permute-done | bytes 3145760 | tf_op jit(solution)/shard_map/ppermute | solution.py:40
  51.0 2.0 %constant_dynamic-update-slice_fusion.16.keys_ref = bf16[3072,1024]{1,0:T(8,128)(2,1)} fusion(bf16[3072,1024]{1,0:T(8,128)(2,1)} %get-tuple-element.17, bf16[1536,1024]{1,0:T(8,128)(2,1)S(1)} %collective-permute-done.15), kind=kLoop, calls=%fused_computation.18 | loop fusion | bytes 6291456 | tf_op jit(solution)/shard_map/concatenate | solution.py:54
  53.0 21.8 %shard_map.41 = (f32[8,1024]{1,0:T(8,128)}, f32[1024,1024]{1,0:T(8,128)}) custom-call(bf16[3072,1024]{1,0:T(8,128)(2,1)} %constant_dynamic-update-slice_fusion.16.keys_ref), custom_call_target="tpu_custom_call" | custom-call | tf_op jit(solution)/shard_map/pallas_call | solution.py:271
  74.8 50.8 %shard_map.42 = (bf16[1024,1024]{1,0:T(8,128)(2,1)}, bf16[1024,1024]{1,0:T(8,128)(2,1)}) custom-call(f32[1024,1024]{1,0:T(8,128)} %get-tuple-element.9.cov_ref), custom_call_target="tpu_custom_call" | custom-call | tf_op jit(solution)/shard_map/pallas_call | solution.py:282
  125.6 26.3 %shard_map.43 = (f32[1,128]{1,0:T(1,128)}, bf16[128,1024]{1,0:T(8,128)(2,1)}) custom-call(s32[2]{0:T(128)} %pad_add_fusion.place_ref, bf16[3072,1024]{1,0:T(8,128)(2,1)} %constant_dynamic-update-slice_fusion.16.keys_ref, bf16[128,1024]{1,0:T(8,128)(2,1)} %own_ref.1, f32[8,1024]{1,0:T(8,128)} %get-tuple-element.8.mean_ref, ...), custom_call_target="tpu_custom_call" | custom-call | tf_op jit(solution)/shard_map/pallas_call | solution.py:298
  (7 shorter events, 0.0 us)
Async XLA Ops:
  2.3 13.3 %collective-permute-start.3 = (bf16[96,1024]{1,0:T(8,128)(2,1)S(1)}, bf16[96,1024]{1,0:T(8,128)(2,1)S(1)}, u32[]{:S(2)}, u32[]{:S(2)}) collective-permute-start(bf16[96,1024]{1,0:T(8,128)(2,1)S(1)} %get-tuple-element.15), channel_id=1, source_target_pairs={{0,16},{1,17},{2,18},{3,19},{4,20},{5,21},{6,22},{7,23},{8,24},{9,... | collective-permute-start | bytes 589832 | tf_op jit(solution)/shard_map/ppermute | solution.py:40
  6.4 10.8 %collective-permute-start = (bf16[96,1024]{1,0:T(8,128)(2,1)S(1)}, bf16[96,1024]{1,0:T(8,128)(2,1)S(1)}, u32[]{:S(2)}, u32[]{:S(2)}) collective-permute-start(bf16[96,1024]{1,0:T(8,128)(2,1)S(1)} %get-tuple-element.15), channel_id=1, source_target_pairs={{0,2},{1,3},{2,0},{3,1},{4,6},{5,7},{6,4},{7,5},{8,10},{9,11},{10,... | collective-permute-start | bytes 589832 | tf_op jit(solution)/shard_map/ppermute | solution.py:40
  7.9 11.5 %collective-permute-start.1 = (bf16[96,1024]{1,0:T(8,128)(2,1)S(1)}, bf16[96,1024]{1,0:T(8,128)(2,1)S(1)}, u32[]{:S(2)}, u32[]{:S(2)}) collective-permute-start(bf16[96,1024]{1,0:T(8,128)(2,1)S(1)} %get-tuple-element.15), channel_id=1, source_target_pairs={{0,4},{1,5},{2,6},{3,7},{4,0},{5,1},{6,2},{7,3},{8,12},{9,13},{10,... | collective-permute-start | bytes 589832 | tf_op jit(solution)/shard_map/ppermute | solution.py:40
  9.4 11.1 %collective-permute-start.2 = (bf16[96,1024]{1,0:T(8,128)(2,1)S(1)}, bf16[96,1024]{1,0:T(8,128)(2,1)S(1)}, u32[]{:S(2)}, u32[]{:S(2)}) collective-permute-start(bf16[96,1024]{1,0:T(8,128)(2,1)S(1)} %get-tuple-element.15), channel_id=1, source_target_pairs={{0,6},{1,7},{2,4},{3,5},{4,2},{5,3},{6,0},{7,1},{8,14},{9,15},{10,... | collective-permute-start | bytes 589832 | tf_op jit(solution)/shard_map/ppermute | solution.py:40
  9.9 12.1 %collective-permute-start.7 = (bf16[96,1024]{1,0:T(8,128)(2,1)S(1)}, bf16[96,1024]{1,0:T(8,128)(2,1)S(1)}, u32[]{:S(2)}, u32[]{:S(2)}) collective-permute-start(bf16[96,1024]{1,0:T(8,128)(2,1)S(1)} %get-tuple-element.15), channel_id=1, source_target_pairs={{0,8},{1,9},{2,10},{3,11},{4,12},{5,13},{6,14},{7,15},{8,0},{9,1},... | collective-permute-start | bytes 589832 | tf_op jit(solution)/shard_map/ppermute | solution.py:40
  15.6 9.3 %collective-permute-start.4 = (bf16[96,1024]{1,0:T(8,128)(2,1)S(1)}, bf16[96,1024]{1,0:T(8,128)(2,1)S(1)}, u32[]{:S(2)}, u32[]{:S(2)}) collective-permute-start(bf16[96,1024]{1,0:T(8,128)(2,1)S(1)} %collective-permute-done.3), channel_id=1, source_target_pairs={{0,2},{1,3},{2,0},{3,1},{4,6},{5,7},{6,4},{7,5},{8,10},{9,11},{10,... | collective-permute-start | bytes 589832 | tf_op jit(solution)/shard_map/ppermute | solution.py:40
  17.2 9.2 %collective-permute-start.5 = (bf16[96,1024]{1,0:T(8,128)(2,1)S(1)}, bf16[96,1024]{1,0:T(8,128)(2,1)S(1)}, u32[]{:S(2)}, u32[]{:S(2)}) collective-permute-start(bf16[96,1024]{1,0:T(8,128)(2,1)S(1)} %collective-permute-done.3), channel_id=1, source_target_pairs={{0,4},{1,5},{2,6},{3,7},{4,0},{5,1},{6,2},{7,3},{8,12},{9,13},{10,... | collective-permute-start | bytes 589832 | tf_op jit(solution)/shard_map/ppermute | solution.py:40
  19.4 11.5 %collective-permute-start.6 = (bf16[96,1024]{1,0:T(8,128)(2,1)S(1)}, bf16[96,1024]{1,0:T(8,128)(2,1)S(1)}, u32[]{:S(2)}, u32[]{:S(2)}) collective-permute-start(bf16[96,1024]{1,0:T(8,128)(2,1)S(1)} %collective-permute-done.3), channel_id=1, source_target_pairs={{0,6},{1,7},{2,4},{3,5},{4,2},{5,3},{6,0},{7,1},{8,14},{9,15},{10,... | collective-permute-start | bytes 589832 | tf_op jit(solution)/shard_map/ppermute | solution.py:40
  20.6 7.1 %collective-permute-start.11 = (bf16[96,1024]{1,0:T(8,128)(2,1)S(1)}, bf16[96,1024]{1,0:T(8,128)(2,1)S(1)}, u32[]{:S(2)}, u32[]{:S(2)}) collective-permute-start(bf16[96,1024]{1,0:T(8,128)(2,1)S(1)} %collective-permute-done.3), channel_id=1, source_target_pairs={{0,8},{1,9},{2,10},{3,11},{4,12},{5,13},{6,14},{7,15},{8,0},{9,1},... | collective-permute-start | bytes 589832 | tf_op jit(solution)/shard_map/ppermute | solution.py:40
  22.0 10.3 %collective-permute-start.8 = (bf16[96,1024]{1,0:T(8,128)(2,1)S(1)}, bf16[96,1024]{1,0:T(8,128)(2,1)S(1)}, u32[]{:S(2)}, u32[]{:S(2)}) collective-permute-start(bf16[96,1024]{1,0:T(8,128)(2,1)S(1)} %collective-permute-done.7), channel_id=1, source_target_pairs={{0,2},{1,3},{2,0},{3,1},{4,6},{5,7},{6,4},{7,5},{8,10},{9,11},{10,... | collective-permute-start | bytes 589832 | tf_op jit(solution)/shard_map/ppermute | solution.py:40
  24.9 12.1 %collective-permute-start.9 = (bf16[96,1024]{1,0:T(8,128)(2,1)S(1)}, bf16[96,1024]{1,0:T(8,128)(2,1)S(1)}, u32[]{:S(2)}, u32[]{:S(2)}) collective-permute-start(bf16[96,1024]{1,0:T(8,128)(2,1)S(1)} %collective-permute-done.7), channel_id=1, source_target_pairs={{0,4},{1,5},{2,6},{3,7},{4,0},{5,1},{6,2},{7,3},{8,12},{9,13},{10,... | collective-permute-start | bytes 589832 | tf_op jit(solution)/shard_map/ppermute | solution.py:40
  26.4 11.3 %collective-permute-start.10 = (bf16[96,1024]{1,0:T(8,128)(2,1)S(1)}, bf16[96,1024]{1,0:T(8,128)(2,1)S(1)}, u32[]{:S(2)}, u32[]{:S(2)}) collective-permute-start(bf16[96,1024]{1,0:T(8,128)(2,1)S(1)} %collective-permute-done.7), channel_id=1, source_target_pairs={{0,6},{1,7},{2,4},{3,5},{4,2},{5,3},{6,0},{7,1},{8,14},{9,15},{10,... | collective-permute-start | bytes 589832 | tf_op jit(solution)/shard_map/ppermute | solution.py:40
  27.6 12.6 %collective-permute-start.12 = (bf16[96,1024]{1,0:T(8,128)(2,1)S(1)}, bf16[96,1024]{1,0:T(8,128)(2,1)S(1)}, u32[]{:S(2)}, u32[]{:S(2)}) collective-permute-start(bf16[96,1024]{1,0:T(8,128)(2,1)S(1)} %collective-permute-done.11), channel_id=1, source_target_pairs={{0,2},{1,3},{2,0},{3,1},{4,6},{5,7},{6,4},{7,5},{8,10},{9,11},{10,... | collective-permute-start | bytes 589832 | tf_op jit(solution)/shard_map/ppermute | solution.py:40
  30.9 13.0 %collective-permute-start.13 = (bf16[96,1024]{1,0:T(8,128)(2,1)S(1)}, bf16[96,1024]{1,0:T(8,128)(2,1)S(1)}, u32[]{:S(2)}, u32[]{:S(2)}) collective-permute-start(bf16[96,1024]{1,0:T(8,128)(2,1)S(1)} %collective-permute-done.11), channel_id=1, source_target_pairs={{0,4},{1,5},{2,6},{3,7},{4,0},{5,1},{6,2},{7,3},{8,12},{9,13},{10,... | collective-permute-start | bytes 589832 | tf_op jit(solution)/shard_map/ppermute | solution.py:40
  32.3 12.3 %collective-permute-start.14 = (bf16[96,1024]{1,0:T(8,128)(2,1)S(1)}, bf16[96,1024]{1,0:T(8,128)(2,1)S(1)}, u32[]{:S(2)}, u32[]{:S(2)}) collective-permute-start(bf16[96,1024]{1,0:T(8,128)(2,1)S(1)} %collective-permute-done.11), channel_id=1, source_target_pairs={{0,6},{1,7},{2,4},{3,5},{4,2},{5,3},{6,0},{7,1},{8,14},{9,15},{10,... | collective-permute-start | bytes 589832 | tf_op jit(solution)/shard_map/ppermute | solution.py:40
  45.4 5.7 %collective-permute-start.15 = (bf16[1536,1024]{1,0:T(8,128)(2,1)S(1)}, bf16[1536,1024]{1,0:T(8,128)(2,1)S(1)}, u32[]{:S(2)}, u32[]{:S(2)}) collective-permute-start(bf16[1536,1024]{1,0:T(8,128)(2,1)S(1)} %get-tuple-element.16), channel_id=1, source_target_pairs={{0,1},{1,0},{2,3},{3,2},{4,5},{5,4},{6,7},{7,6},{8,9},{9,8},{10,11... | collective-permute-start | bytes 9437192 | tf_op jit(solution)/shard_map/ppermute | solution.py:40

commit v3 on v1

--- a/solution.py
+++ b/solution.py
@@ -1,3 +1,4 @@
+import functools
 import math
 
 import jax
@@ -15,7 +16,9 @@
 SUB = 8
 LANES = 128
 TILE = 256
+PACK = 16
 CHUNK = 512
+REST = 128
 VMEM_BYTES = 60 << 20
 EXACT = lax.Precision.HIGHEST
 
@@ -35,52 +38,135 @@
     return high, (value - high.astype(jnp.float32)).astype(jnp.bfloat16)
 
 
-def chunk_of(rows):
-    return math.gcd(rows, CHUNK)
-
-
-def moments_kernel(keys_ref, mean_ref, cov_ref, total):
-    rows, dim = keys_ref.shape
-    step = chunk_of(rows)
+def flipped(value, mask):
+    size = lax.axis_size("dev")
+    return lax.ppermute(value, "dev", [(source, source ^ mask) for source in range(size)])
+
+
+def plane_of(group, near, direct):
+    if near != 8 or direct:
+        return [group] + [flipped(group, mask) for mask in range(2, near, 2)]
+    half = group.shape[0] // 2
+    side, ahead = flipped(group, 2), flipped(group, 4)
+    return [group, side, ahead, flipped(side[:half], 4), flipped(ahead[half:], 2)]
+
+
+def gather_rows(rows):
+    size = lax.axis_size("dev")
+    near, far = size // 4, size // 2
+    across, beside = flipped(rows, far), flipped(rows, near)
+    groups = [rows, across, beside, flipped(across, near)]
+    same_core = [
+        jnp.concatenate(plane_of(group, near, place == 3), axis=0)
+        for place, group in enumerate(groups)
+    ]
+    return same_core + [flipped(group, 1) for group in same_core]
+
+
+def live_of(block):
+    return block[:, :1].astype(jnp.float32) < DEAD_ABOVE
+
+
+def over_chunks(rows, body):
+    whole = rows // CHUNK
+
+    @pl.loop(0, whole)
+    def _(index):
+        body(pl.multiple_of(index * CHUNK, CHUNK), CHUNK)
+
+    @pl.loop(whole * (CHUNK // REST), pl.cdiv(rows, REST))
+    def _(index):
+        body(pl.multiple_of(index * REST, REST), REST)
+
+
+def collect(groups, keys, counts, sizes, starts, arrived, copied):
+    blocks = keys.shape[0] // LIVE_MAX
+    copies, first = [], 0
+    for place, group in enumerate(groups):
+        rows = group.shape[0]
+        copies.append(
+            pltpu.make_async_copy(group, keys.at[pl.ds(first, rows)], arrived.at[place])
+        )
+        copies[-1].start()
+        first += rows
+    first = 0
+    for place, group in enumerate(groups):
+        copies[place].wait()
+        last = first + group.shape[0] // LIVE_MAX
+
+        @pl.loop(first, last)
+        def _(block):
+            start = pl.multiple_of(block * LIVE_MAX, PACK)
+            marks = keys[pl.ds(start, LIVE_MAX), :LANES].astype(jnp.float32)
+            alive = jnp.sum((marks < DEAD_ABOVE).astype(jnp.float32), axis=0, keepdims=True)
+            counts[pl.ds(block, 1), :] = alive.astype(jnp.int32)
+
+        first = last
+    copy = pltpu.make_async_copy(counts, sizes, copied)
+    copy.start()
+    copy.wait()
+
+    def move_block(block, carry):
+        offset, count = carry
+        size = sizes[block, 0]
+        tiles = (size + PACK - 1) // PACK
+        starts[block] = offset
+
+        def move_tile(tile, unused):
+            source = pl.multiple_of(block * LIVE_MAX + tile * PACK, PACK)
+            target = pl.multiple_of(offset + tile * PACK, PACK)
+            keys[pl.ds(target, PACK), :] = keys[pl.ds(source, PACK), :]
+            return unused
+
+        lax.fori_loop(0, tiles, move_tile, 0)
+        return offset + tiles * PACK, count + size
+
+    rows, count = lax.fori_loop(0, blocks, move_block, (jnp.int32(0), jnp.int32(0)))
+
+    @pl.loop(rows // PACK, pl.cdiv(rows, REST) * (REST // PACK))
+    def _(tile):
+        target = pl.multiple_of(tile * PACK, PACK)
+        keys[pl.ds(target, PACK), :] = jnp.full((PACK, keys.shape[1]), DEAD, keys.dtype)
+
+    return rows, count
+
+
+def moments(keys, rows, count, mean_ref, work):
+    dim = keys.shape[1]
     tiles = dim // TILE
 
-    def live_of(block):
-        return block[:, :1] < DEAD_ABOVE
-
-    def add_sums(index, carry):
-        sums, count = carry
-        block = keys_ref[pl.ds(pl.multiple_of(index * step, step), step), :].astype(jnp.float32)
-        live = live_of(block)
-        part = jnp.where(live, block, 0.0).reshape(step // SUB, SUB, dim)
-        alive = live.astype(jnp.float32).reshape(step // SUB, SUB, 1)
-        return sums + jnp.sum(part, axis=0), count + jnp.sum(alive, axis=0)
-
-    start = (jnp.zeros((SUB, dim), jnp.float32), jnp.zeros((SUB, 1), jnp.float32))
-    sums, count = lax.fori_loop(0, rows // step, add_sums, start)
-    count = jnp.sum(count, axis=0, keepdims=True)
+    def add_sums(index, sums):
+        start = pl.multiple_of(index * REST, REST)
+        block = keys[pl.ds(start, REST), :]
+        part = jnp.where(live_of(block), block.astype(jnp.float32), 0.0)
+        return sums + jnp.sum(part.reshape(REST // SUB, SUB, dim), axis=0)
+
+    sums = lax.fori_loop(0, pl.cdiv(rows, REST), add_sums, jnp.zeros((SUB, dim), jnp.float32))
+    count = jnp.full((1, 1), count.astype(jnp.float32))
     mean = jnp.sum(sums, axis=0, keepdims=True) / count
-    mean_ref[...] = jnp.broadcast_to(mean, (SUB, dim))
-    total[...] = jnp.zeros_like(total)
-
-    @pl.loop(0, rows // step)
-    def _(index):
-        block = keys_ref[pl.ds(pl.multiple_of(index * step, step), step), :].astype(jnp.float32)
-        high, low = two_parts(jnp.where(live_of(block), block - mean, 0.0))
+    mean_ref[...] = mean
+    work[...] = jnp.zeros_like(work)
+
+    def add_products(start, step):
+        block = keys[pl.ds(start, step), :]
+        centred = jnp.where(live_of(block), block.astype(jnp.float32) - mean_ref[...], 0.0)
+        high, low = two_parts(centred)
         for tile in range(tiles):
             here = slice(tile * TILE, (tile + 1) * TILE)
             upto = slice(0, (tile + 1) * TILE)
             part = product(high[:, here], high[:, upto], 0, 0)
             part += product(high[:, here], low[:, upto], 0, 0)
             part += product(low[:, here], high[:, upto], 0, 0)
-            total[here, upto] += part
-
+            work[here, upto] += part
+
+    over_chunks(rows, add_products)
     for tile in range(tiles):
         here = slice(tile * TILE, (tile + 1) * TILE)
         upto = slice(0, (tile + 1) * TILE)
         shape = (TILE, (tile + 1) * TILE)
         down = lax.broadcasted_iota(jnp.int32, shape, 0) + tile * TILE
         across = lax.broadcasted_iota(jnp.int32, shape, 1)
-        cov_ref[here, upto] = total[here, upto] / count + jnp.where(down == across, RIDGE, 0.0)
+        work[here, upto] = work[here, upto] / count + jnp.where(down == across, RIDGE, 0.0)
 
 
 def invert_factor(rows, inverse):
@@ -126,11 +212,10 @@
     return inverse
 
 
-def whitener_kernel(cov_ref, high_ref, low_ref, work, found, block, part):
-    dim = cov_ref.shape[0]
-    work[...] = cov_ref[...]
+def whitener(work, found, block, part, high_ref, low_ref):
+    dim = work.shape[0]
     found[...] = jnp.zeros_like(found)
-    block[...] = cov_ref[0:LANES, 0:LANES]
+    block[...] = work[0:LANES, 0:LANES]
     count = LANES // SUB
 
     @pl.loop(0, dim // LANES)
@@ -179,17 +264,13 @@
     low_ref[...] = low
 
 
-def scores_kernel(
-    place_ref, keys_ref, own_ref, mean_ref, high_ref, low_ref, log_ref, out_ref, density, total
-):
-    rows, dim = keys_ref.shape
+def scores(keys, rows, own_ref, own_size, own_start, mean_ref, high_ref, low_ref, density, total):
+    dim = keys.shape[1]
     queries = own_ref.shape[0]
-    step = chunk_of(rows)
     sharpness = 2.0 * math.sqrt(dim)
-    mean = mean_ref[0:1, :]
 
     def whitened(values):
-        high, low = two_parts(values.astype(jnp.float32) - mean)
+        high, low = two_parts(values.astype(jnp.float32) - mean_ref[...])
         parts = []
         for tile in range(dim // TILE):
             here = slice(tile * TILE, (tile + 1) * TILE)
@@ -209,97 +290,98 @@
     density[...] = jnp.zeros_like(density)
     total[...] = jnp.zeros_like(total)
 
-    @pl.loop(0, rows // step)
-    def _(index):
-        start = pl.multiple_of(index * step, step)
-        block = keys_ref[pl.ds(start, step), :]
-        live = block[:, :1].astype(jnp.float32) < DEAD_ABOVE
+    def add_keys(start, step):
+        block = keys[pl.ds(start, step), :]
         white = whitened(block)
         inner = product(white, query, 1, 1)
         scores = sharpness * (lengths(white) * query_norm * inner - 1.0)
         shape = (step, queries)
         key_index = start + lax.broadcasted_iota(jnp.int32, shape, 0)
-        query_index = place_ref[0] + lax.broadcasted_iota(jnp.int32, shape, 1)
-        seen = live & (key_index != query_index)
+        query_index = own_start + lax.broadcasted_iota(jnp.int32, shape, 1)
+        seen = live_of(block) & (key_index != query_index)
         weights = jnp.where(seen, jnp.exp(scores), 0.0)
         density[...] += jnp.sum(weights, axis=0, keepdims=True)
         total[...] += product(weights.astype(jnp.bfloat16), white, 0, 0)
 
-    own_size = place_ref[1]
+    over_chunks(rows, add_keys)
     dense = density[...]
     lane = lax.broadcasted_iota(jnp.int32, dense.shape, 1)
-    log_ref[...] = jnp.where(lane < own_size, jnp.log(dense), 0.0)
+    logs = jnp.where(lane < own_size, jnp.log(dense), 0.0)
     divisor = jnp.broadcast_to(dense, (queries, queries)).T[:, 0:1]
     sublane = lax.broadcasted_iota(jnp.int32, (queries, 1), 0)
-    out_ref[...] = jnp.where(sublane < own_size, total[...] / divisor, 0.0).astype(jnp.bfloat16)
-
-
-def whole(count):
-    return [pl.BlockSpec(memory_space=pltpu.VMEM)] * count
+    means = jnp.where(sublane < own_size, total[...] / divisor, 0.0).astype(jnp.bfloat16)
+    return logs, means
+
+
+def local_kernel(group_count, size_ref, own_ref, *refs):
+    groups, refs = refs[:group_count], refs[group_count:]
+    log_ref, out_ref, keys, counts, sizes, starts, arrived, copied = refs[:8]
+    mean_ref, work, found, block, part, high_ref, low_ref, density, total = refs[8:]
+    rows, count = collect(groups, keys, counts, sizes, starts, arrived, copied)
+    moments(keys, rows, count, mean_ref, work)
+    whitener(work, found, block, part, high_ref, low_ref)
+    block_count = size_ref.shape[0]
+    block_rows = own_ref.shape[0] // block_count
+    for here in range(block_count):
+        span = slice(here * block_rows, (here + 1) * block_rows)
+        log_ref[here : here + 1, :], out_ref[span, :] = scores(
+            keys,
+            rows,
+            own_ref.at[span],
+            size_ref[here],
+            starts[here],
+            mean_ref,
+            high_ref,
+            low_ref,
+            density,
+            total,
+        )
 
 
 def shards(states, bucket_sizes):
     row_count, dim = states.shape
     block_count = bucket_sizes.shape[0]
     block_rows = row_count // block_count
-    params = pltpu.CompilerParams(vmem_limit_bytes=VMEM_BYTES)
-    square = (dim, dim)
     in_block = jnp.arange(LIVE_MAX, dtype=jnp.int32)
     own_live = (in_block[None, :] < bucket_sizes[:, None])[:, :, None]
     prefix = states.reshape(block_count, block_rows, dim)[:, :LIVE_MAX]
     sent = jnp.where(own_live, prefix, jnp.bfloat16(DEAD)).reshape(-1, dim)
-    keys = lax.all_gather(sent, "dev", axis=0, tiled=True)
-    mean, covariance = pl.pallas_call(
-        moments_kernel,
+    groups = gather_rows(sent)
+    key_rows = sum(group.shape[0] for group in groups)
+    blocks = key_rows // LIVE_MAX
+    square = (dim, dim)
+    logs, means = pl.pallas_call(
+        functools.partial(local_kernel, len(groups)),
         out_shape=[
-            jax.ShapeDtypeStruct((SUB, dim), jnp.float32),
-            jax.ShapeDtypeStruct(square, jnp.float32),
+            jax.ShapeDtypeStruct((block_count, block_rows), jnp.float32),
+            jax.ShapeDtypeStruct((row_count, dim), jnp.bfloat16),
         ],
-        in_specs=whole(1),
-        out_specs=whole(2),
-        scratch_shapes=[pltpu.VMEM(square, jnp.float32)],
-        compiler_params=params,
-    )(keys)
-    high, low = pl.pallas_call(
-        whitener_kernel,
-        out_shape=[jax.ShapeDtypeStruct(square, jnp.bfloat16)] * 2,
-        in_specs=whole(1),
-        out_specs=whole(2),
+        in_specs=[
+            pl.BlockSpec(memory_space=pltpu.SMEM),
+            pl.BlockSpec(memory_space=pltpu.VMEM),
+        ]
+        + [pl.BlockSpec(memory_space=pl.ANY)] * len(groups),
+        out_specs=[pl.BlockSpec(memory_space=pltpu.VMEM)] * 2,
         scratch_shapes=[
+            pltpu.VMEM((key_rows, dim), jnp.bfloat16),
+            pltpu.VMEM((blocks, LANES), jnp.int32),
+            pltpu.SMEM((blocks, LANES), jnp.int32),
+            pltpu.SMEM((blocks,), jnp.int32),
+            pltpu.SemaphoreType.DMA((len(groups),)),
+            pltpu.SemaphoreType.DMA,
+            pltpu.VMEM((1, dim), jnp.float32),
             pltpu.VMEM(square, jnp.float32),
             pltpu.VMEM(square, jnp.float32),
             pltpu.VMEM((LANES, LANES), jnp.float32),
             pltpu.VMEM((LANES, LANES), jnp.float32),
+            pltpu.VMEM(square, jnp.bfloat16),
+            pltpu.VMEM(square, jnp.bfloat16),
+            pltpu.VMEM((1, block_rows), jnp.float32),
+            pltpu.VMEM((block_rows, dim), jnp.float32),
         ],
-        compiler_params=params,
-    )(covariance)
-    logs, means = [], []
-    for here in range(block_count):
-        place = (lax.axis_index("dev") * block_count + here) * LIVE_MAX
-        log_part, mean_part = pl.pallas_call(
-            scores_kernel,
-            out_shape=[
-                jax.ShapeDtypeStruct((1, block_rows), jnp.float32),
-                jax.ShapeDtypeStruct((block_rows, dim), jnp.bfloat16),
-            ],
-            in_specs=[pl.BlockSpec(memory_space=pltpu.SMEM)] + whole(5),
-            out_specs=whole(2),
-            scratch_shapes=[
-                pltpu.VMEM((1, block_rows), jnp.float32),
-                pltpu.VMEM((block_rows, dim), jnp.float32),
-            ],
-            compiler_params=params,
-        )(
-            jnp.stack([place, bucket_sizes[here]]),
-            keys,
-            lax.slice_in_dim(states, here * block_rows, (here + 1) * block_rows),
-            mean,
-            high,
-            low,
-        )
-        logs.append(log_part.reshape(block_rows))
-        means.append(mean_part)
-    return jnp.concatenate(logs), jnp.concatenate(means)
+        compiler_params=pltpu.CompilerParams(vmem_limit_bytes=VMEM_BYTES),
+    )(bucket_sizes, states, *groups)
+    return logs.reshape(row_count), means
 
 
 def solution(mesh):

time: 190 us -> 136 us (0.72)
  waiting for transfers between devices: 73.5 us -> 21 us
  starting transfers between devices: 0.04 us -> 23.6 us
  between operations: 14.7 us -> 1.7 us
  Pallas kernels: 98.9 us -> 87.5 us
    all_gather x1 -> x0, waiting for transfers between devices: 73.5 us -> none  [shards(): keys = lax.all_gather(sent, 'dev', axis=0, tiled=True)]
    ppermute x0 -> x22, starting transfers between devices: none -> 23.6 us  [flipped(): lax.ppermute(value, 'dev', [(source, source ^ mask) for source in range(s...]
    ppermute x0 -> x22, waiting for transfers between devices: none -> 21 us  [flipped(): lax.ppermute(value, 'dev', [(source, source ^ mask) for source in range(s...]
    pallas_call x3 -> x1, Pallas kernels: 98.9 us -> 87.5 us  [shards(): pl.pallas_call(functools.partial(local_kernel, len(groups)), out_shape=[j...]
  transfers between devices with their start and end apart: 1 -> 22, of which waited for: 1 -> 8; matrix products, arithmetic and copies ran while one was open for 0% -> 0% of each run, Pallas kernels for 0% -> 0%
where the time goes in v3:
time: 136 us
  Pallas kernels  87.5 us (64%)
  starting transfers between devices  23.6 us (17%)
  waiting for transfers between devices  21 us (15%)
  between operations  1.7 us (1%)
    pallas_call x1, Pallas kernels, shards(): pl.pallas_call(functools.partial(local_kernel, len(groups)), out_shape=[j...  87.5 us
    ppermute x22, starting transfers between devices, flipped(): lax.ppermute(value, 'dev', [(source, source ^ mask) for source in range(s...  23.6 us
    ppermute x22, waiting for transfers between devices, flipped(): lax.ppermute(value, 'dev', [(source, source ^ mask) for source in range(s...  21 us
  transfers between devices with their start and end apart: 22, of which 8 were waited for; matrix products, arithmetic and copies ran while one was open for 0% of the time, Pallas kernels for 0%

profile of v3, /device:TPU:0, one launch (start us, length us, event | category | flops | bytes accessed | tf_op | source)
XLA Modules:
  0.0 136.0 jit_solution(9260794094427916196)
XLA Ops:
  1.3 1.0 constant_dynamic-update-slice_fusion.4
  2.3 3.0 %collective-permute-start.1 = (bf16[96,1024]{1,0:T(8,128)(2,1)S(1)}, bf16[96,1024]{1,0:T(8,128)(2,1)S(1)}, u32[]{:S(2)}, u32[]{:S(2)}) collective-permute-start(bf16[96,1024]{1,0:T(8,128)(2,1)S(1)} %get-tuple-element.7), channel_id=1, source_target_pairs={{0,4},{1,5},{2,6},{3,7},{4,0},{5,1},{6,2},{7,3},{8,12},{9,13},{10,... | collective-permute-start | bytes 589832 | tf_op jit(solution)/shard_map/ppermute | solution.py:43
  5.4 1.5 %collective-permute-start = (bf16[96,1024]{1,0:T(8,128)(2,1)S(1)}, bf16[96,1024]{1,0:T(8,128)(2,1)S(1)}, u32[]{:S(2)}, u32[]{:S(2)}) collective-permute-start(bf16[96,1024]{1,0:T(8,128)(2,1)S(1)} %get-tuple-element.7), channel_id=1, source_target_pairs={{0,2},{1,3},{2,0},{3,1},{4,6},{5,7},{6,4},{7,5},{8,10},{9,11},{10,... | collective-permute-start | bytes 589832 | tf_op jit(solution)/shard_map/ppermute | solution.py:43
  6.8 2.6 %collective-permute-start.4 = (bf16[96,1024]{1,0:T(8,128)(2,1)S(1)}, bf16[96,1024]{1,0:T(8,128)(2,1)S(1)}, u32[]{:S(2)}, u32[]{:S(2)}) collective-permute-start(bf16[96,1024]{1,0:T(8,128)(2,1)S(1)} %get-tuple-element.7), channel_id=1, source_target_pairs={{0,16},{1,17},{2,18},{3,19},{4,20},{5,21},{6,22},{7,23},{8,24},{9,... | collective-permute-start | bytes 589832 | tf_op jit(solution)/shard_map/ppermute | solution.py:43
  9.4 1.6 %collective-permute-start.9 = (bf16[96,1024]{1,0:T(8,128)(2,1)S(1)}, bf16[96,1024]{1,0:T(8,128)(2,1)S(1)}, u32[]{:S(2)}, u32[]{:S(2)}) collective-permute-start(bf16[96,1024]{1,0:T(8,128)(2,1)S(1)} %get-tuple-element.7), channel_id=1, source_target_pairs={{0,8},{1,9},{2,10},{3,11},{4,12},{5,13},{6,14},{7,15},{8,0},{9,1},... | collective-permute-start | bytes 589832 | tf_op jit(solution)/shard_map/ppermute | solution.py:43
  11.0 0.0 collective-permute-done.1
  11.0 1.0 collective-permute-start.3
  12.0 0.0 collective-permute-done
  12.1 1.6 %collective-permute-start.2 = (bf16[48,1024]{1,0:T(8,128)(2,1)S(1)}, bf16[48,1024]{1,0:T(8,128)(2,1)S(1)}, u32[]{:S(2)}, u32[]{:S(2)}) collective-permute-start(bf16[48,1024]{1,0:T(8,128)(2,1)S(1)} %slice.29), channel_id=1, source_target_pairs={{0,4},{1,5},{2,6},{3,7},{4,0},{5,1},{6,2},{7,3},{8,12},{9,13},{10,... | collective-permute-start | bytes 294920 | tf_op jit(solution)/shard_map/ppermute | solution.py:43
  13.6 4.5 %collective-permute-done.4 = bf16[96,1024]{1,0:T(8,128)(2,1)S(1)} collective-permute-done((bf16[96,1024]{1,0:T(8,128)(2,1)S(1)}, bf16[96,1024]{1,0:T(8,128)(2,1)S(1)}, u32[]{:S(2)}, u32[]{:S(2)}) %collective-permute-start.4) | collective-permute-done | bytes 196640 | tf_op jit(solution)/shard_map/ppermute | solution.py:43
  18.1 0.5 collective-permute-start.6
  18.7 0.5 collective-permute-start.5
  19.1 0.0 collective-permute-done.9
  19.1 1.6 %collective-permute-start.11 = (bf16[96,1024]{1,0:T(8,128)(2,1)S(1)}, bf16[96,1024]{1,0:T(8,128)(2,1)S(1)}, u32[]{:S(2)}, u32[]{:S(2)}) collective-permute-start(bf16[96,1024]{1,0:T(8,128)(2,1)S(1)} %collective-permute-done.9), channel_id=1, source_target_pairs={{0,4},{1,5},{2,6},{3,7},{4,0},{5,1},{6,2},{7,3},{8,12},{9,13},{10,... | collective-permute-start | bytes 589832 | tf_op jit(solution)/shard_map/ppermute | solution.py:43
  20.8 0.0 collective-permute-done.2
  20.8 1.6 %collective-permute-start.10 = (bf16[96,1024]{1,0:T(8,128)(2,1)S(1)}, bf16[96,1024]{1,0:T(8,128)(2,1)S(1)}, u32[]{:S(2)}, u32[]{:S(2)}) collective-permute-start(bf16[96,1024]{1,0:T(8,128)(2,1)S(1)} %collective-permute-done.9), channel_id=1, source_target_pairs={{0,2},{1,3},{2,0},{3,1},{4,6},{5,7},{6,4},{7,5},{8,10},{9,11},{10,... | collective-permute-start | bytes 589832 | tf_op jit(solution)/shard_map/ppermute | solution.py:43
  22.4 0.0 collective-permute-done.3
  22.4 0.7 collective-permute-start.14
  23.1 2.8 %collective-permute-done.6 = bf16[96,1024]{1,0:T(8,128)(2,1)S(1)} collective-permute-done((bf16[96,1024]{1,0:T(8,128)(2,1)S(1)}, bf16[96,1024]{1,0:T(8,128)(2,1)S(1)}, u32[]{:S(2)}, u32[]{:S(2)}) %collective-permute-start.6) | collective-permute-done | bytes 196640 | tf_op jit(solution)/shard_map/ppermute | solution.py:43
  25.9 0.0 collective-permute-start.18
  25.9 0.2 collective-permute-done.5
  26.1 0.5 collective-permute-start.8
  26.7 1.3 collective-permute-done.11
  28.0 0.5 collective-permute-start.7
  28.5 0.0 collective-permute-done.10
  28.5 1.3 collective-permute-start.13
  29.9 0.0 collective-permute-done.14
  29.9 0.9 collective-permute-start.12
  30.8 3.7 %collective-permute-done.12 = bf16[48,1024]{1,0:T(8,128)(2,1)S(1)} collective-permute-done((bf16[48,1024]{1,0:T(8,128)(2,1)S(1)}, bf16[48,1024]{1,0:T(8,128)(2,1)S(1)}, u32[]{:S(2)}, u32[]{:S(2)}) %collective-permute-start.12) | collective-permute-done | bytes 98336 | tf_op jit(solution)/shard_map/ppermute | solution.py:43
  34.6 1.7 %collective-permute-start.17 = (bf16[96,1024]{1,0:T(8,128)(2,1)S(1)}, bf16[96,1024]{1,0:T(8,128)(2,1)S(1)}, u32[]{:S(2)}, u32[]{:S(2)}) collective-permute-start(bf16[96,1024]{1,0:T(8,128)(2,1)S(1)} %collective-permute-done.14), channel_id=1, source_target_pairs={{0,6},{1,7},{2,4},{3,5},{4,2},{5,3},{6,0},{7,1},{8,14},{9,15},{10,... | collective-permute-start | bytes 589832 | tf_op jit(solution)/shard_map/ppermute | solution.py:43
  36.3 0.0 collective-permute-done.7
  36.3 0.6 collective-permute-start.16
  36.9 0.0 collective-permute-done.8
  36.9 1.3 collective-permute-start.15
  38.2 0.0 collective-permute-done.13
  38.2 0.1 collective-permute-start.19
  38.4 6.4 %collective-permute-done.15 = bf16[96,1024]{1,0:T(8,128)(2,1)S(1)} collective-permute-done((bf16[96,1024]{1,0:T(8,128)(2,1)S(1)}, bf16[96,1024]{1,0:T(8,128)(2,1)S(1)}, u32[]{:S(2)}, u32[]{:S(2)}) %collective-permute-start.15) | collective-permute-done | bytes 196640 | tf_op jit(solution)/shard_map/ppermute | solution.py:43
  44.8 0.0 collective-permute-start.20
  44.8 0.0 collective-permute-done.16
  44.8 0.0 collective-permute-done.17
  44.9 0.6 collective-permute-start.21
  45.5 0.0 collective-permute-done.18.refs_4_
  45.5 0.0 collective-permute-done.19.refs_5_
  45.5 1.6 %collective-permute-done.20.refs_6_ = bf16[384,1024]{1,0:T(8,128)(2,1)S(1)} collective-permute-done((bf16[384,1024]{1,0:T(8,128)(2,1)S(1)}, bf16[384,1024]{1,0:T(8,128)(2,1)S(1)}, u32[]{:S(2)}, u32[]{:S(2)}) %collective-permute-start.20) | collective-permute-done | bytes 786464 | tf_op jit(solution)/shard_map/ppermute | solution.py:43
  47.1 0.9 copy-done.6
  48.0 0.3 collective-permute-done.21.refs_7_
  48.3 0.0 copy-done
  48.4 87.5 %shard_map.41 = (f32[1,128]{1,0:T(1,128)}, bf16[128,1024]{1,0:T(8,128)(2,1)}) custom-call(s32[1]{0:T(128)} %copy.19.size_ref, bf16[128,1024]{1,0:T(8,128)(2,1)} %own_ref.1, bf16[384,1024]{1,0:T(8,128)(2,1)} %copy-done.3, bf16[384,1024]{1,0:T(8,128)(2,1)} %copy-done, bf16[384,1024]{1,0:T(8,128)(2,1)} %copy-done.1, bf16[384,1024]{1,0:T(8,128)(2,1)} %copy-done.2, ...), custom_call_target="tpu_custom_call" | custom-call | tf_op jit(solution)/shard_map/pallas_call | solution.py:353
  (37 shorter events, 0.3 us)
Async XLA Ops:
  2.3 8.7 %collective-permute-start.1 = (bf16[96,1024]{1,0:T(8,128)(2,1)S(1)}, bf16[96,1024]{1,0:T(8,128)(2,1)S(1)}, u32[]{:S(2)}, u32[]{:S(2)}) collective-permute-start(bf16[96,1024]{1,0:T(8,128)(2,1)S(1)} %get-tuple-element.7), channel_id=1, source_target_pairs={{0,4},{1,5},{2,6},{3,7},{4,0},{5,1},{6,2},{7,3},{8,12},{9,13},{10,... | collective-permute-start | bytes 589832 | tf_op jit(solution)/shard_map/ppermute | solution.py:43
  5.4 6.7 %collective-permute-start = (bf16[96,1024]{1,0:T(8,128)(2,1)S(1)}, bf16[96,1024]{1,0:T(8,128)(2,1)S(1)}, u32[]{:S(2)}, u32[]{:S(2)}) collective-permute-start(bf16[96,1024]{1,0:T(8,128)(2,1)S(1)} %get-tuple-element.7), channel_id=1, source_target_pairs={{0,2},{1,3},{2,0},{3,1},{4,6},{5,7},{6,4},{7,5},{8,10},{9,11},{10,... | collective-permute-start | bytes 589832 | tf_op jit(solution)/shard_map/ppermute | solution.py:43
  6.8 11.3 %collective-permute-start.4 = (bf16[96,1024]{1,0:T(8,128)(2,1)S(1)}, bf16[96,1024]{1,0:T(8,128)(2,1)S(1)}, u32[]{:S(2)}, u32[]{:S(2)}) collective-permute-start(bf16[96,1024]{1,0:T(8,128)(2,1)S(1)} %get-tuple-element.7), channel_id=1, source_target_pairs={{0,16},{1,17},{2,18},{3,19},{4,20},{5,21},{6,22},{7,23},{8,24},{9,... | collective-permute-start | bytes 589832 | tf_op jit(solution)/shard_map/ppermute | solution.py:43
  9.4 9.7 %collective-permute-start.9 = (bf16[96,1024]{1,0:T(8,128)(2,1)S(1)}, bf16[96,1024]{1,0:T(8,128)(2,1)S(1)}, u32[]{:S(2)}, u32[]{:S(2)}) collective-permute-start(bf16[96,1024]{1,0:T(8,128)(2,1)S(1)} %get-tuple-element.7), channel_id=1, source_target_pairs={{0,8},{1,9},{2,10},{3,11},{4,12},{5,13},{6,14},{7,15},{8,0},{9,1},... | collective-permute-start | bytes 589832 | tf_op jit(solution)/shard_map/ppermute | solution.py:43
  11.0 11.3 %collective-permute-start.3 = (bf16[48,1024]{1,0:T(8,128)(2,1)S(1)}, bf16[48,1024]{1,0:T(8,128)(2,1)S(1)}, u32[]{:S(2)}, u32[]{:S(2)}) collective-permute-start(bf16[48,1024]{1,0:T(8,128)(2,1)S(1)} %slice.30), channel_id=1, source_target_pairs={{0,2},{1,3},{2,0},{3,1},{4,6},{5,7},{6,4},{7,5},{8,10},{9,11},{10,... | collective-permute-start | bytes 294920 | tf_op jit(solution)/shard_map/ppermute | solution.py:43
  12.1 8.7 %collective-permute-start.2 = (bf16[48,1024]{1,0:T(8,128)(2,1)S(1)}, bf16[48,1024]{1,0:T(8,128)(2,1)S(1)}, u32[]{:S(2)}, u32[]{:S(2)}) collective-permute-start(bf16[48,1024]{1,0:T(8,128)(2,1)S(1)} %slice.29), channel_id=1, source_target_pairs={{0,4},{1,5},{2,6},{3,7},{4,0},{5,1},{6,2},{7,3},{8,12},{9,13},{10,... | collective-permute-start | bytes 294920 | tf_op jit(solution)/shard_map/ppermute | solution.py:43
  18.1 7.7 %collective-permute-start.6 = (bf16[96,1024]{1,0:T(8,128)(2,1)S(1)}, bf16[96,1024]{1,0:T(8,128)(2,1)S(1)}, u32[]{:S(2)}, u32[]{:S(2)}) collective-permute-start(bf16[96,1024]{1,0:T(8,128)(2,1)S(1)} %collective-permute-done.4), channel_id=1, source_target_pairs={{0,4},{1,5},{2,6},{3,7},{4,0},{5,1},{6,2},{7,3},{8,12},{9,13},{10,... | collective-permute-start | bytes 589832 | tf_op jit(solution)/shard_map/ppermute | solution.py:43
  18.7 7.5 %collective-permute-start.5 = (bf16[96,1024]{1,0:T(8,128)(2,1)S(1)}, bf16[96,1024]{1,0:T(8,128)(2,1)S(1)}, u32[]{:S(2)}, u32[]{:S(2)}) collective-permute-start(bf16[96,1024]{1,0:T(8,128)(2,1)S(1)} %collective-permute-done.4), channel_id=1, source_target_pairs={{0,2},{1,3},{2,0},{3,1},{4,6},{5,7},{6,4},{7,5},{8,10},{9,11},{10,... | collective-permute-start | bytes 589832 | tf_op jit(solution)/shard_map/ppermute | solution.py:43
  19.1 8.9 %collective-permute-start.11 = (bf16[96,1024]{1,0:T(8,128)(2,1)S(1)}, bf16[96,1024]{1,0:T(8,128)(2,1)S(1)}, u32[]{:S(2)}, u32[]{:S(2)}) collective-permute-start(bf16[96,1024]{1,0:T(8,128)(2,1)S(1)} %collective-permute-done.9), channel_id=1, source_target_pairs={{0,4},{1,5},{2,6},{3,7},{4,0},{5,1},{6,2},{7,3},{8,12},{9,13},{10,... | collective-permute-start | bytes 589832 | tf_op jit(solution)/shard_map/ppermute | solution.py:43
  20.8 7.7 %collective-permute-start.10 = (bf16[96,1024]{1,0:T(8,128)(2,1)S(1)}, bf16[96,1024]{1,0:T(8,128)(2,1)S(1)}, u32[]{:S(2)}, u32[]{:S(2)}) collective-permute-start(bf16[96,1024]{1,0:T(8,128)(2,1)S(1)} %collective-permute-done.9), channel_id=1, source_target_pairs={{0,2},{1,3},{2,0},{3,1},{4,6},{5,7},{6,4},{7,5},{8,10},{9,11},{10,... | collective-permute-start | bytes 589832 | tf_op jit(solution)/shard_map/ppermute | solution.py:43
  22.4 7.5 %collective-permute-start.14 = (bf16[96,1024]{1,0:T(8,128)(2,1)S(1)}, bf16[96,1024]{1,0:T(8,128)(2,1)S(1)}, u32[]{:S(2)}, u32[]{:S(2)}) collective-permute-start(bf16[96,1024]{1,0:T(8,128)(2,1)S(1)} %collective-permute-done.4), channel_id=1, source_target_pairs={{0,8},{1,9},{2,10},{3,11},{4,12},{5,13},{6,14},{7,15},{8,0},{9,1},... | collective-permute-start | bytes 589832 | tf_op jit(solution)/shard_map/ppermute | solution.py:43
  23.0 6.8 %copy-start.3 = (bf16[384,1024]{1,0:T(8,128)(2,1)}, bf16[384,1024]{1,0:T(8,128)(2,1)S(1)}, u32[]{:S(2)}) copy-start(bf16[384,1024]{1,0:T(8,128)(2,1)S(1)} %constant_dynamic-update-slice_fusion.refs_0_) | copy-start | bytes 2359300
  25.9 19.6 %collective-permute-start.18 = (bf16[384,1024]{1,0:T(8,128)(2,1)S(1)}, bf16[384,1024]{1,0:T(8,128)(2,1)S(1)}, u32[]{:S(2)}, u32[]{:S(2)}) collective-permute-start(bf16[384,1024]{1,0:T(8,128)(2,1)S(1)} %constant_dynamic-update-slice_fusion.refs_0_), channel_id=1, source_target_pairs={{0,1},{1,0},{2,3},{3,2},{4,5},{5,4},{6,7},{7,6},{8,9},{9,8},{10,11... | collective-permute-start | bytes 2359304 | tf_op jit(solution)/shard_map/ppermute | solution.py:43
  26.1 10.8 %collective-permute-start.8 = (bf16[48,1024]{1,0:T(8,128)(2,1)S(1)}, bf16[48,1024]{1,0:T(8,128)(2,1)S(1)}, u32[]{:S(2)}, u32[]{:S(2)}) collective-permute-start(bf16[48,1024]{1,0:T(8,128)(2,1)S(1)} %slice.32), channel_id=1, source_target_pairs={{0,2},{1,3},{2,0},{3,1},{4,6},{5,7},{6,4},{7,5},{8,10},{9,11},{10,... | collective-permute-start | bytes 294920 | tf_op jit(solution)/shard_map/ppermute | solution.py:43
  28.0 8.3 %collective-permute-start.7 = (bf16[48,1024]{1,0:T(8,128)(2,1)S(1)}, bf16[48,1024]{1,0:T(8,128)(2,1)S(1)}, u32[]{:S(2)}, u32[]{:S(2)}) collective-permute-start(bf16[48,1024]{1,0:T(8,128)(2,1)S(1)} %slice.31), channel_id=1, source_target_pairs={{0,4},{1,5},{2,6},{3,7},{4,0},{5,1},{6,2},{7,3},{8,12},{9,13},{10,... | collective-permute-start | bytes 294920 | tf_op jit(solution)/shard_map/ppermute | solution.py:43
  28.5 9.7 %collective-permute-start.13 = (bf16[48,1024]{1,0:T(8,128)(2,1)S(1)}, bf16[48,1024]{1,0:T(8,128)(2,1)S(1)}, u32[]{:S(2)}, u32[]{:S(2)}) collective-permute-start(bf16[48,1024]{1,0:T(8,128)(2,1)S(1)} %slice.34), channel_id=1, source_target_pairs={{0,2},{1,3},{2,0},{3,1},{4,6},{5,7},{6,4},{7,5},{8,10},{9,11},{10,... | collective-permute-start | bytes 294920 | tf_op jit(solution)/shard_map/ppermute | solution.py:43
  29.9 4.7 %collective-permute-start.12 = (bf16[48,1024]{1,0:T(8,128)(2,1)S(1)}, bf16[48,1024]{1,0:T(8,128)(2,1)S(1)}, u32[]{:S(2)}, u32[]{:S(2)}) collective-permute-start(bf16[48,1024]{1,0:T(8,128)(2,1)S(1)} %slice.33), channel_id=1, source_target_pairs={{0,4},{1,5},{2,6},{3,7},{4,0},{5,1},{6,2},{7,3},{8,12},{9,13},{10,... | collective-permute-start | bytes 294920 | tf_op jit(solution)/shard_map/ppermute | solution.py:43
  34.6 10.3 %collective-permute-start.17 = (bf16[96,1024]{1,0:T(8,128)(2,1)S(1)}, bf16[96,1024]{1,0:T(8,128)(2,1)S(1)}, u32[]{:S(2)}, u32[]{:S(2)}) collective-permute-start(bf16[96,1024]{1,0:T(8,128)(2,1)S(1)} %collective-permute-done.14), channel_id=1, source_target_pairs={{0,6},{1,7},{2,4},{3,5},{4,2},{5,3},{6,0},{7,1},{8,14},{9,15},{10,... | collective-permute-start | bytes 589832 | tf_op jit(solution)/shard_map/ppermute | solution.py:43
  36.3 8.5 %collective-permute-start.16 = (bf16[96,1024]{1,0:T(8,128)(2,1)S(1)}, bf16[96,1024]{1,0:T(8,128)(2,1)S(1)}, u32[]{:S(2)}, u32[]{:S(2)}) collective-permute-start(bf16[96,1024]{1,0:T(8,128)(2,1)S(1)} %collective-permute-done.14), channel_id=1, source_target_pairs={{0,4},{1,5},{2,6},{3,7},{4,0},{5,1},{6,2},{7,3},{8,12},{9,13},{10,... | collective-permute-start | bytes 589832 | tf_op jit(solution)/shard_map/ppermute | solution.py:43
  36.9 7.9 %collective-permute-start.15 = (bf16[96,1024]{1,0:T(8,128)(2,1)S(1)}, bf16[96,1024]{1,0:T(8,128)(2,1)S(1)}, u32[]{:S(2)}, u32[]{:S(2)}) collective-permute-start(bf16[96,1024]{1,0:T(8,128)(2,1)S(1)} %collective-permute-done.14), channel_id=1, source_target_pairs={{0,2},{1,3},{2,0},{3,1},{4,6},{5,7},{6,4},{7,5},{8,10},{9,11},{10,... | collective-permute-start | bytes 589832 | tf_op jit(solution)/shard_map/ppermute | solution.py:43
  38.2 10.1 %copy-start = (bf16[384,1024]{1,0:T(8,128)(2,1)}, bf16[384,1024]{1,0:T(8,128)(2,1)S(1)}, u32[]{:S(2)}) copy-start(bf16[384,1024]{1,0:T(8,128)(2,1)S(1)} %constant_dynamic-update-slice_fusion.5.refs_1_) | copy-start | bytes 2359300
  38.2 7.2 %collective-permute-start.19 = (bf16[384,1024]{1,0:T(8,128)(2,1)S(1)}, bf16[384,1024]{1,0:T(8,128)(2,1)S(1)}, u32[]{:S(2)}, u32[]{:S(2)}) collective-permute-start(bf16[384,1024]{1,0:T(8,128)(2,1)S(1)} %constant_dynamic-update-slice_fusion.5.refs_1_), channel_id=1, source_target_pairs={{0,1},{1,0},{2,3},{3,2},{4,5},{5,4},{6,7},{7,6},{8,9},{9,8},{10,11... | collective-permute-start | bytes 2359304 | tf_op jit(solution)/shard_map/ppermute | solution.py:43
  38.3 10.0 %copy-start.1 = (bf16[384,1024]{1,0:T(8,128)(2,1)}, bf16[384,1024]{1,0:T(8,128)(2,1)S(1)}, u32[]{:S(2)}) copy-start(bf16[384,1024]{1,0:T(8,128)(2,1)S(1)} %constant_dynamic-update-slice_fusion.10.refs_2_) | copy-start | bytes 2359300
  44.8 2.3 %collective-permute-start.20 = (bf16[384,1024]{1,0:T(8,128)(2,1)S(1)}, bf16[384,1024]{1,0:T(8,128)(2,1)S(1)}, u32[]{:S(2)}, u32[]{:S(2)}) collective-permute-start(bf16[384,1024]{1,0:T(8,128)(2,1)S(1)} %constant_dynamic-update-slice_fusion.10.refs_2_), channel_id=1, source_target_pairs={{0,1},{1,0},{2,3},{3,2},{4,5},{5,4},{6,7},{7,6},{8,9},{9,8},{10,11... | collective-permute-start | bytes 2359304 | tf_op jit(solution)/shard_map/ppermute | solution.py:43
  44.9 3.5 %copy-start.2 = (bf16[384,1024]{1,0:T(8,128)(2,1)}, bf16[384,1024]{1,0:T(8,128)(2,1)S(1)}, u32[]{:S(2)}) copy-start(bf16[384,1024]{1,0:T(8,128)(2,1)S(1)} %constant_dynamic-update-slice_fusion.15.refs_3_) | copy-start | bytes 2359300
  44.9 3.4 %collective-permute-start.21 = (bf16[384,1024]{1,0:T(8,128)(2,1)S(1)}, bf16[384,1024]{1,0:T(8,128)(2,1)}, u32[]{:S(2)}, u32[]{:S(2)}) collective-permute-start(bf16[384,1024]{1,0:T(8,128)(2,1)S(1)} %constant_dynamic-update-slice_fusion.15.refs_3_), channel_id=1, source_target_pairs={{0,1},{1,0},{2,3},{3,2},{4,5},{5,4},{6,7},{7,6},{8,9},{9,8},{10,11... | collective-permute-start | bytes 2359304 | tf_op jit(solution)/shard_map/ppermute | solution.py:43
  45.5 2.9 %copy-start.4 = (bf16[384,1024]{1,0:T(8,128)(2,1)}, bf16[384,1024]{1,0:T(8,128)(2,1)S(1)}, u32[]{:S(2)}) copy-start(bf16[384,1024]{1,0:T(8,128)(2,1)S(1)} %collective-permute-done.18.refs_4_) | copy-start | bytes 2359300
  45.5 1.6 %copy-start.5 = (bf16[384,1024]{1,0:T(8,128)(2,1)}, bf16[384,1024]{1,0:T(8,128)(2,1)S(1)}, u32[]{:S(2)}) copy-start(bf16[384,1024]{1,0:T(8,128)(2,1)S(1)} %collective-permute-done.19.refs_5_) | copy-start | bytes 2359300
  47.1 0.9 copy-start.6

commit v4 on v3

--- a/solution.py
+++ b/solution.py
@@ -18,7 +18,7 @@
 TILE = 256
 PACK = 16
 CHUNK = 512
-REST = 128
+REST = 256
 VMEM_BYTES = 60 << 20
 EXACT = lax.Precision.HIGHEST
 
@@ -36,6 +36,16 @@
 def two_parts(value):
     high = value.astype(jnp.bfloat16)
     return high, (value - high.astype(jnp.float32)).astype(jnp.bfloat16)
+
+
+def three_products(left, right):
+    left_high, left_low = two_parts(left)
+    right_high, right_low = two_parts(right)
+    return (
+        product(left_high, right_high, 1, 0)
+        + product(left_high, right_low, 1, 0)
+        + product(left_low, right_high, 1, 0)
+    )
 
 
 def flipped(value, mask):
@@ -68,15 +78,15 @@
 
 
 def over_chunks(rows, body):
-    whole = rows // CHUNK
+    whole = (rows + (CHUNK - REST - 1)) // CHUNK
 
     @pl.loop(0, whole)
     def _(index):
         body(pl.multiple_of(index * CHUNK, CHUNK), CHUNK)
 
-    @pl.loop(whole * (CHUNK // REST), pl.cdiv(rows, REST))
-    def _(index):
-        body(pl.multiple_of(index * REST, REST), REST)
+    @pl.when(whole * CHUNK < rows)
+    def _():
+        body(pl.multiple_of(whole * CHUNK, CHUNK), REST)
 
 
 def collect(groups, keys, counts, sizes, starts, arrived, copied):
@@ -253,10 +263,10 @@
                         )
                     block[...] = work[end : end + LANES, end : end + LANES]
                 if top > 0:
-                    found[top:end, 0:top] = product(pair, found[top:end, 0:top], 1, 0, EXACT)
+                    found[top:end, 0:top] = three_products(pair, found[top:end, 0:top])
                 if end < dim:
-                    found[end:dim, 0:end] = found[end:dim, 0:end] - product(
-                        panel, found[top:end, 0:end], 1, 0, EXACT
+                    found[end:dim, 0:end] = found[end:dim, 0:end] - three_products(
+                        panel, found[top:end, 0:end]
                     )
 
     high, low = two_parts(found[...])
@@ -338,15 +348,10 @@
         )
 
 
-def shards(states, bucket_sizes):
+def local_call(bucket_sizes, states, groups):
     row_count, dim = states.shape
     block_count = bucket_sizes.shape[0]
     block_rows = row_count // block_count
-    in_block = jnp.arange(LIVE_MAX, dtype=jnp.int32)
-    own_live = (in_block[None, :] < bucket_sizes[:, None])[:, :, None]
-    prefix = states.reshape(block_count, block_rows, dim)[:, :LIVE_MAX]
-    sent = jnp.where(own_live, prefix, jnp.bfloat16(DEAD)).reshape(-1, dim)
-    groups = gather_rows(sent)
     key_rows = sum(group.shape[0] for group in groups)
     blocks = key_rows // LIVE_MAX
     square = (dim, dim)
@@ -384,6 +389,18 @@
     return logs.reshape(row_count), means
 
 
+def shards(states, bucket_sizes):
+    row_count, dim = states.shape
+    block_count = bucket_sizes.shape[0]
+    block_rows = row_count // block_count
+    in_block = jnp.arange(LIVE_MAX, dtype=jnp.int32)
+    own_live = (in_block[None, :] < bucket_sizes[:, None])[:, :, None]
+    prefix = states.reshape(block_count, block_rows, dim)[:, :LIVE_MAX]
+    sent = jnp.where(own_live, prefix, jnp.bfloat16(DEAD)).reshape(-1, dim)
+    groups = gather_rows(sent)
+    return local_call(bucket_sizes, states, groups)
+
+
 def solution(mesh):
     placed = (P("dev", None), P("dev"))
     return jax.shard_map(

time: 136 us -> 127 us (0.934)
  Pallas kernels: 87.5 us -> 78.5 us
    pallas_call x1, Pallas kernels: 87.5 us -> 78.5 us  [local_call(): pl.pallas_call(functools.partial(local_kernel, len(groups)), out_shape=[j...]
where the time goes in v4:
time: 127 us
  Pallas kernels  78.5 us (62%)
  starting transfers between devices  23.6 us (19%)
  waiting for transfers between devices  21 us (17%)
  between operations  1.7 us (1%)
    pallas_call x1, Pallas kernels, local_call(): pl.pallas_call(functools.partial(local_kernel, len(groups)), out_shape=[j...  78.5 us
    ppermute x22, starting transfers between devices, flipped(): lax.ppermute(value, 'dev', [(source, source ^ mask) for source in range(s...  23.6 us
    ppermute x22, waiting for transfers between devices, flipped(): lax.ppermute(value, 'dev', [(source, source ^ mask) for source in range(s...  21 us
  transfers between devices with their start and end apart: 22, of which 8 were waited for; matrix products, arithmetic and copies ran while one was open for 0% of the time, Pallas kernels for 0%

profile of v4, /device:TPU:0, one launch (start us, length us, event | category | flops | bytes accessed | tf_op | source)
XLA Modules:
  0.0 127.0 jit_solution(18138997564504768318)
XLA Ops:
  1.3 1.0 constant_dynamic-update-slice_fusion.4
  2.3 3.0 %collective-permute-start.1 = (bf16[96,1024]{1,0:T(8,128)(2,1)S(1)}, bf16[96,1024]{1,0:T(8,128)(2,1)S(1)}, u32[]{:S(2)}, u32[]{:S(2)}) collective-permute-start(bf16[96,1024]{1,0:T(8,128)(2,1)S(1)} %get-tuple-element.7), channel_id=1, source_target_pairs={{0,4},{1,5},{2,6},{3,7},{4,0},{5,1},{6,2},{7,3},{8,12},{9,13},{10,... | collective-permute-start | bytes 589832 | tf_op jit(solution)/shard_map/ppermute | solution.py:53
  5.4 1.5 %collective-permute-start = (bf16[96,1024]{1,0:T(8,128)(2,1)S(1)}, bf16[96,1024]{1,0:T(8,128)(2,1)S(1)}, u32[]{:S(2)}, u32[]{:S(2)}) collective-permute-start(bf16[96,1024]{1,0:T(8,128)(2,1)S(1)} %get-tuple-element.7), channel_id=1, source_target_pairs={{0,2},{1,3},{2,0},{3,1},{4,6},{5,7},{6,4},{7,5},{8,10},{9,11},{10,... | collective-permute-start | bytes 589832 | tf_op jit(solution)/shard_map/ppermute | solution.py:53
  6.8 2.6 %collective-permute-start.4 = (bf16[96,1024]{1,0:T(8,128)(2,1)S(1)}, bf16[96,1024]{1,0:T(8,128)(2,1)S(1)}, u32[]{:S(2)}, u32[]{:S(2)}) collective-permute-start(bf16[96,1024]{1,0:T(8,128)(2,1)S(1)} %get-tuple-element.7), channel_id=1, source_target_pairs={{0,16},{1,17},{2,18},{3,19},{4,20},{5,21},{6,22},{7,23},{8,24},{9,... | collective-permute-start | bytes 589832 | tf_op jit(solution)/shard_map/ppermute | solution.py:53
  9.4 1.6 %collective-permute-start.9 = (bf16[96,1024]{1,0:T(8,128)(2,1)S(1)}, bf16[96,1024]{1,0:T(8,128)(2,1)S(1)}, u32[]{:S(2)}, u32[]{:S(2)}) collective-permute-start(bf16[96,1024]{1,0:T(8,128)(2,1)S(1)} %get-tuple-element.7), channel_id=1, source_target_pairs={{0,8},{1,9},{2,10},{3,11},{4,12},{5,13},{6,14},{7,15},{8,0},{9,1},... | collective-permute-start | bytes 589832 | tf_op jit(solution)/shard_map/ppermute | solution.py:53
  11.0 0.0 collective-permute-done.1
  11.0 1.0 collective-permute-start.3
  12.0 0.0 collective-permute-done
  12.1 1.6 %collective-permute-start.2 = (bf16[48,1024]{1,0:T(8,128)(2,1)S(1)}, bf16[48,1024]{1,0:T(8,128)(2,1)S(1)}, u32[]{:S(2)}, u32[]{:S(2)}) collective-permute-start(bf16[48,1024]{1,0:T(8,128)(2,1)S(1)} %slice.29), channel_id=1, source_target_pairs={{0,4},{1,5},{2,6},{3,7},{4,0},{5,1},{6,2},{7,3},{8,12},{9,13},{10,... | collective-permute-start | bytes 294920 | tf_op jit(solution)/shard_map/ppermute | solution.py:53
  13.6 4.5 %collective-permute-done.4 = bf16[96,1024]{1,0:T(8,128)(2,1)S(1)} collective-permute-done((bf16[96,1024]{1,0:T(8,128)(2,1)S(1)}, bf16[96,1024]{1,0:T(8,128)(2,1)S(1)}, u32[]{:S(2)}, u32[]{:S(2)}) %collective-permute-start.4) | collective-permute-done | bytes 196640 | tf_op jit(solution)/shard_map/ppermute | solution.py:53
  18.1 0.5 collective-permute-start.6
  18.7 0.5 collective-permute-start.5
  19.1 0.0 collective-permute-done.9
  19.1 1.6 %collective-permute-start.11 = (bf16[96,1024]{1,0:T(8,128)(2,1)S(1)}, bf16[96,1024]{1,0:T(8,128)(2,1)S(1)}, u32[]{:S(2)}, u32[]{:S(2)}) collective-permute-start(bf16[96,1024]{1,0:T(8,128)(2,1)S(1)} %collective-permute-done.9), channel_id=1, source_target_pairs={{0,4},{1,5},{2,6},{3,7},{4,0},{5,1},{6,2},{7,3},{8,12},{9,13},{10,... | collective-permute-start | bytes 589832 | tf_op jit(solution)/shard_map/ppermute | solution.py:53
  20.8 0.0 collective-permute-done.2
  20.8 1.6 %collective-permute-start.10 = (bf16[96,1024]{1,0:T(8,128)(2,1)S(1)}, bf16[96,1024]{1,0:T(8,128)(2,1)S(1)}, u32[]{:S(2)}, u32[]{:S(2)}) collective-permute-start(bf16[96,1024]{1,0:T(8,128)(2,1)S(1)} %collective-permute-done.9), channel_id=1, source_target_pairs={{0,2},{1,3},{2,0},{3,1},{4,6},{5,7},{6,4},{7,5},{8,10},{9,11},{10,... | collective-permute-start | bytes 589832 | tf_op jit(solution)/shard_map/ppermute | solution.py:53
  22.4 0.0 collective-permute-done.3
  22.4 0.7 collective-permute-start.14
  23.1 2.8 %collective-permute-done.6 = bf16[96,1024]{1,0:T(8,128)(2,1)S(1)} collective-permute-done((bf16[96,1024]{1,0:T(8,128)(2,1)S(1)}, bf16[96,1024]{1,0:T(8,128)(2,1)S(1)}, u32[]{:S(2)}, u32[]{:S(2)}) %collective-permute-start.6) | collective-permute-done | bytes 196640 | tf_op jit(solution)/shard_map/ppermute | solution.py:53
  25.9 0.0 collective-permute-start.18
  25.9 0.2 collective-permute-done.5
  26.1 0.5 collective-permute-start.8
  26.7 1.3 %collective-permute-done.11 = bf16[96,1024]{1,0:T(8,128)(2,1)S(1)} collective-permute-done((bf16[96,1024]{1,0:T(8,128)(2,1)S(1)}, bf16[96,1024]{1,0:T(8,128)(2,1)S(1)}, u32[]{:S(2)}, u32[]{:S(2)}) %collective-permute-start.11) | collective-permute-done | bytes 196640 | tf_op jit(solution)/shard_map/ppermute | solution.py:53
  28.0 0.5 collective-permute-start.7
  28.5 0.0 collective-permute-done.10
  28.5 1.3 %collective-permute-start.13 = (bf16[48,1024]{1,0:T(8,128)(2,1)S(1)}, bf16[48,1024]{1,0:T(8,128)(2,1)S(1)}, u32[]{:S(2)}, u32[]{:S(2)}) collective-permute-start(bf16[48,1024]{1,0:T(8,128)(2,1)S(1)} %slice.34), channel_id=1, source_target_pairs={{0,2},{1,3},{2,0},{3,1},{4,6},{5,7},{6,4},{7,5},{8,10},{9,11},{10,... | collective-permute-start | bytes 294920 | tf_op jit(solution)/shard_map/ppermute | solution.py:53
  29.9 0.0 collective-permute-done.14
  29.9 0.9 collective-permute-start.12
  30.8 3.7 %collective-permute-done.12 = bf16[48,1024]{1,0:T(8,128)(2,1)S(1)} collective-permute-done((bf16[48,1024]{1,0:T(8,128)(2,1)S(1)}, bf16[48,1024]{1,0:T(8,128)(2,1)S(1)}, u32[]{:S(2)}, u32[]{:S(2)}) %collective-permute-start.12) | collective-permute-done | bytes 98336 | tf_op jit(solution)/shard_map/ppermute | solution.py:53
  34.6 1.7 %collective-permute-start.17 = (bf16[96,1024]{1,0:T(8,128)(2,1)S(1)}, bf16[96,1024]{1,0:T(8,128)(2,1)S(1)}, u32[]{:S(2)}, u32[]{:S(2)}) collective-permute-start(bf16[96,1024]{1,0:T(8,128)(2,1)S(1)} %collective-permute-done.14), channel_id=1, source_target_pairs={{0,6},{1,7},{2,4},{3,5},{4,2},{5,3},{6,0},{7,1},{8,14},{9,15},{10,... | collective-permute-start | bytes 589832 | tf_op jit(solution)/shard_map/ppermute | solution.py:53
  36.3 0.0 collective-permute-done.7
  36.3 0.6 collective-permute-start.16
  36.9 0.0 collective-permute-done.8
  36.9 1.3 %collective-permute-start.15 = (bf16[96,1024]{1,0:T(8,128)(2,1)S(1)}, bf16[96,1024]{1,0:T(8,128)(2,1)S(1)}, u32[]{:S(2)}, u32[]{:S(2)}) collective-permute-start(bf16[96,1024]{1,0:T(8,128)(2,1)S(1)} %collective-permute-done.14), channel_id=1, source_target_pairs={{0,2},{1,3},{2,0},{3,1},{4,6},{5,7},{6,4},{7,5},{8,10},{9,11},{10,... | collective-permute-start | bytes 589832 | tf_op jit(solution)/shard_map/ppermute | solution.py:53
  38.2 0.0 collective-permute-done.13
  38.2 0.1 collective-permute-start.19
  38.4 6.4 %collective-permute-done.15 = bf16[96,1024]{1,0:T(8,128)(2,1)S(1)} collective-permute-done((bf16[96,1024]{1,0:T(8,128)(2,1)S(1)}, bf16[96,1024]{1,0:T(8,128)(2,1)S(1)}, u32[]{:S(2)}, u32[]{:S(2)}) %collective-permute-start.15) | collective-permute-done | bytes 196640 | tf_op jit(solution)/shard_map/ppermute | solution.py:53
  44.8 0.0 collective-permute-start.20
  44.8 0.0 collective-permute-done.16
  44.8 0.0 collective-permute-done.17
  44.9 0.6 collective-permute-start.21
  45.5 0.0 collective-permute-done.18.refs_4_
  45.5 0.0 collective-permute-done.19.refs_5_
  45.5 1.6 %collective-permute-done.20.refs_6_ = bf16[384,1024]{1,0:T(8,128)(2,1)S(1)} collective-permute-done((bf16[384,1024]{1,0:T(8,128)(2,1)S(1)}, bf16[384,1024]{1,0:T(8,128)(2,1)S(1)}, u32[]{:S(2)}, u32[]{:S(2)}) %collective-permute-start.20) | collective-permute-done | bytes 786464 | tf_op jit(solution)/shard_map/ppermute | solution.py:53
  47.1 0.9 copy-done.6
  48.0 0.3 collective-permute-done.21.refs_7_
  48.3 0.0 copy-done
  48.4 78.5 %shard_map.41 = (f32[1,128]{1,0:T(1,128)}, bf16[128,1024]{1,0:T(8,128)(2,1)}) custom-call(s32[1]{0:T(128)} %copy.19.size_ref, bf16[128,1024]{1,0:T(8,128)(2,1)} %own_ref.1, bf16[384,1024]{1,0:T(8,128)(2,1)} %copy-done.3, bf16[384,1024]{1,0:T(8,128)(2,1)} %copy-done, bf16[384,1024]{1,0:T(8,128)(2,1)} %copy-done.1, bf16[384,1024]{1,0:T(8,128)(2,1)} %copy-done.2, ...), custom_call_target="tpu_custom_call" | custom-call | tf_op jit(solution)/shard_map/pallas_call | solution.py:358
  (37 shorter events, 0.3 us)
Async XLA Ops:
  2.3 8.7 %collective-permute-start.1 = (bf16[96,1024]{1,0:T(8,128)(2,1)S(1)}, bf16[96,1024]{1,0:T(8,128)(2,1)S(1)}, u32[]{:S(2)}, u32[]{:S(2)}) collective-permute-start(bf16[96,1024]{1,0:T(8,128)(2,1)S(1)} %get-tuple-element.7), channel_id=1, source_target_pairs={{0,4},{1,5},{2,6},{3,7},{4,0},{5,1},{6,2},{7,3},{8,12},{9,13},{10,... | collective-permute-start | bytes 589832 | tf_op jit(solution)/shard_map/ppermute | solution.py:53
  5.4 6.7 %collective-permute-start = (bf16[96,1024]{1,0:T(8,128)(2,1)S(1)}, bf16[96,1024]{1,0:T(8,128)(2,1)S(1)}, u32[]{:S(2)}, u32[]{:S(2)}) collective-permute-start(bf16[96,1024]{1,0:T(8,128)(2,1)S(1)} %get-tuple-element.7), channel_id=1, source_target_pairs={{0,2},{1,3},{2,0},{3,1},{4,6},{5,7},{6,4},{7,5},{8,10},{9,11},{10,... | collective-permute-start | bytes 589832 | tf_op jit(solution)/shard_map/ppermute | solution.py:53
  6.8 11.3 %collective-permute-start.4 = (bf16[96,1024]{1,0:T(8,128)(2,1)S(1)}, bf16[96,1024]{1,0:T(8,128)(2,1)S(1)}, u32[]{:S(2)}, u32[]{:S(2)}) collective-permute-start(bf16[96,1024]{1,0:T(8,128)(2,1)S(1)} %get-tuple-element.7), channel_id=1, source_target_pairs={{0,16},{1,17},{2,18},{3,19},{4,20},{5,21},{6,22},{7,23},{8,24},{9,... | collective-permute-start | bytes 589832 | tf_op jit(solution)/shard_map/ppermute | solution.py:53
  9.4 9.7 %collective-permute-start.9 = (bf16[96,1024]{1,0:T(8,128)(2,1)S(1)}, bf16[96,1024]{1,0:T(8,128)(2,1)S(1)}, u32[]{:S(2)}, u32[]{:S(2)}) collective-permute-start(bf16[96,1024]{1,0:T(8,128)(2,1)S(1)} %get-tuple-element.7), channel_id=1, source_target_pairs={{0,8},{1,9},{2,10},{3,11},{4,12},{5,13},{6,14},{7,15},{8,0},{9,1},... | collective-permute-start | bytes 589832 | tf_op jit(solution)/shard_map/ppermute | solution.py:53
  11.0 11.3 %collective-permute-start.3 = (bf16[48,1024]{1,0:T(8,128)(2,1)S(1)}, bf16[48,1024]{1,0:T(8,128)(2,1)S(1)}, u32[]{:S(2)}, u32[]{:S(2)}) collective-permute-start(bf16[48,1024]{1,0:T(8,128)(2,1)S(1)} %slice.30), channel_id=1, source_target_pairs={{0,2},{1,3},{2,0},{3,1},{4,6},{5,7},{6,4},{7,5},{8,10},{9,11},{10,... | collective-permute-start | bytes 294920 | tf_op jit(solution)/shard_map/ppermute | solution.py:53
  12.1 8.7 %collective-permute-start.2 = (bf16[48,1024]{1,0:T(8,128)(2,1)S(1)}, bf16[48,1024]{1,0:T(8,128)(2,1)S(1)}, u32[]{:S(2)}, u32[]{:S(2)}) collective-permute-start(bf16[48,1024]{1,0:T(8,128)(2,1)S(1)} %slice.29), channel_id=1, source_target_pairs={{0,4},{1,5},{2,6},{3,7},{4,0},{5,1},{6,2},{7,3},{8,12},{9,13},{10,... | collective-permute-start | bytes 294920 | tf_op jit(solution)/shard_map/ppermute | solution.py:53
  18.1 7.7 %collective-permute-start.6 = (bf16[96,1024]{1,0:T(8,128)(2,1)S(1)}, bf16[96,1024]{1,0:T(8,128)(2,1)S(1)}, u32[]{:S(2)}, u32[]{:S(2)}) collective-permute-start(bf16[96,1024]{1,0:T(8,128)(2,1)S(1)} %collective-permute-done.4), channel_id=1, source_target_pairs={{0,4},{1,5},{2,6},{3,7},{4,0},{5,1},{6,2},{7,3},{8,12},{9,13},{10,... | collective-permute-start | bytes 589832 | tf_op jit(solution)/shard_map/ppermute | solution.py:53
  18.7 7.5 %collective-permute-start.5 = (bf16[96,1024]{1,0:T(8,128)(2,1)S(1)}, bf16[96,1024]{1,0:T(8,128)(2,1)S(1)}, u32[]{:S(2)}, u32[]{:S(2)}) collective-permute-start(bf16[96,1024]{1,0:T(8,128)(2,1)S(1)} %collective-permute-done.4), channel_id=1, source_target_pairs={{0,2},{1,3},{2,0},{3,1},{4,6},{5,7},{6,4},{7,5},{8,10},{9,11},{10,... | collective-permute-start | bytes 589832 | tf_op jit(solution)/shard_map/ppermute | solution.py:53
  19.1 8.9 %collective-permute-start.11 = (bf16[96,1024]{1,0:T(8,128)(2,1)S(1)}, bf16[96,1024]{1,0:T(8,128)(2,1)S(1)}, u32[]{:S(2)}, u32[]{:S(2)}) collective-permute-start(bf16[96,1024]{1,0:T(8,128)(2,1)S(1)} %collective-permute-done.9), channel_id=1, source_target_pairs={{0,4},{1,5},{2,6},{3,7},{4,0},{5,1},{6,2},{7,3},{8,12},{9,13},{10,... | collective-permute-start | bytes 589832 | tf_op jit(solution)/shard_map/ppermute | solution.py:53
  20.8 7.7 %collective-permute-start.10 = (bf16[96,1024]{1,0:T(8,128)(2,1)S(1)}, bf16[96,1024]{1,0:T(8,128)(2,1)S(1)}, u32[]{:S(2)}, u32[]{:S(2)}) collective-permute-start(bf16[96,1024]{1,0:T(8,128)(2,1)S(1)} %collective-permute-done.9), channel_id=1, source_target_pairs={{0,2},{1,3},{2,0},{3,1},{4,6},{5,7},{6,4},{7,5},{8,10},{9,11},{10,... | collective-permute-start | bytes 589832 | tf_op jit(solution)/shard_map/ppermute | solution.py:53
  22.4 7.5 %collective-permute-start.14 = (bf16[96,1024]{1,0:T(8,128)(2,1)S(1)}, bf16[96,1024]{1,0:T(8,128)(2,1)S(1)}, u32[]{:S(2)}, u32[]{:S(2)}) collective-permute-start(bf16[96,1024]{1,0:T(8,128)(2,1)S(1)} %collective-permute-done.4), channel_id=1, source_target_pairs={{0,8},{1,9},{2,10},{3,11},{4,12},{5,13},{6,14},{7,15},{8,0},{9,1},... | collective-permute-start | bytes 589832 | tf_op jit(solution)/shard_map/ppermute | solution.py:53
  23.0 6.8 %copy-start.3 = (bf16[384,1024]{1,0:T(8,128)(2,1)}, bf16[384,1024]{1,0:T(8,128)(2,1)S(1)}, u32[]{:S(2)}) copy-start(bf16[384,1024]{1,0:T(8,128)(2,1)S(1)} %constant_dynamic-update-slice_fusion.refs_0_) | copy-start | bytes 2359300
  25.9 19.6 %collective-permute-start.18 = (bf16[384,1024]{1,0:T(8,128)(2,1)S(1)}, bf16[384,1024]{1,0:T(8,128)(2,1)S(1)}, u32[]{:S(2)}, u32[]{:S(2)}) collective-permute-start(bf16[384,1024]{1,0:T(8,128)(2,1)S(1)} %constant_dynamic-update-slice_fusion.refs_0_), channel_id=1, source_target_pairs={{0,1},{1,0},{2,3},{3,2},{4,5},{5,4},{6,7},{7,6},{8,9},{9,8},{10,11... | collective-permute-start | bytes 2359304 | tf_op jit(solution)/shard_map/ppermute | solution.py:53
  26.1 10.8 %collective-permute-start.8 = (bf16[48,1024]{1,0:T(8,128)(2,1)S(1)}, bf16[48,1024]{1,0:T(8,128)(2,1)S(1)}, u32[]{:S(2)}, u32[]{:S(2)}) collective-permute-start(bf16[48,1024]{1,0:T(8,128)(2,1)S(1)} %slice.32), channel_id=1, source_target_pairs={{0,2},{1,3},{2,0},{3,1},{4,6},{5,7},{6,4},{7,5},{8,10},{9,11},{10,... | collective-permute-start | bytes 294920 | tf_op jit(solution)/shard_map/ppermute | solution.py:53
  28.0 8.3 %collective-permute-start.7 = (bf16[48,1024]{1,0:T(8,128)(2,1)S(1)}, bf16[48,1024]{1,0:T(8,128)(2,1)S(1)}, u32[]{:S(2)}, u32[]{:S(2)}) collective-permute-start(bf16[48,1024]{1,0:T(8,128)(2,1)S(1)} %slice.31), channel_id=1, source_target_pairs={{0,4},{1,5},{2,6},{3,7},{4,0},{5,1},{6,2},{7,3},{8,12},{9,13},{10,... | collective-permute-start | bytes 294920 | tf_op jit(solution)/shard_map/ppermute | solution.py:53
  28.5 9.7 %collective-permute-start.13 = (bf16[48,1024]{1,0:T(8,128)(2,1)S(1)}, bf16[48,1024]{1,0:T(8,128)(2,1)S(1)}, u32[]{:S(2)}, u32[]{:S(2)}) collective-permute-start(bf16[48,1024]{1,0:T(8,128)(2,1)S(1)} %slice.34), channel_id=1, source_target_pairs={{0,2},{1,3},{2,0},{3,1},{4,6},{5,7},{6,4},{7,5},{8,10},{9,11},{10,... | collective-permute-start | bytes 294920 | tf_op jit(solution)/shard_map/ppermute | solution.py:53
  29.9 4.7 %collective-permute-start.12 = (bf16[48,1024]{1,0:T(8,128)(2,1)S(1)}, bf16[48,1024]{1,0:T(8,128)(2,1)S(1)}, u32[]{:S(2)}, u32[]{:S(2)}) collective-permute-start(bf16[48,1024]{1,0:T(8,128)(2,1)S(1)} %slice.33), channel_id=1, source_target_pairs={{0,4},{1,5},{2,6},{3,7},{4,0},{5,1},{6,2},{7,3},{8,12},{9,13},{10,... | collective-permute-start | bytes 294920 | tf_op jit(solution)/shard_map/ppermute | solution.py:53
  34.6 10.3 %collective-permute-start.17 = (bf16[96,1024]{1,0:T(8,128)(2,1)S(1)}, bf16[96,1024]{1,0:T(8,128)(2,1)S(1)}, u32[]{:S(2)}, u32[]{:S(2)}) collective-permute-start(bf16[96,1024]{1,0:T(8,128)(2,1)S(1)} %collective-permute-done.14), channel_id=1, source_target_pairs={{0,6},{1,7},{2,4},{3,5},{4,2},{5,3},{6,0},{7,1},{8,14},{9,15},{10,... | collective-permute-start | bytes 589832 | tf_op jit(solution)/shard_map/ppermute | solution.py:53
  36.3 8.5 %collective-permute-start.16 = (bf16[96,1024]{1,0:T(8,128)(2,1)S(1)}, bf16[96,1024]{1,0:T(8,128)(2,1)S(1)}, u32[]{:S(2)}, u32[]{:S(2)}) collective-permute-start(bf16[96,1024]{1,0:T(8,128)(2,1)S(1)} %collective-permute-done.14), channel_id=1, source_target_pairs={{0,4},{1,5},{2,6},{3,7},{4,0},{5,1},{6,2},{7,3},{8,12},{9,13},{10,... | collective-permute-start | bytes 589832 | tf_op jit(solution)/shard_map/ppermute | solution.py:53
  36.9 7.9 %collective-permute-start.15 = (bf16[96,1024]{1,0:T(8,128)(2,1)S(1)}, bf16[96,1024]{1,0:T(8,128)(2,1)S(1)}, u32[]{:S(2)}, u32[]{:S(2)}) collective-permute-start(bf16[96,1024]{1,0:T(8,128)(2,1)S(1)} %collective-permute-done.14), channel_id=1, source_target_pairs={{0,2},{1,3},{2,0},{3,1},{4,6},{5,7},{6,4},{7,5},{8,10},{9,11},{10,... | collective-permute-start | bytes 589832 | tf_op jit(solution)/shard_map/ppermute | solution.py:53
  38.2 10.1 %copy-start = (bf16[384,1024]{1,0:T(8,128)(2,1)}, bf16[384,1024]{1,0:T(8,128)(2,1)S(1)}, u32[]{:S(2)}) copy-start(bf16[384,1024]{1,0:T(8,128)(2,1)S(1)} %constant_dynamic-update-slice_fusion.5.refs_1_) | copy-start | bytes 2359300
  38.2 7.2 %collective-permute-start.19 = (bf16[384,1024]{1,0:T(8,128)(2,1)S(1)}, bf16[384,1024]{1,0:T(8,128)(2,1)S(1)}, u32[]{:S(2)}, u32[]{:S(2)}) collective-permute-start(bf16[384,1024]{1,0:T(8,128)(2,1)S(1)} %constant_dynamic-update-slice_fusion.5.refs_1_), channel_id=1, source_target_pairs={{0,1},{1,0},{2,3},{3,2},{4,5},{5,4},{6,7},{7,6},{8,9},{9,8},{10,11... | collective-permute-start | bytes 2359304 | tf_op jit(solution)/shard_map/ppermute | solution.py:53
  38.3 10.0 %copy-start.1 = (bf16[384,1024]{1,0:T(8,128)(2,1)}, bf16[384,1024]{1,0:T(8,128)(2,1)S(1)}, u32[]{:S(2)}) copy-start(bf16[384,1024]{1,0:T(8,128)(2,1)S(1)} %constant_dynamic-update-slice_fusion.10.refs_2_) | copy-start | bytes 2359300
  44.8 2.3 %collective-permute-start.20 = (bf16[384,1024]{1,0:T(8,128)(2,1)S(1)}, bf16[384,1024]{1,0:T(8,128)(2,1)S(1)}, u32[]{:S(2)}, u32[]{:S(2)}) collective-permute-start(bf16[384,1024]{1,0:T(8,128)(2,1)S(1)} %constant_dynamic-update-slice_fusion.10.refs_2_), channel_id=1, source_target_pairs={{0,1},{1,0},{2,3},{3,2},{4,5},{5,4},{6,7},{7,6},{8,9},{9,8},{10,11... | collective-permute-start | bytes 2359304 | tf_op jit(solution)/shard_map/ppermute | solution.py:53
  44.9 3.5 %copy-start.2 = (bf16[384,1024]{1,0:T(8,128)(2,1)}, bf16[384,1024]{1,0:T(8,128)(2,1)S(1)}, u32[]{:S(2)}) copy-start(bf16[384,1024]{1,0:T(8,128)(2,1)S(1)} %constant_dynamic-update-slice_fusion.15.refs_3_) | copy-start | bytes 2359300
  44.9 3.4 %collective-permute-start.21 = (bf16[384,1024]{1,0:T(8,128)(2,1)S(1)}, bf16[384,1024]{1,0:T(8,128)(2,1)}, u32[]{:S(2)}, u32[]{:S(2)}) collective-permute-start(bf16[384,1024]{1,0:T(8,128)(2,1)S(1)} %constant_dynamic-update-slice_fusion.15.refs_3_), channel_id=1, source_target_pairs={{0,1},{1,0},{2,3},{3,2},{4,5},{5,4},{6,7},{7,6},{8,9},{9,8},{10,11... | collective-permute-start | bytes 2359304 | tf_op jit(solution)/shard_map/ppermute | solution.py:53
  45.5 2.9 %copy-start.4 = (bf16[384,1024]{1,0:T(8,128)(2,1)}, bf16[384,1024]{1,0:T(8,128)(2,1)S(1)}, u32[]{:S(2)}) copy-start(bf16[384,1024]{1,0:T(8,128)(2,1)S(1)} %collective-permute-done.18.refs_4_) | copy-start | bytes 2359300
  45.5 1.6 %copy-start.5 = (bf16[384,1024]{1,0:T(8,128)(2,1)}, bf16[384,1024]{1,0:T(8,128)(2,1)S(1)}, u32[]{:S(2)}) copy-start(bf16[384,1024]{1,0:T(8,128)(2,1)S(1)} %collective-permute-done.19.refs_5_) | copy-start | bytes 2359300
  47.1 0.9 copy-start.6

commit v5 on v4

--- a/solution.py
+++ b/solution.py
@@ -14,6 +14,7 @@
 DEAD = 1024.0
 DEAD_ABOVE = 512.0
 SUB = 8
+HALF = 8
 LANES = 128
 TILE = 256
 PACK = 16
@@ -67,7 +68,7 @@
     across, beside = flipped(rows, far), flipped(rows, near)
     groups = [rows, across, beside, flipped(across, near)]
     same_core = [
-        jnp.concatenate(plane_of(group, near, place == 3), axis=0)
+        jnp.concatenate(plane_of(group, near, place in (0, 3)), axis=0)
         for place, group in enumerate(groups)
     ]
     return same_core + [flipped(group, 1) for group in same_core]
@@ -189,36 +190,56 @@
     def over_sublanes(value, row):
         return jnp.broadcast_to(value[row : row + 1, :], (SUB, LANES))
 
-    for step in range(count):
-        first = SUB * step
-        pivot_rows, inverse_rows = rows[step], inverse[step]
-        columns = [over_lanes(pivot_rows, first + t) for t in range(SUB)]
-        below = {
-            i: [over_lanes(rows[i], first + t) for t in range(SUB)]
-            for i in range(step + 1, count)
-        }
-        scale, entry, upper, solved = [], {}, [], []
-        for t in range(SUB):
-            root = lax.rsqrt(over_sublanes(columns[t], t))
-            scale.append(root)
-            down = jnp.where(sublane > t, columns[t] * root, 0.0)
-            upper.append(over_sublanes(pivot_rows, t) * root)
-            solved.append(over_sublanes(inverse_rows, t) * root)
-            for q in range(t + 1, SUB):
-                entry[q, t] = over_sublanes(columns[q], t) * root
-                columns[q] = columns[q] - down * entry[q, t]
-            pivot_rows = pivot_rows - down * upper[t]
-            inverse_rows = jnp.where(sublane == t, solved[t], inverse_rows - down * solved[t])
-        inverse[step] = inverse_rows
-        for i in range(step + 1, count):
-            column, row, other = below[i], rows[i], inverse[i]
-            for t in range(SUB):
-                factor = column[t] * scale[t]
-                for q in range(t + 1, SUB):
-                    column[q] = column[q] - factor * entry[q, t]
-                row = row - factor * upper[t]
-                other = other - factor * solved[t]
-            rows[i], inverse[i] = row, other
+    upper = list(rows)
+    for half in range(0, count, HALF):
+        for step in range(half, half + HALF, 2):
+            first = SUB * step
+            pair = range(step, step + 2)
+            columns = [[over_lanes(rows[v], first + t) for v in pair] for t in range(2 * SUB)]
+            left, right = [rows[v] for v in pair], [inverse[v] for v in pair]
+            done, solved = list(left), list(right)
+            for t in range(2 * SUB):
+                v, s = divmod(t, SUB)
+                here = sublane == s
+                pivot = over_sublanes(columns[t][v], s)
+                root = lax.rsqrt(pivot)
+                reciprocal = root * root
+                factor = list(columns[t])
+                factor[v] = jnp.where(here, -1.0, factor[v])
+
+                def eliminate(values, raw):
+                    scaled = raw * reciprocal
+                    kept = list(values)
+                    kept[v] = jnp.where(here, 0.0, kept[v])
+                    return [k - f * scaled for k, f in zip(kept, factor)]
+
+                for q in range(t + 1, 2 * SUB):
+                    columns[q] = eliminate(columns[q], over_sublanes(columns[q][v], s))
+                raw = over_sublanes(left[v], s)
+                done[v] = jnp.where(here, raw * root, done[v])
+                left = eliminate(left, raw)
+                raw = over_sublanes(right[v], s)
+                solved[v] = jnp.where(here, raw * root, solved[v])
+                right = eliminate(right, raw)
+            for v in range(2):
+                upper[step + v], inverse[step + v] = done[v], solved[v]
+            left = [over_sublanes(left[t // SUB], t % SUB) for t in range(2 * SUB)]
+            right = [over_sublanes(right[t // SUB], t % SUB) for t in range(2 * SUB)]
+            for i in range(step + 2, half + HALF):
+                row, beside = rows[i], inverse[i]
+                for t in range(2 * SUB):
+                    column = over_lanes(rows[i], first + t)
+                    row = row - column * left[t]
+                    beside = beside - column * right[t]
+                rows[i], inverse[i] = row, beside
+        if half + HALF < count:
+            span = slice(half, half + HALF)
+            down = jnp.concatenate(upper[span], axis=0)
+            across = jnp.concatenate([down, jnp.concatenate(inverse[span], axis=0)], axis=1)
+            change = product(down, across, 0, 0, EXACT)
+            for i in range(half + HALF, count):
+                rows[i] = rows[i] - change[SUB * i : SUB * i + SUB, :LANES]
+                inverse[i] = inverse[i] - change[SUB * i : SUB * i + SUB, LANES:]
     return inverse
 
 

time: 127 us -> 124 us (0.976)
  Pallas kernels: 78.5 us -> 74.7 us
  starting transfers between devices: 23.6 us -> 25.7 us
  waiting for transfers between devices: 21 us -> 19.3 us
    pallas_call x1, Pallas kernels: 78.5 us -> 74.7 us  [local_call(): pl.pallas_call(functools.partial(local_kernel, len(groups)), out_shape=[j...]
    ppermute x22 -> x21, starting transfers between devices: 23.6 us -> 25.7 us  [flipped(): lax.ppermute(value, 'dev', [(source, source ^ mask) for source in range(s...]
    ppermute x22 -> x21, waiting for transfers between devices: 21 us -> 19.3 us  [flipped(): lax.ppermute(value, 'dev', [(source, source ^ mask) for source in range(s...]
  transfers between devices with their start and end apart: 22 -> 21, of which waited for: 8 -> 12; matrix products, arithmetic and copies ran while one was open for 0% -> 0% of each run, Pallas kernels for 0% -> 0%
where the time goes in v5:
time: 124 us
  Pallas kernels  74.7 us (60%)
  starting transfers between devices  25.7 us (21%)
  waiting for transfers between devices  19.3 us (16%)
  between operations  1.67 us (1%)
    pallas_call x1, Pallas kernels, local_call(): pl.pallas_call(functools.partial(local_kernel, len(groups)), out_shape=[j...  74.7 us
    ppermute x21, starting transfers between devices, flipped(): lax.ppermute(value, 'dev', [(source, source ^ mask) for source in range(s...  25.7 us
    ppermute x21, waiting for transfers between devices, flipped(): lax.ppermute(value, 'dev', [(source, source ^ mask) for source in range(s...  19.3 us
  transfers between devices with their start and end apart: 21, of which 12 were waited for; matrix products, arithmetic and copies ran while one was open for 0% of the time, Pallas kernels for 0%

profile of v5, /device:TPU:0, one launch (start us, length us, event | category | flops | bytes accessed | tf_op | source)
XLA Modules:
  0.0 123.6 jit_solution(12458171194171560472)
XLA Ops:
  1.3 1.0 fusion
  2.3 3.1 %collective-permute-start.8 = (bf16[96,1024]{1,0:T(8,128)(2,1)S(1)}, bf16[96,1024]{1,0:T(8,128)(2,1)S(1)}, u32[]{:S(2)}, u32[]{:S(2)}) collective-permute-start(bf16[96,1024]{1,0:T(8,128)(2,1)S(1)} %fusion), channel_id=1, source_target_pairs={{0,8},{1,9},{2,10},{3,11},{4,12},{5,13},{6,14},{7,15},{8,0},{9,1},... | collective-permute-start | bytes 589832 | tf_op jit(solution)/shard_map/ppermute | solution.py:54
  5.4 2.6 %collective-permute-start.3 = (bf16[96,1024]{1,0:T(8,128)(2,1)S(1)}, bf16[96,1024]{1,0:T(8,128)(2,1)S(1)}, u32[]{:S(2)}, u32[]{:S(2)}) collective-permute-start(bf16[96,1024]{1,0:T(8,128)(2,1)S(1)} %fusion), channel_id=1, source_target_pairs={{0,16},{1,17},{2,18},{3,19},{4,20},{5,21},{6,22},{7,23},{8,24},{9,... | collective-permute-start | bytes 589832 | tf_op jit(solution)/shard_map/ppermute | solution.py:54
  8.0 2.4 %collective-permute-start.2 = (bf16[96,1024]{1,0:T(8,128)(2,1)S(1)}, bf16[96,1024]{1,0:T(8,128)(2,1)S(1)}, u32[]{:S(2)}, u32[]{:S(2)}) collective-permute-start(bf16[96,1024]{1,0:T(8,128)(2,1)S(1)} %fusion), channel_id=1, source_target_pairs={{0,6},{1,7},{2,4},{3,5},{4,2},{5,3},{6,0},{7,1},{8,14},{9,15},{10,... | collective-permute-start | bytes 589832 | tf_op jit(solution)/shard_map/ppermute | solution.py:54
  10.4 0.5 collective-permute-start.1
  10.9 0.5 collective-permute-start
  11.5 2.9 %collective-permute-done.8 = bf16[96,1024]{1,0:T(8,128)(2,1)S(1)} collective-permute-done((bf16[96,1024]{1,0:T(8,128)(2,1)S(1)}, bf16[96,1024]{1,0:T(8,128)(2,1)S(1)}, u32[]{:S(2)}, u32[]{:S(2)}) %collective-permute-start.8) | collective-permute-done | bytes 196640 | tf_op jit(solution)/shard_map/ppermute | solution.py:54
  14.4 1.7 %collective-permute-start.10 = (bf16[96,1024]{1,0:T(8,128)(2,1)S(1)}, bf16[96,1024]{1,0:T(8,128)(2,1)S(1)}, u32[]{:S(2)}, u32[]{:S(2)}) collective-permute-start(bf16[96,1024]{1,0:T(8,128)(2,1)S(1)} %collective-permute-done.8), channel_id=1, source_target_pairs={{0,4},{1,5},{2,6},{3,7},{4,0},{5,1},{6,2},{7,3},{8,12},{9,13},{10,... | collective-permute-start | bytes 589832 | tf_op jit(solution)/shard_map/ppermute | solution.py:54
  16.1 0.8 collective-permute-done.3
  16.9 1.5 %collective-permute-start.9 = (bf16[96,1024]{1,0:T(8,128)(2,1)S(1)}, bf16[96,1024]{1,0:T(8,128)(2,1)S(1)}, u32[]{:S(2)}, u32[]{:S(2)}) collective-permute-start(bf16[96,1024]{1,0:T(8,128)(2,1)S(1)} %collective-permute-done.8), channel_id=1, source_target_pairs={{0,2},{1,3},{2,0},{3,1},{4,6},{5,7},{6,4},{7,5},{8,10},{9,11},{10,... | collective-permute-start | bytes 589832 | tf_op jit(solution)/shard_map/ppermute | solution.py:54
  18.4 0.0 collective-permute-done.2
  18.4 0.5 collective-permute-start.13
  19.0 0.7 collective-permute-done.1
  19.6 1.2 collective-permute-start.5
  20.8 0.2 collective-permute-done
  21.0 1.4 %collective-permute-start.4 = (bf16[96,1024]{1,0:T(8,128)(2,1)S(1)}, bf16[96,1024]{1,0:T(8,128)(2,1)S(1)}, u32[]{:S(2)}, u32[]{:S(2)}) collective-permute-start(bf16[96,1024]{1,0:T(8,128)(2,1)S(1)} %collective-permute-done.3), channel_id=1, source_target_pairs={{0,2},{1,3},{2,0},{3,1},{4,6},{5,7},{6,4},{7,5},{8,10},{9,11},{10,... | collective-permute-start | bytes 589832 | tf_op jit(solution)/shard_map/ppermute | solution.py:54
  22.5 0.1 pad_maximum_fusion.refs_0_
  22.6 1.3 %collective-permute-done.10 = bf16[96,1024]{1,0:T(8,128)(2,1)S(1)} collective-permute-done((bf16[96,1024]{1,0:T(8,128)(2,1)S(1)}, bf16[96,1024]{1,0:T(8,128)(2,1)S(1)}, u32[]{:S(2)}, u32[]{:S(2)}) %collective-permute-start.10) | collective-permute-done | bytes 196640 | tf_op jit(solution)/shard_map/ppermute | solution.py:54
  23.9 0.0 collective-permute-start.17
  23.9 0.2 collective-permute-done.9
  24.1 2.5 %collective-permute-start.12 = (bf16[48,1024]{1,0:T(8,128)(2,1)S(1)}, bf16[48,1024]{1,0:T(8,128)(2,1)S(1)}, u32[]{:S(2)}, u32[]{:S(2)}) collective-permute-start(bf16[48,1024]{1,0:T(8,128)(2,1)S(1)} %slice.24), channel_id=1, source_target_pairs={{0,2},{1,3},{2,0},{3,1},{4,6},{5,7},{6,4},{7,5},{8,10},{9,11},{10,... | collective-permute-start | bytes 294920 | tf_op jit(solution)/shard_map/ppermute | solution.py:54
  26.6 1.0 collective-permute-done.5
  27.6 1.5 %collective-permute-start.11 = (bf16[48,1024]{1,0:T(8,128)(2,1)S(1)}, bf16[48,1024]{1,0:T(8,128)(2,1)S(1)}, u32[]{:S(2)}, u32[]{:S(2)}) collective-permute-start(bf16[48,1024]{1,0:T(8,128)(2,1)S(1)} %slice.23), channel_id=1, source_target_pairs={{0,4},{1,5},{2,6},{3,7},{4,0},{5,1},{6,2},{7,3},{8,12},{9,13},{10,... | collective-permute-start | bytes 294920 | tf_op jit(solution)/shard_map/ppermute | solution.py:54
  29.1 0.0 collective-permute-done.4
  29.1 1.0 collective-permute-start.7
  30.2 0.0 collective-permute-done.13
  30.2 1.1 collective-permute-start.6
  31.4 3.5 %collective-permute-done.6 = bf16[48,1024]{1,0:T(8,128)(2,1)S(1)} collective-permute-done((bf16[48,1024]{1,0:T(8,128)(2,1)S(1)}, bf16[48,1024]{1,0:T(8,128)(2,1)S(1)}, u32[]{:S(2)}, u32[]{:S(2)}) %collective-permute-start.6) | collective-permute-done | bytes 98336 | tf_op jit(solution)/shard_map/ppermute | solution.py:54
  34.9 1.2 collective-permute-start.16
  36.1 0.0 collective-permute-done.11
  36.1 1.4 %collective-permute-start.15 = (bf16[96,1024]{1,0:T(8,128)(2,1)S(1)}, bf16[96,1024]{1,0:T(8,128)(2,1)S(1)}, u32[]{:S(2)}, u32[]{:S(2)}) collective-permute-start(bf16[96,1024]{1,0:T(8,128)(2,1)S(1)} %collective-permute-done.13), channel_id=1, source_target_pairs={{0,4},{1,5},{2,6},{3,7},{4,0},{5,1},{6,2},{7,3},{8,12},{9,13},{10,... | collective-permute-start | bytes 589832 | tf_op jit(solution)/shard_map/ppermute | solution.py:54
  37.5 0.0 collective-permute-done.12
  37.5 1.0 collective-permute-start.14
  38.5 0.0 collective-permute-done.7
  38.5 0.1 collective-permute-start.19
  38.6 6.5 %collective-permute-done.14 = bf16[96,1024]{1,0:T(8,128)(2,1)S(1)} collective-permute-done((bf16[96,1024]{1,0:T(8,128)(2,1)S(1)}, bf16[96,1024]{1,0:T(8,128)(2,1)S(1)}, u32[]{:S(2)}, u32[]{:S(2)}) %collective-permute-start.14) | collective-permute-done | bytes 196640 | tf_op jit(solution)/shard_map/ppermute | solution.py:54
  45.2 0.0 collective-permute-start.18
  45.2 0.1 collective-permute-done.15
  45.3 0.0 collective-permute-done.16
  45.4 0.5 collective-permute-start.20
  45.9 0.0 collective-permute-done.17.refs_4_
  45.9 0.0 collective-permute-done.19.refs_6_
  45.9 1.6 %collective-permute-done.18.refs_5_ = bf16[384,1024]{1,0:T(8,128)(2,1)S(1)} collective-permute-done((bf16[384,1024]{1,0:T(8,128)(2,1)S(1)}, bf16[384,1024]{1,0:T(8,128)(2,1)S(1)}, u32[]{:S(2)}, u32[]{:S(2)}) %collective-permute-start.18) | collective-permute-done | bytes 786464 | tf_op jit(solution)/shard_map/ppermute | solution.py:54
  47.5 0.0 copy-done.5
  47.5 0.9 copy-done.6
  48.4 0.4 collective-permute-done.20.refs_7_
  48.7 0.0 copy-done.2
  48.7 74.7 %shard_map.41 = (f32[1,128]{1,0:T(1,128)}, bf16[128,1024]{1,0:T(8,128)(2,1)}) custom-call(s32[1]{0:T(128)} %copy.15.size_ref, bf16[128,1024]{1,0:T(8,128)(2,1)} %own_ref.1, bf16[384,1024]{1,0:T(8,128)(2,1)} %copy-done, bf16[384,1024]{1,0:T(8,128)(2,1)} %copy-done.1, bf16[384,1024]{1,0:T(8,128)(2,1)} %copy-done.3, bf16[384,1024]{1,0:T(8,128)(2,1)} %copy-done.2, ...), custom_call_target="tpu_custom_call" | custom-call | tf_op jit(solution)/shard_map/pallas_call | solution.py:379
  (30 shorter events, 0.2 us)
Async XLA Ops:
  2.3 12.1 %collective-permute-start.8 = (bf16[96,1024]{1,0:T(8,128)(2,1)S(1)}, bf16[96,1024]{1,0:T(8,128)(2,1)S(1)}, u32[]{:S(2)}, u32[]{:S(2)}) collective-permute-start(bf16[96,1024]{1,0:T(8,128)(2,1)S(1)} %fusion), channel_id=1, source_target_pairs={{0,8},{1,9},{2,10},{3,11},{4,12},{5,13},{6,14},{7,15},{8,0},{9,1},... | collective-permute-start | bytes 589832 | tf_op jit(solution)/shard_map/ppermute | solution.py:54
  5.4 11.5 %collective-permute-start.3 = (bf16[96,1024]{1,0:T(8,128)(2,1)S(1)}, bf16[96,1024]{1,0:T(8,128)(2,1)S(1)}, u32[]{:S(2)}, u32[]{:S(2)}) collective-permute-start(bf16[96,1024]{1,0:T(8,128)(2,1)S(1)} %fusion), channel_id=1, source_target_pairs={{0,16},{1,17},{2,18},{3,19},{4,20},{5,21},{6,22},{7,23},{8,24},{9,... | collective-permute-start | bytes 589832 | tf_op jit(solution)/shard_map/ppermute | solution.py:54
  8.0 10.4 %collective-permute-start.2 = (bf16[96,1024]{1,0:T(8,128)(2,1)S(1)}, bf16[96,1024]{1,0:T(8,128)(2,1)S(1)}, u32[]{:S(2)}, u32[]{:S(2)}) collective-permute-start(bf16[96,1024]{1,0:T(8,128)(2,1)S(1)} %fusion), channel_id=1, source_target_pairs={{0,6},{1,7},{2,4},{3,5},{4,2},{5,3},{6,0},{7,1},{8,14},{9,15},{10,... | collective-permute-start | bytes 589832 | tf_op jit(solution)/shard_map/ppermute | solution.py:54
  10.4 9.2 %collective-permute-start.1 = (bf16[96,1024]{1,0:T(8,128)(2,1)S(1)}, bf16[96,1024]{1,0:T(8,128)(2,1)S(1)}, u32[]{:S(2)}, u32[]{:S(2)}) collective-permute-start(bf16[96,1024]{1,0:T(8,128)(2,1)S(1)} %fusion), channel_id=1, source_target_pairs={{0,4},{1,5},{2,6},{3,7},{4,0},{5,1},{6,2},{7,3},{8,12},{9,13},{10,... | collective-permute-start | bytes 589832 | tf_op jit(solution)/shard_map/ppermute | solution.py:54
  10.9 10.1 %collective-permute-start = (bf16[96,1024]{1,0:T(8,128)(2,1)S(1)}, bf16[96,1024]{1,0:T(8,128)(2,1)S(1)}, u32[]{:S(2)}, u32[]{:S(2)}) collective-permute-start(bf16[96,1024]{1,0:T(8,128)(2,1)S(1)} %fusion), channel_id=1, source_target_pairs={{0,2},{1,3},{2,0},{3,1},{4,6},{5,7},{6,4},{7,5},{8,10},{9,11},{10,... | collective-permute-start | bytes 589832 | tf_op jit(solution)/shard_map/ppermute | solution.py:54
  14.4 9.5 %collective-permute-start.10 = (bf16[96,1024]{1,0:T(8,128)(2,1)S(1)}, bf16[96,1024]{1,0:T(8,128)(2,1)S(1)}, u32[]{:S(2)}, u32[]{:S(2)}) collective-permute-start(bf16[96,1024]{1,0:T(8,128)(2,1)S(1)} %collective-permute-done.8), channel_id=1, source_target_pairs={{0,4},{1,5},{2,6},{3,7},{4,0},{5,1},{6,2},{7,3},{8,12},{9,13},{10,... | collective-permute-start | bytes 589832 | tf_op jit(solution)/shard_map/ppermute | solution.py:54
  16.9 7.2 %collective-permute-start.9 = (bf16[96,1024]{1,0:T(8,128)(2,1)S(1)}, bf16[96,1024]{1,0:T(8,128)(2,1)S(1)}, u32[]{:S(2)}, u32[]{:S(2)}) collective-permute-start(bf16[96,1024]{1,0:T(8,128)(2,1)S(1)} %collective-permute-done.8), channel_id=1, source_target_pairs={{0,2},{1,3},{2,0},{3,1},{4,6},{5,7},{6,4},{7,5},{8,10},{9,11},{10,... | collective-permute-start | bytes 589832 | tf_op jit(solution)/shard_map/ppermute | solution.py:54
  18.4 11.7 %collective-permute-start.13 = (bf16[96,1024]{1,0:T(8,128)(2,1)S(1)}, bf16[96,1024]{1,0:T(8,128)(2,1)S(1)}, u32[]{:S(2)}, u32[]{:S(2)}) collective-permute-start(bf16[96,1024]{1,0:T(8,128)(2,1)S(1)} %collective-permute-done.3), channel_id=1, source_target_pairs={{0,8},{1,9},{2,10},{3,11},{4,12},{5,13},{6,14},{7,15},{8,0},{9,1},... | collective-permute-start | bytes 589832 | tf_op jit(solution)/shard_map/ppermute | solution.py:54
  19.6 8.0 %collective-permute-start.5 = (bf16[96,1024]{1,0:T(8,128)(2,1)S(1)}, bf16[96,1024]{1,0:T(8,128)(2,1)S(1)}, u32[]{:S(2)}, u32[]{:S(2)}) collective-permute-start(bf16[96,1024]{1,0:T(8,128)(2,1)S(1)} %collective-permute-done.3), channel_id=1, source_target_pairs={{0,4},{1,5},{2,6},{3,7},{4,0},{5,1},{6,2},{7,3},{8,12},{9,13},{10,... | collective-permute-start | bytes 589832 | tf_op jit(solution)/shard_map/ppermute | solution.py:54
  21.0 8.1 %collective-permute-start.4 = (bf16[96,1024]{1,0:T(8,128)(2,1)S(1)}, bf16[96,1024]{1,0:T(8,128)(2,1)S(1)}, u32[]{:S(2)}, u32[]{:S(2)}) collective-permute-start(bf16[96,1024]{1,0:T(8,128)(2,1)S(1)} %collective-permute-done.3), channel_id=1, source_target_pairs={{0,2},{1,3},{2,0},{3,1},{4,6},{5,7},{6,4},{7,5},{8,10},{9,11},{10,... | collective-permute-start | bytes 589832 | tf_op jit(solution)/shard_map/ppermute | solution.py:54
  22.6 8.8 %copy-start = (bf16[384,1024]{1,0:T(8,128)(2,1)}, bf16[384,1024]{1,0:T(8,128)(2,1)S(1)}, u32[]{:S(2)}) copy-start(bf16[384,1024]{1,0:T(8,128)(2,1)S(1)} %pad_maximum_fusion.refs_0_) | copy-start | bytes 2359300
  23.9 22.0 %collective-permute-start.17 = (bf16[384,1024]{1,0:T(8,128)(2,1)S(1)}, bf16[384,1024]{1,0:T(8,128)(2,1)S(1)}, u32[]{:S(2)}, u32[]{:S(2)}) collective-permute-start(bf16[384,1024]{1,0:T(8,128)(2,1)S(1)} %pad_maximum_fusion.refs_0_), channel_id=1, source_target_pairs={{0,1},{1,0},{2,3},{3,2},{4,5},{5,4},{6,7},{7,6},{8,9},{9,8},{10,11... | collective-permute-start | bytes 2359304 | tf_op jit(solution)/shard_map/ppermute | solution.py:54
  24.1 13.4 %collective-permute-start.12 = (bf16[48,1024]{1,0:T(8,128)(2,1)S(1)}, bf16[48,1024]{1,0:T(8,128)(2,1)S(1)}, u32[]{:S(2)}, u32[]{:S(2)}) collective-permute-start(bf16[48,1024]{1,0:T(8,128)(2,1)S(1)} %slice.24), channel_id=1, source_target_pairs={{0,2},{1,3},{2,0},{3,1},{4,6},{5,7},{6,4},{7,5},{8,10},{9,11},{10,... | collective-permute-start | bytes 294920 | tf_op jit(solution)/shard_map/ppermute | solution.py:54
  27.6 8.5 %collective-permute-start.11 = (bf16[48,1024]{1,0:T(8,128)(2,1)S(1)}, bf16[48,1024]{1,0:T(8,128)(2,1)S(1)}, u32[]{:S(2)}, u32[]{:S(2)}) collective-permute-start(bf16[48,1024]{1,0:T(8,128)(2,1)S(1)} %slice.23), channel_id=1, source_target_pairs={{0,4},{1,5},{2,6},{3,7},{4,0},{5,1},{6,2},{7,3},{8,12},{9,13},{10,... | collective-permute-start | bytes 294920 | tf_op jit(solution)/shard_map/ppermute | solution.py:54
  29.1 9.4 %collective-permute-start.7 = (bf16[48,1024]{1,0:T(8,128)(2,1)S(1)}, bf16[48,1024]{1,0:T(8,128)(2,1)S(1)}, u32[]{:S(2)}, u32[]{:S(2)}) collective-permute-start(bf16[48,1024]{1,0:T(8,128)(2,1)S(1)} %slice.22), channel_id=1, source_target_pairs={{0,2},{1,3},{2,0},{3,1},{4,6},{5,7},{6,4},{7,5},{8,10},{9,11},{10,... | collective-permute-start | bytes 294920 | tf_op jit(solution)/shard_map/ppermute | solution.py:54
  30.2 4.7 %collective-permute-start.6 = (bf16[48,1024]{1,0:T(8,128)(2,1)S(1)}, bf16[48,1024]{1,0:T(8,128)(2,1)S(1)}, u32[]{:S(2)}, u32[]{:S(2)}) collective-permute-start(bf16[48,1024]{1,0:T(8,128)(2,1)S(1)} %slice.21), channel_id=1, source_target_pairs={{0,4},{1,5},{2,6},{3,7},{4,0},{5,1},{6,2},{7,3},{8,12},{9,13},{10,... | collective-permute-start | bytes 294920 | tf_op jit(solution)/shard_map/ppermute | solution.py:54
  34.9 10.5 %collective-permute-start.16 = (bf16[96,1024]{1,0:T(8,128)(2,1)S(1)}, bf16[96,1024]{1,0:T(8,128)(2,1)S(1)}, u32[]{:S(2)}, u32[]{:S(2)}) collective-permute-start(bf16[96,1024]{1,0:T(8,128)(2,1)S(1)} %collective-permute-done.13), channel_id=1, source_target_pairs={{0,6},{1,7},{2,4},{3,5},{4,2},{5,3},{6,0},{7,1},{8,14},{9,15},{10,... | collective-permute-start | bytes 589832 | tf_op jit(solution)/shard_map/ppermute | solution.py:54
  36.1 9.2 %collective-permute-start.15 = (bf16[96,1024]{1,0:T(8,128)(2,1)S(1)}, bf16[96,1024]{1,0:T(8,128)(2,1)S(1)}, u32[]{:S(2)}, u32[]{:S(2)}) collective-permute-start(bf16[96,1024]{1,0:T(8,128)(2,1)S(1)} %collective-permute-done.13), channel_id=1, source_target_pairs={{0,4},{1,5},{2,6},{3,7},{4,0},{5,1},{6,2},{7,3},{8,12},{9,13},{10,... | collective-permute-start | bytes 589832 | tf_op jit(solution)/shard_map/ppermute | solution.py:54
  37.5 7.7 %collective-permute-start.14 = (bf16[96,1024]{1,0:T(8,128)(2,1)S(1)}, bf16[96,1024]{1,0:T(8,128)(2,1)S(1)}, u32[]{:S(2)}, u32[]{:S(2)}) collective-permute-start(bf16[96,1024]{1,0:T(8,128)(2,1)S(1)} %collective-permute-done.13), channel_id=1, source_target_pairs={{0,2},{1,3},{2,0},{3,1},{4,6},{5,7},{6,4},{7,5},{8,10},{9,11},{10,... | collective-permute-start | bytes 589832 | tf_op jit(solution)/shard_map/ppermute | solution.py:54
  38.5 10.2 %copy-start.3 = (bf16[384,1024]{1,0:T(8,128)(2,1)}, bf16[384,1024]{1,0:T(8,128)(2,1)S(1)}, u32[]{:S(2)}) copy-start(bf16[384,1024]{1,0:T(8,128)(2,1)S(1)} %constant_dynamic-update-slice_fusion.5.refs_2_) | copy-start | bytes 2359300
  38.5 7.3 %collective-permute-start.19 = (bf16[384,1024]{1,0:T(8,128)(2,1)S(1)}, bf16[384,1024]{1,0:T(8,128)(2,1)S(1)}, u32[]{:S(2)}, u32[]{:S(2)}) collective-permute-start(bf16[384,1024]{1,0:T(8,128)(2,1)S(1)} %constant_dynamic-update-slice_fusion.5.refs_2_), channel_id=1, source_target_pairs={{0,1},{1,0},{2,3},{3,2},{4,5},{5,4},{6,7},{7,6},{8,9},{9,8},{10,11... | collective-permute-start | bytes 2359304 | tf_op jit(solution)/shard_map/ppermute | solution.py:54
  38.6 10.1 %copy-start.1 = (bf16[384,1024]{1,0:T(8,128)(2,1)}, bf16[384,1024]{1,0:T(8,128)(2,1)S(1)}, u32[]{:S(2)}) copy-start(bf16[384,1024]{1,0:T(8,128)(2,1)S(1)} %constant_dynamic-update-slice_fusion.refs_1_) | copy-start | bytes 2359300
  45.2 2.3 %collective-permute-start.18 = (bf16[384,1024]{1,0:T(8,128)(2,1)S(1)}, bf16[384,1024]{1,0:T(8,128)(2,1)S(1)}, u32[]{:S(2)}, u32[]{:S(2)}) collective-permute-start(bf16[384,1024]{1,0:T(8,128)(2,1)S(1)} %constant_dynamic-update-slice_fusion.refs_1_), channel_id=1, source_target_pairs={{0,1},{1,0},{2,3},{3,2},{4,5},{5,4},{6,7},{7,6},{8,9},{9,8},{10,11... | collective-permute-start | bytes 2359304 | tf_op jit(solution)/shard_map/ppermute | solution.py:54
  45.4 3.4 %copy-start.2 = (bf16[384,1024]{1,0:T(8,128)(2,1)}, bf16[384,1024]{1,0:T(8,128)(2,1)S(1)}, u32[]{:S(2)}) copy-start(bf16[384,1024]{1,0:T(8,128)(2,1)S(1)} %constant_dynamic-update-slice_fusion.10.refs_3_) | copy-start | bytes 2359300
  45.4 3.3 %collective-permute-start.20 = (bf16[384,1024]{1,0:T(8,128)(2,1)S(1)}, bf16[384,1024]{1,0:T(8,128)(2,1)}, u32[]{:S(2)}, u32[]{:S(2)}) collective-permute-start(bf16[384,1024]{1,0:T(8,128)(2,1)S(1)} %constant_dynamic-update-slice_fusion.10.refs_3_), channel_id=1, source_target_pairs={{0,1},{1,0},{2,3},{3,2},{4,5},{5,4},{6,7},{7,6},{8,9},{9,8},{10,11... | collective-permute-start | bytes 2359304 | tf_op jit(solution)/shard_map/ppermute | solution.py:54
  45.9 2.9 %copy-start.4 = (bf16[384,1024]{1,0:T(8,128)(2,1)}, bf16[384,1024]{1,0:T(8,128)(2,1)S(1)}, u32[]{:S(2)}) copy-start(bf16[384,1024]{1,0:T(8,128)(2,1)S(1)} %collective-permute-done.17.refs_4_) | copy-start | bytes 2359300
  45.9 1.6 %copy-start.5 = (bf16[384,1024]{1,0:T(8,128)(2,1)}, bf16[384,1024]{1,0:T(8,128)(2,1)S(1)}, u32[]{:S(2)}) copy-start(bf16[384,1024]{1,0:T(8,128)(2,1)S(1)} %collective-permute-done.19.refs_6_) | copy-start | bytes 2359300
  47.5 0.9 copy-start.6

commit v6 on v5

--- a/solution.py
+++ b/solution.py
@@ -15,6 +15,7 @@
 DEAD_ABOVE = 512.0
 SUB = 8
 HALF = 8
+NEAR = 16.0
 LANES = 128
 TILE = 256
 PACK = 16
@@ -142,42 +143,63 @@
     return rows, count
 
 
-def moments(keys, rows, count, mean_ref, work):
+def moments(keys, rows, count, centre_ref, mean_ref, sums_ref, work):
     dim = keys.shape[1]
-    tiles = dim // TILE
-
-    def add_sums(index, sums):
-        start = pl.multiple_of(index * REST, REST)
-        block = keys[pl.ds(start, REST), :]
-        part = jnp.where(live_of(block), block.astype(jnp.float32), 0.0)
-        return sums + jnp.sum(part.reshape(REST // SUB, SUB, dim), axis=0)
-
-    sums = lax.fori_loop(0, pl.cdiv(rows, REST), add_sums, jnp.zeros((SUB, dim), jnp.float32))
+    spans = [
+        (slice(tile * TILE, (tile + 1) * TILE), slice(0, (tile + 1) * TILE))
+        for tile in range(dim // TILE)
+    ]
+    work[...] = jnp.zeros_like(work)
+    sums_ref[...] = jnp.zeros_like(sums_ref)
+
+    def add_plain(start, step):
+        block = keys[pl.ds(start, step), :]
+        live = live_of(block)
+        high = jnp.where(live, block.astype(jnp.float32), 0.0).astype(block.dtype)
+        alive = jnp.where(live, jnp.ones((step, LANES), jnp.float32), 0.0).astype(block.dtype)
+        sums_ref[...] += product(alive, high, 0, 0)
+        for here, upto in spans:
+            work[here, upto] += product(high[:, here], high[:, upto], 0, 0)
+
+    over_chunks(rows, add_plain)
     count = jnp.full((1, 1), count.astype(jnp.float32))
-    mean = jnp.sum(sums, axis=0, keepdims=True) / count
-    mean_ref[...] = mean
-    work[...] = jnp.zeros_like(work)
-
-    def add_products(start, step):
-        block = keys[pl.ds(start, step), :]
-        centred = jnp.where(live_of(block), block.astype(jnp.float32) - mean_ref[...], 0.0)
-        high, low = two_parts(centred)
-        for tile in range(tiles):
-            here = slice(tile * TILE, (tile + 1) * TILE)
-            upto = slice(0, (tile + 1) * TILE)
-            part = product(high[:, here], high[:, upto], 0, 0)
-            part += product(high[:, here], low[:, upto], 0, 0)
-            part += product(low[:, here], high[:, upto], 0, 0)
-            work[here, upto] += part
-
-    over_chunks(rows, add_products)
-    for tile in range(tiles):
-        here = slice(tile * TILE, (tile + 1) * TILE)
-        upto = slice(0, (tile + 1) * TILE)
-        shape = (TILE, (tile + 1) * TILE)
-        down = lax.broadcasted_iota(jnp.int32, shape, 0) + tile * TILE
+    mean = sums_ref[0:1, :] / count
+    squares = []
+    for here, upto in spans:
+        shape = (TILE, TILE)
+        down, across = (lax.broadcasted_iota(jnp.int32, shape, axis) for axis in (0, 1))
+        diagonal = jnp.where(down == across, work[here, here], 0.0)
+        squares.append(jnp.sum(diagonal, axis=0, keepdims=True))
+    spread = jnp.concatenate(squares, axis=1) / count - mean * mean
+    offset = jnp.max(jnp.where(mean * mean > NEAR * spread, 1.0, 0.0)) > 0.5
+    centre_ref[...] = jnp.where(offset, mean, 0.0)
+    mean_ref[...] = jnp.where(offset, 0.0, mean)
+
+    @pl.when(offset)
+    def _():
+        work[...] = jnp.zeros_like(work)
+
+        def add_centred(start, step):
+            block = keys[pl.ds(start, step), :]
+            centred = block.astype(jnp.float32) - centre_ref[...]
+            high, low = two_parts(jnp.where(live_of(block), centred, 0.0))
+            for here, upto in spans:
+                part = product(high[:, here], high[:, upto], 0, 0)
+                part += product(high[:, here], low[:, upto], 0, 0)
+                part += product(low[:, here], high[:, upto], 0, 0)
+                work[here, upto] += part
+
+        over_chunks(rows, add_centred)
+
+    for here, upto in spans:
+        shape = (TILE, upto.stop)
+        down = lax.broadcasted_iota(jnp.int32, shape, 0) + here.start
         across = lax.broadcasted_iota(jnp.int32, shape, 1)
-        work[here, upto] = work[here, upto] / count + jnp.where(down == across, RIDGE, 0.0)
+        column = jnp.broadcast_to(mean_ref[:, here], (LANES, TILE)).T
+        outer = jnp.concatenate([column] * (upto.stop // LANES), axis=1) * mean_ref[:, upto]
+        ridge = jnp.where(down == across, RIDGE, 0.0)
+        work[here, upto] = work[here, upto] / count - outer + ridge
+    return offset
 
 
 def invert_factor(rows, inverse):
@@ -295,22 +317,56 @@
     low_ref[...] = low
 
 
-def scores(keys, rows, own_ref, own_size, own_start, mean_ref, high_ref, low_ref, density, total):
+def scores(
+    keys,
+    rows,
+    offset,
+    own_ref,
+    own_size,
+    own_start,
+    centre_ref,
+    mean_ref,
+    high_ref,
+    low_ref,
+    white_ref,
+    density,
+    total,
+):
     dim = keys.shape[1]
     queries = own_ref.shape[0]
     sharpness = 2.0 * math.sqrt(dim)
+    mean_high, mean_low = two_parts(jnp.broadcast_to(mean_ref[...], (PACK, dim)))
+    spans = [
+        (slice(tile * TILE, (tile + 1) * TILE), slice(0, (tile + 1) * TILE))
+        for tile in range(dim // TILE)
+    ]
+    moved = []
+    for here, upto in spans:
+        part = product(mean_high[:, upto], high_ref[here, upto], 1, 1)
+        part += product(mean_high[:, upto], low_ref[here, upto], 1, 1)
+        part += product(mean_low[:, upto], high_ref[here, upto], 1, 1)
+        moved.append(part[0:1, :])
 
     def whitened(values):
-        high, low = two_parts(values.astype(jnp.float32) - mean_ref[...])
-        parts = []
-        for tile in range(dim // TILE):
-            here = slice(tile * TILE, (tile + 1) * TILE)
-            upto = slice(0, (tile + 1) * TILE)
-            part = product(high[:, upto], high_ref[here, upto], 1, 1)
-            part += product(high[:, upto], low_ref[here, upto], 1, 1)
-            part += product(low[:, upto], high_ref[here, upto], 1, 1)
-            parts.append(part.astype(jnp.bfloat16))
-        return jnp.concatenate(parts, axis=1)
+        count = values.shape[0]
+
+        @pl.when(offset)
+        def _():
+            high, low = two_parts(values.astype(jnp.float32) - centre_ref[...])
+            for here, upto in spans:
+                part = product(high[:, upto], high_ref[here, upto], 1, 1)
+                part += product(high[:, upto], low_ref[here, upto], 1, 1)
+                part += product(low[:, upto], high_ref[here, upto], 1, 1)
+                white_ref[0:count, here] = part.astype(jnp.bfloat16)
+
+        @pl.when(jnp.logical_not(offset))
+        def _():
+            for (here, upto), shift in zip(spans, moved):
+                part = product(values[:, upto], high_ref[here, upto], 1, 1)
+                part += product(values[:, upto], low_ref[here, upto], 1, 1)
+                white_ref[0:count, here] = (part - shift).astype(jnp.bfloat16)
+
+        return white_ref[0:count, :]
 
     def lengths(white):
         wide = white.astype(jnp.float32)
@@ -347,9 +403,10 @@
 def local_kernel(group_count, size_ref, own_ref, *refs):
     groups, refs = refs[:group_count], refs[group_count:]
     log_ref, out_ref, keys, counts, sizes, starts, arrived, copied = refs[:8]
-    mean_ref, work, found, block, part, high_ref, low_ref, density, total = refs[8:]
+    centre_ref, mean_ref, sums_ref, work, found, block, part, high_ref, low_ref = refs[8:17]
+    white_ref, density, total = refs[17:]
     rows, count = collect(groups, keys, counts, sizes, starts, arrived, copied)
-    moments(keys, rows, count, mean_ref, work)
+    offset = moments(keys, rows, count, centre_ref, mean_ref, sums_ref, work)
     whitener(work, found, block, part, high_ref, low_ref)
     block_count = size_ref.shape[0]
     block_rows = own_ref.shape[0] // block_count
@@ -358,12 +415,15 @@
         log_ref[here : here + 1, :], out_ref[span, :] = scores(
             keys,
             rows,
+            offset,
             own_ref.at[span],
             size_ref[here],
             starts[here],
+            centre_ref,
             mean_ref,
             high_ref,
             low_ref,
+            white_ref,
             density,
             total,
         )
@@ -396,12 +456,15 @@
             pltpu.SemaphoreType.DMA((len(groups),)),
             pltpu.SemaphoreType.DMA,
             pltpu.VMEM((1, dim), jnp.float32),
+            pltpu.VMEM((1, dim), jnp.float32),
+            pltpu.VMEM((LANES, dim), jnp.float32),
             pltpu.VMEM(square, jnp.float32),
             pltpu.VMEM(square, jnp.float32),
             pltpu.VMEM((LANES, LANES), jnp.float32),
             pltpu.VMEM((LANES, LANES), jnp.float32),
             pltpu.VMEM(square, jnp.bfloat16),
             pltpu.VMEM(square, jnp.bfloat16),
+            pltpu.VMEM((CHUNK, dim), jnp.bfloat16),
             pltpu.VMEM((1, block_rows), jnp.float32),
             pltpu.VMEM((block_rows, dim), jnp.float32),
         ],

time: 124 us -> 116 us (0.935)
  Pallas kernels: 74.7 us -> 66.9 us
    pallas_call x1, Pallas kernels: 74.7 us -> 66.9 us  [local_call(): pl.pallas_call(functools.partial(local_kernel, len(groups)), out_shape=[j...]
where the time goes in v6:
time: 116 us
  Pallas kernels  66.9 us (58%)
  starting transfers between devices  25.7 us (22%)
  waiting for transfers between devices  19.3 us (17%)
  between operations  1.67 us (1%)
    pallas_call x1, Pallas kernels, local_call(): pl.pallas_call(functools.partial(local_kernel, len(groups)), out_shape=[j...  66.9 us
    ppermute x21, starting transfers between devices, flipped(): lax.ppermute(value, 'dev', [(source, source ^ mask) for source in range(s...  25.7 us
    ppermute x21, waiting for transfers between devices, flipped(): lax.ppermute(value, 'dev', [(source, source ^ mask) for source in range(s...  19.3 us
  transfers between devices with their start and end apart: 21, of which 12 were waited for; matrix products, arithmetic and copies ran while one was open for 0% of the time, Pallas kernels for 0%

profile of v6, /device:TPU:0, one launch (start us, length us, event | category | flops | bytes accessed | tf_op | source)
XLA Modules:
  0.0 115.8 jit_solution(4880849434582891877)
XLA Ops:
  1.3 1.0 fusion
  2.3 3.1 %collective-permute-start.8 = (bf16[96,1024]{1,0:T(8,128)(2,1)S(1)}, bf16[96,1024]{1,0:T(8,128)(2,1)S(1)}, u32[]{:S(2)}, u32[]{:S(2)}) collective-permute-start(bf16[96,1024]{1,0:T(8,128)(2,1)S(1)} %fusion), channel_id=1, source_target_pairs={{0,8},{1,9},{2,10},{3,11},{4,12},{5,13},{6,14},{7,15},{8,0},{9,1},... | collective-permute-start | bytes 589832 | tf_op jit(solution)/shard_map/ppermute | solution.py:55
  5.4 2.6 %collective-permute-start.3 = (bf16[96,1024]{1,0:T(8,128)(2,1)S(1)}, bf16[96,1024]{1,0:T(8,128)(2,1)S(1)}, u32[]{:S(2)}, u32[]{:S(2)}) collective-permute-start(bf16[96,1024]{1,0:T(8,128)(2,1)S(1)} %fusion), channel_id=1, source_target_pairs={{0,16},{1,17},{2,18},{3,19},{4,20},{5,21},{6,22},{7,23},{8,24},{9,... | collective-permute-start | bytes 589832 | tf_op jit(solution)/shard_map/ppermute | solution.py:55
  8.0 2.4 %collective-permute-start.2 = (bf16[96,1024]{1,0:T(8,128)(2,1)S(1)}, bf16[96,1024]{1,0:T(8,128)(2,1)S(1)}, u32[]{:S(2)}, u32[]{:S(2)}) collective-permute-start(bf16[96,1024]{1,0:T(8,128)(2,1)S(1)} %fusion), channel_id=1, source_target_pairs={{0,6},{1,7},{2,4},{3,5},{4,2},{5,3},{6,0},{7,1},{8,14},{9,15},{10,... | collective-permute-start | bytes 589832 | tf_op jit(solution)/shard_map/ppermute | solution.py:55
  10.4 0.5 collective-permute-start.1
  10.9 0.5 collective-permute-start
  11.5 2.9 %collective-permute-done.8 = bf16[96,1024]{1,0:T(8,128)(2,1)S(1)} collective-permute-done((bf16[96,1024]{1,0:T(8,128)(2,1)S(1)}, bf16[96,1024]{1,0:T(8,128)(2,1)S(1)}, u32[]{:S(2)}, u32[]{:S(2)}) %collective-permute-start.8) | collective-permute-done | bytes 196640 | tf_op jit(solution)/shard_map/ppermute | solution.py:55
  14.4 1.7 %collective-permute-start.10 = (bf16[96,1024]{1,0:T(8,128)(2,1)S(1)}, bf16[96,1024]{1,0:T(8,128)(2,1)S(1)}, u32[]{:S(2)}, u32[]{:S(2)}) collective-permute-start(bf16[96,1024]{1,0:T(8,128)(2,1)S(1)} %collective-permute-done.8), channel_id=1, source_target_pairs={{0,4},{1,5},{2,6},{3,7},{4,0},{5,1},{6,2},{7,3},{8,12},{9,13},{10,... | collective-permute-start | bytes 589832 | tf_op jit(solution)/shard_map/ppermute | solution.py:55
  16.1 0.8 collective-permute-done.3
  16.9 1.5 %collective-permute-start.9 = (bf16[96,1024]{1,0:T(8,128)(2,1)S(1)}, bf16[96,1024]{1,0:T(8,128)(2,1)S(1)}, u32[]{:S(2)}, u32[]{:S(2)}) collective-permute-start(bf16[96,1024]{1,0:T(8,128)(2,1)S(1)} %collective-permute-done.8), channel_id=1, source_target_pairs={{0,2},{1,3},{2,0},{3,1},{4,6},{5,7},{6,4},{7,5},{8,10},{9,11},{10,... | collective-permute-start | bytes 589832 | tf_op jit(solution)/shard_map/ppermute | solution.py:55
  18.4 0.0 collective-permute-done.2
  18.4 0.5 collective-permute-start.13
  19.0 0.7 collective-permute-done.1
  19.6 1.2 collective-permute-start.5
  20.8 0.2 collective-permute-done
  21.0 1.4 %collective-permute-start.4 = (bf16[96,1024]{1,0:T(8,128)(2,1)S(1)}, bf16[96,1024]{1,0:T(8,128)(2,1)S(1)}, u32[]{:S(2)}, u32[]{:S(2)}) collective-permute-start(bf16[96,1024]{1,0:T(8,128)(2,1)S(1)} %collective-permute-done.3), channel_id=1, source_target_pairs={{0,2},{1,3},{2,0},{3,1},{4,6},{5,7},{6,4},{7,5},{8,10},{9,11},{10,... | collective-permute-start | bytes 589832 | tf_op jit(solution)/shard_map/ppermute | solution.py:55
  22.5 0.1 pad_maximum_fusion.refs_0_
  22.6 1.3 %collective-permute-done.10 = bf16[96,1024]{1,0:T(8,128)(2,1)S(1)} collective-permute-done((bf16[96,1024]{1,0:T(8,128)(2,1)S(1)}, bf16[96,1024]{1,0:T(8,128)(2,1)S(1)}, u32[]{:S(2)}, u32[]{:S(2)}) %collective-permute-start.10) | collective-permute-done | bytes 196640 | tf_op jit(solution)/shard_map/ppermute | solution.py:55
  23.9 0.0 collective-permute-start.17
  23.9 0.2 collective-permute-done.9
  24.1 2.5 %collective-permute-start.12 = (bf16[48,1024]{1,0:T(8,128)(2,1)S(1)}, bf16[48,1024]{1,0:T(8,128)(2,1)S(1)}, u32[]{:S(2)}, u32[]{:S(2)}) collective-permute-start(bf16[48,1024]{1,0:T(8,128)(2,1)S(1)} %slice.24), channel_id=1, source_target_pairs={{0,2},{1,3},{2,0},{3,1},{4,6},{5,7},{6,4},{7,5},{8,10},{9,11},{10,... | collective-permute-start | bytes 294920 | tf_op jit(solution)/shard_map/ppermute | solution.py:55
  26.6 1.0 collective-permute-done.5
  27.6 1.5 %collective-permute-start.11 = (bf16[48,1024]{1,0:T(8,128)(2,1)S(1)}, bf16[48,1024]{1,0:T(8,128)(2,1)S(1)}, u32[]{:S(2)}, u32[]{:S(2)}) collective-permute-start(bf16[48,1024]{1,0:T(8,128)(2,1)S(1)} %slice.23), channel_id=1, source_target_pairs={{0,4},{1,5},{2,6},{3,7},{4,0},{5,1},{6,2},{7,3},{8,12},{9,13},{10,... | collective-permute-start | bytes 294920 | tf_op jit(solution)/shard_map/ppermute | solution.py:55
  29.1 0.0 collective-permute-done.4
  29.1 1.0 collective-permute-start.7
  30.2 0.0 collective-permute-done.13
  30.2 1.1 collective-permute-start.6
  31.4 3.5 %collective-permute-done.6 = bf16[48,1024]{1,0:T(8,128)(2,1)S(1)} collective-permute-done((bf16[48,1024]{1,0:T(8,128)(2,1)S(1)}, bf16[48,1024]{1,0:T(8,128)(2,1)S(1)}, u32[]{:S(2)}, u32[]{:S(2)}) %collective-permute-start.6) | collective-permute-done | bytes 98336 | tf_op jit(solution)/shard_map/ppermute | solution.py:55
  34.9 1.2 %collective-permute-start.16 = (bf16[96,1024]{1,0:T(8,128)(2,1)S(1)}, bf16[96,1024]{1,0:T(8,128)(2,1)S(1)}, u32[]{:S(2)}, u32[]{:S(2)}) collective-permute-start(bf16[96,1024]{1,0:T(8,128)(2,1)S(1)} %collective-permute-done.13), channel_id=1, source_target_pairs={{0,6},{1,7},{2,4},{3,5},{4,2},{5,3},{6,0},{7,1},{8,14},{9,15},{10,... | collective-permute-start | bytes 589832 | tf_op jit(solution)/shard_map/ppermute | solution.py:55
  36.1 0.0 collective-permute-done.11
  36.1 1.4 %collective-permute-start.15 = (bf16[96,1024]{1,0:T(8,128)(2,1)S(1)}, bf16[96,1024]{1,0:T(8,128)(2,1)S(1)}, u32[]{:S(2)}, u32[]{:S(2)}) collective-permute-start(bf16[96,1024]{1,0:T(8,128)(2,1)S(1)} %collective-permute-done.13), channel_id=1, source_target_pairs={{0,4},{1,5},{2,6},{3,7},{4,0},{5,1},{6,2},{7,3},{8,12},{9,13},{10,... | collective-permute-start | bytes 589832 | tf_op jit(solution)/shard_map/ppermute | solution.py:55
  37.5 0.0 collective-permute-done.12
  37.5 1.0 collective-permute-start.14
  38.5 0.0 collective-permute-done.7
  38.5 0.1 collective-permute-start.19
  38.6 6.5 %collective-permute-done.14 = bf16[96,1024]{1,0:T(8,128)(2,1)S(1)} collective-permute-done((bf16[96,1024]{1,0:T(8,128)(2,1)S(1)}, bf16[96,1024]{1,0:T(8,128)(2,1)S(1)}, u32[]{:S(2)}, u32[]{:S(2)}) %collective-permute-start.14) | collective-permute-done | bytes 196640 | tf_op jit(solution)/shard_map/ppermute | solution.py:55
  45.2 0.0 collective-permute-start.18
  45.2 0.1 collective-permute-done.15
  45.3 0.0 collective-permute-done.16
  45.4 0.5 collective-permute-start.20
  45.9 0.0 collective-permute-done.17.refs_4_
  45.9 0.0 collective-permute-done.19.refs_6_
  45.9 1.6 %collective-permute-done.18.refs_5_ = bf16[384,1024]{1,0:T(8,128)(2,1)S(1)} collective-permute-done((bf16[384,1024]{1,0:T(8,128)(2,1)S(1)}, bf16[384,1024]{1,0:T(8,128)(2,1)S(1)}, u32[]{:S(2)}, u32[]{:S(2)}) %collective-permute-start.18) | collective-permute-done | bytes 786464 | tf_op jit(solution)/shard_map/ppermute | solution.py:55
  47.5 0.0 copy-done.5
  47.5 0.9 copy-done.6
  48.4 0.4 collective-permute-done.20.refs_7_
  48.7 0.0 copy-done.2
  48.7 66.9 %shard_map.41 = (f32[1,128]{1,0:T(1,128)}, bf16[128,1024]{1,0:T(8,128)(2,1)}) custom-call(s32[1]{0:T(128)} %copy.15.size_ref, bf16[128,1024]{1,0:T(8,128)(2,1)} %own_ref.1, bf16[384,1024]{1,0:T(8,128)(2,1)} %copy-done, bf16[384,1024]{1,0:T(8,128)(2,1)} %copy-done.1, bf16[384,1024]{1,0:T(8,128)(2,1)} %copy-done.3, bf16[384,1024]{1,0:T(8,128)(2,1)} %copy-done.2, ...), custom_call_target="tpu_custom_call" | custom-call | tf_op jit(solution)/shard_map/pallas_call | solution.py:439
  (30 shorter events, 0.2 us)
Async XLA Ops:
  2.3 12.1 %collective-permute-start.8 = (bf16[96,1024]{1,0:T(8,128)(2,1)S(1)}, bf16[96,1024]{1,0:T(8,128)(2,1)S(1)}, u32[]{:S(2)}, u32[]{:S(2)}) collective-permute-start(bf16[96,1024]{1,0:T(8,128)(2,1)S(1)} %fusion), channel_id=1, source_target_pairs={{0,8},{1,9},{2,10},{3,11},{4,12},{5,13},{6,14},{7,15},{8,0},{9,1},... | collective-permute-start | bytes 589832 | tf_op jit(solution)/shard_map/ppermute | solution.py:55
  5.4 11.5 %collective-permute-start.3 = (bf16[96,1024]{1,0:T(8,128)(2,1)S(1)}, bf16[96,1024]{1,0:T(8,128)(2,1)S(1)}, u32[]{:S(2)}, u32[]{:S(2)}) collective-permute-start(bf16[96,1024]{1,0:T(8,128)(2,1)S(1)} %fusion), channel_id=1, source_target_pairs={{0,16},{1,17},{2,18},{3,19},{4,20},{5,21},{6,22},{7,23},{8,24},{9,... | collective-permute-start | bytes 589832 | tf_op jit(solution)/shard_map/ppermute | solution.py:55
  8.0 10.4 %collective-permute-start.2 = (bf16[96,1024]{1,0:T(8,128)(2,1)S(1)}, bf16[96,1024]{1,0:T(8,128)(2,1)S(1)}, u32[]{:S(2)}, u32[]{:S(2)}) collective-permute-start(bf16[96,1024]{1,0:T(8,128)(2,1)S(1)} %fusion), channel_id=1, source_target_pairs={{0,6},{1,7},{2,4},{3,5},{4,2},{5,3},{6,0},{7,1},{8,14},{9,15},{10,... | collective-permute-start | bytes 589832 | tf_op jit(solution)/shard_map/ppermute | solution.py:55
  10.4 9.2 %collective-permute-start.1 = (bf16[96,1024]{1,0:T(8,128)(2,1)S(1)}, bf16[96,1024]{1,0:T(8,128)(2,1)S(1)}, u32[]{:S(2)}, u32[]{:S(2)}) collective-permute-start(bf16[96,1024]{1,0:T(8,128)(2,1)S(1)} %fusion), channel_id=1, source_target_pairs={{0,4},{1,5},{2,6},{3,7},{4,0},{5,1},{6,2},{7,3},{8,12},{9,13},{10,... | collective-permute-start | bytes 589832 | tf_op jit(solution)/shard_map/ppermute | solution.py:55
  10.9 10.1 %collective-permute-start = (bf16[96,1024]{1,0:T(8,128)(2,1)S(1)}, bf16[96,1024]{1,0:T(8,128)(2,1)S(1)}, u32[]{:S(2)}, u32[]{:S(2)}) collective-permute-start(bf16[96,1024]{1,0:T(8,128)(2,1)S(1)} %fusion), channel_id=1, source_target_pairs={{0,2},{1,3},{2,0},{3,1},{4,6},{5,7},{6,4},{7,5},{8,10},{9,11},{10,... | collective-permute-start | bytes 589832 | tf_op jit(solution)/shard_map/ppermute | solution.py:55
  14.4 9.5 %collective-permute-start.10 = (bf16[96,1024]{1,0:T(8,128)(2,1)S(1)}, bf16[96,1024]{1,0:T(8,128)(2,1)S(1)}, u32[]{:S(2)}, u32[]{:S(2)}) collective-permute-start(bf16[96,1024]{1,0:T(8,128)(2,1)S(1)} %collective-permute-done.8), channel_id=1, source_target_pairs={{0,4},{1,5},{2,6},{3,7},{4,0},{5,1},{6,2},{7,3},{8,12},{9,13},{10,... | collective-permute-start | bytes 589832 | tf_op jit(solution)/shard_map/ppermute | solution.py:55
  16.9 7.2 %collective-permute-start.9 = (bf16[96,1024]{1,0:T(8,128)(2,1)S(1)}, bf16[96,1024]{1,0:T(8,128)(2,1)S(1)}, u32[]{:S(2)}, u32[]{:S(2)}) collective-permute-start(bf16[96,1024]{1,0:T(8,128)(2,1)S(1)} %collective-permute-done.8), channel_id=1, source_target_pairs={{0,2},{1,3},{2,0},{3,1},{4,6},{5,7},{6,4},{7,5},{8,10},{9,11},{10,... | collective-permute-start | bytes 589832 | tf_op jit(solution)/shard_map/ppermute | solution.py:55
  18.4 11.7 %collective-permute-start.13 = (bf16[96,1024]{1,0:T(8,128)(2,1)S(1)}, bf16[96,1024]{1,0:T(8,128)(2,1)S(1)}, u32[]{:S(2)}, u32[]{:S(2)}) collective-permute-start(bf16[96,1024]{1,0:T(8,128)(2,1)S(1)} %collective-permute-done.3), channel_id=1, source_target_pairs={{0,8},{1,9},{2,10},{3,11},{4,12},{5,13},{6,14},{7,15},{8,0},{9,1},... | collective-permute-start | bytes 589832 | tf_op jit(solution)/shard_map/ppermute | solution.py:55
  19.6 8.0 %collective-permute-start.5 = (bf16[96,1024]{1,0:T(8,128)(2,1)S(1)}, bf16[96,1024]{1,0:T(8,128)(2,1)S(1)}, u32[]{:S(2)}, u32[]{:S(2)}) collective-permute-start(bf16[96,1024]{1,0:T(8,128)(2,1)S(1)} %collective-permute-done.3), channel_id=1, source_target_pairs={{0,4},{1,5},{2,6},{3,7},{4,0},{5,1},{6,2},{7,3},{8,12},{9,13},{10,... | collective-permute-start | bytes 589832 | tf_op jit(solution)/shard_map/ppermute | solution.py:55
  21.0 8.1 %collective-permute-start.4 = (bf16[96,1024]{1,0:T(8,128)(2,1)S(1)}, bf16[96,1024]{1,0:T(8,128)(2,1)S(1)}, u32[]{:S(2)}, u32[]{:S(2)}) collective-permute-start(bf16[96,1024]{1,0:T(8,128)(2,1)S(1)} %collective-permute-done.3), channel_id=1, source_target_pairs={{0,2},{1,3},{2,0},{3,1},{4,6},{5,7},{6,4},{7,5},{8,10},{9,11},{10,... | collective-permute-start | bytes 589832 | tf_op jit(solution)/shard_map/ppermute | solution.py:55
  22.6 8.8 %copy-start = (bf16[384,1024]{1,0:T(8,128)(2,1)}, bf16[384,1024]{1,0:T(8,128)(2,1)S(1)}, u32[]{:S(2)}) copy-start(bf16[384,1024]{1,0:T(8,128)(2,1)S(1)} %pad_maximum_fusion.refs_0_) | copy-start | bytes 2359300
  23.9 22.0 %collective-permute-start.17 = (bf16[384,1024]{1,0:T(8,128)(2,1)S(1)}, bf16[384,1024]{1,0:T(8,128)(2,1)S(1)}, u32[]{:S(2)}, u32[]{:S(2)}) collective-permute-start(bf16[384,1024]{1,0:T(8,128)(2,1)S(1)} %pad_maximum_fusion.refs_0_), channel_id=1, source_target_pairs={{0,1},{1,0},{2,3},{3,2},{4,5},{5,4},{6,7},{7,6},{8,9},{9,8},{10,11... | collective-permute-start | bytes 2359304 | tf_op jit(solution)/shard_map/ppermute | solution.py:55
  24.1 13.4 %collective-permute-start.12 = (bf16[48,1024]{1,0:T(8,128)(2,1)S(1)}, bf16[48,1024]{1,0:T(8,128)(2,1)S(1)}, u32[]{:S(2)}, u32[]{:S(2)}) collective-permute-start(bf16[48,1024]{1,0:T(8,128)(2,1)S(1)} %slice.24), channel_id=1, source_target_pairs={{0,2},{1,3},{2,0},{3,1},{4,6},{5,7},{6,4},{7,5},{8,10},{9,11},{10,... | collective-permute-start | bytes 294920 | tf_op jit(solution)/shard_map/ppermute | solution.py:55
  27.6 8.5 %collective-permute-start.11 = (bf16[48,1024]{1,0:T(8,128)(2,1)S(1)}, bf16[48,1024]{1,0:T(8,128)(2,1)S(1)}, u32[]{:S(2)}, u32[]{:S(2)}) collective-permute-start(bf16[48,1024]{1,0:T(8,128)(2,1)S(1)} %slice.23), channel_id=1, source_target_pairs={{0,4},{1,5},{2,6},{3,7},{4,0},{5,1},{6,2},{7,3},{8,12},{9,13},{10,... | collective-permute-start | bytes 294920 | tf_op jit(solution)/shard_map/ppermute | solution.py:55
  29.1 9.4 %collective-permute-start.7 = (bf16[48,1024]{1,0:T(8,128)(2,1)S(1)}, bf16[48,1024]{1,0:T(8,128)(2,1)S(1)}, u32[]{:S(2)}, u32[]{:S(2)}) collective-permute-start(bf16[48,1024]{1,0:T(8,128)(2,1)S(1)} %slice.22), channel_id=1, source_target_pairs={{0,2},{1,3},{2,0},{3,1},{4,6},{5,7},{6,4},{7,5},{8,10},{9,11},{10,... | collective-permute-start | bytes 294920 | tf_op jit(solution)/shard_map/ppermute | solution.py:55
  30.2 4.7 %collective-permute-start.6 = (bf16[48,1024]{1,0:T(8,128)(2,1)S(1)}, bf16[48,1024]{1,0:T(8,128)(2,1)S(1)}, u32[]{:S(2)}, u32[]{:S(2)}) collective-permute-start(bf16[48,1024]{1,0:T(8,128)(2,1)S(1)} %slice.21), channel_id=1, source_target_pairs={{0,4},{1,5},{2,6},{3,7},{4,0},{5,1},{6,2},{7,3},{8,12},{9,13},{10,... | collective-permute-start | bytes 294920 | tf_op jit(solution)/shard_map/ppermute | solution.py:55
  34.9 10.5 %collective-permute-start.16 = (bf16[96,1024]{1,0:T(8,128)(2,1)S(1)}, bf16[96,1024]{1,0:T(8,128)(2,1)S(1)}, u32[]{:S(2)}, u32[]{:S(2)}) collective-permute-start(bf16[96,1024]{1,0:T(8,128)(2,1)S(1)} %collective-permute-done.13), channel_id=1, source_target_pairs={{0,6},{1,7},{2,4},{3,5},{4,2},{5,3},{6,0},{7,1},{8,14},{9,15},{10,... | collective-permute-start | bytes 589832 | tf_op jit(solution)/shard_map/ppermute | solution.py:55
  36.1 9.2 %collective-permute-start.15 = (bf16[96,1024]{1,0:T(8,128)(2,1)S(1)}, bf16[96,1024]{1,0:T(8,128)(2,1)S(1)}, u32[]{:S(2)}, u32[]{:S(2)}) collective-permute-start(bf16[96,1024]{1,0:T(8,128)(2,1)S(1)} %collective-permute-done.13), channel_id=1, source_target_pairs={{0,4},{1,5},{2,6},{3,7},{4,0},{5,1},{6,2},{7,3},{8,12},{9,13},{10,... | collective-permute-start | bytes 589832 | tf_op jit(solution)/shard_map/ppermute | solution.py:55
  37.5 7.7 %collective-permute-start.14 = (bf16[96,1024]{1,0:T(8,128)(2,1)S(1)}, bf16[96,1024]{1,0:T(8,128)(2,1)S(1)}, u32[]{:S(2)}, u32[]{:S(2)}) collective-permute-start(bf16[96,1024]{1,0:T(8,128)(2,1)S(1)} %collective-permute-done.13), channel_id=1, source_target_pairs={{0,2},{1,3},{2,0},{3,1},{4,6},{5,7},{6,4},{7,5},{8,10},{9,11},{10,... | collective-permute-start | bytes 589832 | tf_op jit(solution)/shard_map/ppermute | solution.py:55
  38.5 10.2 %copy-start.3 = (bf16[384,1024]{1,0:T(8,128)(2,1)}, bf16[384,1024]{1,0:T(8,128)(2,1)S(1)}, u32[]{:S(2)}) copy-start(bf16[384,1024]{1,0:T(8,128)(2,1)S(1)} %constant_dynamic-update-slice_fusion.5.refs_2_) | copy-start | bytes 2359300
  38.5 7.3 %collective-permute-start.19 = (bf16[384,1024]{1,0:T(8,128)(2,1)S(1)}, bf16[384,1024]{1,0:T(8,128)(2,1)S(1)}, u32[]{:S(2)}, u32[]{:S(2)}) collective-permute-start(bf16[384,1024]{1,0:T(8,128)(2,1)S(1)} %constant_dynamic-update-slice_fusion.5.refs_2_), channel_id=1, source_target_pairs={{0,1},{1,0},{2,3},{3,2},{4,5},{5,4},{6,7},{7,6},{8,9},{9,8},{10,11... | collective-permute-start | bytes 2359304 | tf_op jit(solution)/shard_map/ppermute | solution.py:55
  38.6 10.1 %copy-start.1 = (bf16[384,1024]{1,0:T(8,128)(2,1)}, bf16[384,1024]{1,0:T(8,128)(2,1)S(1)}, u32[]{:S(2)}) copy-start(bf16[384,1024]{1,0:T(8,128)(2,1)S(1)} %constant_dynamic-update-slice_fusion.refs_1_) | copy-start | bytes 2359300
  45.2 2.3 %collective-permute-start.18 = (bf16[384,1024]{1,0:T(8,128)(2,1)S(1)}, bf16[384,1024]{1,0:T(8,128)(2,1)S(1)}, u32[]{:S(2)}, u32[]{:S(2)}) collective-permute-start(bf16[384,1024]{1,0:T(8,128)(2,1)S(1)} %constant_dynamic-update-slice_fusion.refs_1_), channel_id=1, source_target_pairs={{0,1},{1,0},{2,3},{3,2},{4,5},{5,4},{6,7},{7,6},{8,9},{9,8},{10,11... | collective-permute-start | bytes 2359304 | tf_op jit(solution)/shard_map/ppermute | solution.py:55
  45.4 3.4 %copy-start.2 = (bf16[384,1024]{1,0:T(8,128)(2,1)}, bf16[384,1024]{1,0:T(8,128)(2,1)S(1)}, u32[]{:S(2)}) copy-start(bf16[384,1024]{1,0:T(8,128)(2,1)S(1)} %constant_dynamic-update-slice_fusion.10.refs_3_) | copy-start | bytes 2359300
  45.4 3.3 %collective-permute-start.20 = (bf16[384,1024]{1,0:T(8,128)(2,1)S(1)}, bf16[384,1024]{1,0:T(8,128)(2,1)}, u32[]{:S(2)}, u32[]{:S(2)}) collective-permute-start(bf16[384,1024]{1,0:T(8,128)(2,1)S(1)} %constant_dynamic-update-slice_fusion.10.refs_3_), channel_id=1, source_target_pairs={{0,1},{1,0},{2,3},{3,2},{4,5},{5,4},{6,7},{7,6},{8,9},{9,8},{10,11... | collective-permute-start | bytes 2359304 | tf_op jit(solution)/shard_map/ppermute | solution.py:55
  45.9 2.9 %copy-start.4 = (bf16[384,1024]{1,0:T(8,128)(2,1)}, bf16[384,1024]{1,0:T(8,128)(2,1)S(1)}, u32[]{:S(2)}) copy-start(bf16[384,1024]{1,0:T(8,128)(2,1)S(1)} %collective-permute-done.17.refs_4_) | copy-start | bytes 2359300
  45.9 1.6 %copy-start.5 = (bf16[384,1024]{1,0:T(8,128)(2,1)}, bf16[384,1024]{1,0:T(8,128)(2,1)S(1)}, u32[]{:S(2)}) copy-start(bf16[384,1024]{1,0:T(8,128)(2,1)S(1)} %collective-permute-done.19.refs_6_) | copy-start | bytes 2359300
  47.5 0.9 copy-start.6

commit v7 on v6

--- a/solution.py
+++ b/solution.py
@@ -19,7 +19,7 @@
 LANES = 128
 TILE = 256
 PACK = 16
-CHUNK = 512
+CHUNK = 1024
 REST = 256
 VMEM_BYTES = 60 << 20
 EXACT = lax.Precision.HIGHEST
@@ -79,14 +79,24 @@
     return block[:, :1].astype(jnp.float32) < DEAD_ABOVE
 
 
+def chunk_plan(rows):
+    parts = pl.cdiv(rows, REST)
+    whole = (parts + 1) // (CHUNK // REST)
+    return parts, whole, parts - whole * (CHUNK // REST)
+
+
 def over_chunks(rows, body):
-    whole = (rows + (CHUNK - REST - 1)) // CHUNK
+    _, whole, left = chunk_plan(rows)
 
     @pl.loop(0, whole)
     def _(index):
         body(pl.multiple_of(index * CHUNK, CHUNK), CHUNK)
 
-    @pl.when(whole * CHUNK < rows)
+    @pl.when(left == 2)
+    def _():
+        body(pl.multiple_of(whole * CHUNK, CHUNK), 2 * REST)
+
+    @pl.when(left == 1)
     def _():
         body(pl.multiple_of(whole * CHUNK, CHUNK), REST)
 
@@ -135,7 +145,10 @@
 
     rows, count = lax.fori_loop(0, blocks, move_block, (jnp.int32(0), jnp.int32(0)))
 
-    @pl.loop(rows // PACK, pl.cdiv(rows, REST) * (REST // PACK))
+    parts, whole, _ = chunk_plan(rows)
+    filled = jnp.maximum(parts * REST, whole * CHUNK)
+
+    @pl.loop(rows // PACK, filled // PACK)
     def _(tile):
         target = pl.multiple_of(tile * PACK, PACK)
         keys[pl.ds(target, PACK), :] = jnp.full((PACK, keys.shape[1]), DEAD, keys.dtype)
@@ -189,7 +202,9 @@
                 part += product(low[:, here], high[:, upto], 0, 0)
                 work[here, upto] += part
 
-        over_chunks(rows, add_centred)
+        @pl.loop(0, pl.cdiv(rows, REST))
+        def _(index):
+            add_centred(pl.multiple_of(index * REST, REST), REST)
 
     for here, upto in spans:
         shape = (TILE, upto.stop)

time: 116 us -> 115 us (level)
  Pallas kernels: 66.9 us -> 65.6 us
    pallas_call x1, Pallas kernels: 66.9 us -> 65.6 us  [local_call(): pl.pallas_call(functools.partial(local_kernel, len(groups)), out_shape=[j...]
where the time goes in v7:
time: 115 us
  Pallas kernels  65.6 us (57%)
  starting transfers between devices  25.7 us (22%)
  waiting for transfers between devices  19.3 us (17%)
  between operations  1.67 us (1%)
    pallas_call x1, Pallas kernels, local_call(): pl.pallas_call(functools.partial(local_kernel, len(groups)), out_shape=[j...  65.6 us
    ppermute x21, starting transfers between devices, flipped(): lax.ppermute(value, 'dev', [(source, source ^ mask) for source in range(s...  25.7 us
    ppermute x21, waiting for transfers between devices, flipped(): lax.ppermute(value, 'dev', [(source, source ^ mask) for source in range(s...  19.3 us
  transfers between devices with their start and end apart: 21, of which 12 were waited for; matrix products, arithmetic and copies ran while one was open for 0% of the time, Pallas kernels for 0%

profile of v7, /device:TPU:0, one launch (start us, length us, event | category | flops | bytes accessed | tf_op | source)
XLA Modules:
  0.0 114.5 jit_solution(16412044422438321436)
XLA Ops:
  1.3 1.0 fusion
  2.3 3.1 %collective-permute-start.8 = (bf16[96,1024]{1,0:T(8,128)(2,1)S(1)}, bf16[96,1024]{1,0:T(8,128)(2,1)S(1)}, u32[]{:S(2)}, u32[]{:S(2)}) collective-permute-start(bf16[96,1024]{1,0:T(8,128)(2,1)S(1)} %fusion), channel_id=1, source_target_pairs={{0,8},{1,9},{2,10},{3,11},{4,12},{5,13},{6,14},{7,15},{8,0},{9,1},... | collective-permute-start | bytes 589832 | tf_op jit(solution)/shard_map/ppermute | solution.py:55
  5.4 2.6 %collective-permute-start.3 = (bf16[96,1024]{1,0:T(8,128)(2,1)S(1)}, bf16[96,1024]{1,0:T(8,128)(2,1)S(1)}, u32[]{:S(2)}, u32[]{:S(2)}) collective-permute-start(bf16[96,1024]{1,0:T(8,128)(2,1)S(1)} %fusion), channel_id=1, source_target_pairs={{0,16},{1,17},{2,18},{3,19},{4,20},{5,21},{6,22},{7,23},{8,24},{9,... | collective-permute-start | bytes 589832 | tf_op jit(solution)/shard_map/ppermute | solution.py:55
  8.0 2.4 %collective-permute-start.2 = (bf16[96,1024]{1,0:T(8,128)(2,1)S(1)}, bf16[96,1024]{1,0:T(8,128)(2,1)S(1)}, u32[]{:S(2)}, u32[]{:S(2)}) collective-permute-start(bf16[96,1024]{1,0:T(8,128)(2,1)S(1)} %fusion), channel_id=1, source_target_pairs={{0,6},{1,7},{2,4},{3,5},{4,2},{5,3},{6,0},{7,1},{8,14},{9,15},{10,... | collective-permute-start | bytes 589832 | tf_op jit(solution)/shard_map/ppermute | solution.py:55
  10.4 0.5 collective-permute-start.1
  10.9 0.5 collective-permute-start
  11.5 2.9 %collective-permute-done.8 = bf16[96,1024]{1,0:T(8,128)(2,1)S(1)} collective-permute-done((bf16[96,1024]{1,0:T(8,128)(2,1)S(1)}, bf16[96,1024]{1,0:T(8,128)(2,1)S(1)}, u32[]{:S(2)}, u32[]{:S(2)}) %collective-permute-start.8) | collective-permute-done | bytes 196640 | tf_op jit(solution)/shard_map/ppermute | solution.py:55
  14.4 1.7 %collective-permute-start.10 = (bf16[96,1024]{1,0:T(8,128)(2,1)S(1)}, bf16[96,1024]{1,0:T(8,128)(2,1)S(1)}, u32[]{:S(2)}, u32[]{:S(2)}) collective-permute-start(bf16[96,1024]{1,0:T(8,128)(2,1)S(1)} %collective-permute-done.8), channel_id=1, source_target_pairs={{0,4},{1,5},{2,6},{3,7},{4,0},{5,1},{6,2},{7,3},{8,12},{9,13},{10,... | collective-permute-start | bytes 589832 | tf_op jit(solution)/shard_map/ppermute | solution.py:55
  16.1 0.8 collective-permute-done.3
  16.9 1.5 %collective-permute-start.9 = (bf16[96,1024]{1,0:T(8,128)(2,1)S(1)}, bf16[96,1024]{1,0:T(8,128)(2,1)S(1)}, u32[]{:S(2)}, u32[]{:S(2)}) collective-permute-start(bf16[96,1024]{1,0:T(8,128)(2,1)S(1)} %collective-permute-done.8), channel_id=1, source_target_pairs={{0,2},{1,3},{2,0},{3,1},{4,6},{5,7},{6,4},{7,5},{8,10},{9,11},{10,... | collective-permute-start | bytes 589832 | tf_op jit(solution)/shard_map/ppermute | solution.py:55
  18.4 0.0 collective-permute-done.2
  18.4 0.5 collective-permute-start.13
  19.0 0.7 collective-permute-done.1
  19.6 1.2 %collective-permute-start.5 = (bf16[96,1024]{1,0:T(8,128)(2,1)S(1)}, bf16[96,1024]{1,0:T(8,128)(2,1)S(1)}, u32[]{:S(2)}, u32[]{:S(2)}) collective-permute-start(bf16[96,1024]{1,0:T(8,128)(2,1)S(1)} %collective-permute-done.3), channel_id=1, source_target_pairs={{0,4},{1,5},{2,6},{3,7},{4,0},{5,1},{6,2},{7,3},{8,12},{9,13},{10,... | collective-permute-start | bytes 589832 | tf_op jit(solution)/shard_map/ppermute | solution.py:55
  20.8 0.2 collective-permute-done
  21.0 1.4 %collective-permute-start.4 = (bf16[96,1024]{1,0:T(8,128)(2,1)S(1)}, bf16[96,1024]{1,0:T(8,128)(2,1)S(1)}, u32[]{:S(2)}, u32[]{:S(2)}) collective-permute-start(bf16[96,1024]{1,0:T(8,128)(2,1)S(1)} %collective-permute-done.3), channel_id=1, source_target_pairs={{0,2},{1,3},{2,0},{3,1},{4,6},{5,7},{6,4},{7,5},{8,10},{9,11},{10,... | collective-permute-start | bytes 589832 | tf_op jit(solution)/shard_map/ppermute | solution.py:55
  22.5 0.1 pad_maximum_fusion.refs_0_
  22.6 1.3 %collective-permute-done.10 = bf16[96,1024]{1,0:T(8,128)(2,1)S(1)} collective-permute-done((bf16[96,1024]{1,0:T(8,128)(2,1)S(1)}, bf16[96,1024]{1,0:T(8,128)(2,1)S(1)}, u32[]{:S(2)}, u32[]{:S(2)}) %collective-permute-start.10) | collective-permute-done | bytes 196640 | tf_op jit(solution)/shard_map/ppermute | solution.py:55
  23.9 0.0 collective-permute-start.17
  23.9 0.2 collective-permute-done.9
  24.1 2.5 %collective-permute-start.12 = (bf16[48,1024]{1,0:T(8,128)(2,1)S(1)}, bf16[48,1024]{1,0:T(8,128)(2,1)S(1)}, u32[]{:S(2)}, u32[]{:S(2)}) collective-permute-start(bf16[48,1024]{1,0:T(8,128)(2,1)S(1)} %slice.24), channel_id=1, source_target_pairs={{0,2},{1,3},{2,0},{3,1},{4,6},{5,7},{6,4},{7,5},{8,10},{9,11},{10,... | collective-permute-start | bytes 294920 | tf_op jit(solution)/shard_map/ppermute | solution.py:55
  26.6 1.0 collective-permute-done.5
  27.6 1.5 %collective-permute-start.11 = (bf16[48,1024]{1,0:T(8,128)(2,1)S(1)}, bf16[48,1024]{1,0:T(8,128)(2,1)S(1)}, u32[]{:S(2)}, u32[]{:S(2)}) collective-permute-start(bf16[48,1024]{1,0:T(8,128)(2,1)S(1)} %slice.23), channel_id=1, source_target_pairs={{0,4},{1,5},{2,6},{3,7},{4,0},{5,1},{6,2},{7,3},{8,12},{9,13},{10,... | collective-permute-start | bytes 294920 | tf_op jit(solution)/shard_map/ppermute | solution.py:55
  29.1 0.0 collective-permute-done.4
  29.1 1.0 collective-permute-start.7
  30.2 0.0 collective-permute-done.13
  30.2 1.1 collective-permute-start.6
  31.4 3.5 %collective-permute-done.6 = bf16[48,1024]{1,0:T(8,128)(2,1)S(1)} collective-permute-done((bf16[48,1024]{1,0:T(8,128)(2,1)S(1)}, bf16[48,1024]{1,0:T(8,128)(2,1)S(1)}, u32[]{:S(2)}, u32[]{:S(2)}) %collective-permute-start.6) | collective-permute-done | bytes 98336 | tf_op jit(solution)/shard_map/ppermute | solution.py:55
  34.9 1.2 %collective-permute-start.16 = (bf16[96,1024]{1,0:T(8,128)(2,1)S(1)}, bf16[96,1024]{1,0:T(8,128)(2,1)S(1)}, u32[]{:S(2)}, u32[]{:S(2)}) collective-permute-start(bf16[96,1024]{1,0:T(8,128)(2,1)S(1)} %collective-permute-done.13), channel_id=1, source_target_pairs={{0,6},{1,7},{2,4},{3,5},{4,2},{5,3},{6,0},{7,1},{8,14},{9,15},{10,... | collective-permute-start | bytes 589832 | tf_op jit(solution)/shard_map/ppermute | solution.py:55
  36.1 0.0 collective-permute-done.11
  36.1 1.4 %collective-permute-start.15 = (bf16[96,1024]{1,0:T(8,128)(2,1)S(1)}, bf16[96,1024]{1,0:T(8,128)(2,1)S(1)}, u32[]{:S(2)}, u32[]{:S(2)}) collective-permute-start(bf16[96,1024]{1,0:T(8,128)(2,1)S(1)} %collective-permute-done.13), channel_id=1, source_target_pairs={{0,4},{1,5},{2,6},{3,7},{4,0},{5,1},{6,2},{7,3},{8,12},{9,13},{10,... | collective-permute-start | bytes 589832 | tf_op jit(solution)/shard_map/ppermute | solution.py:55
  37.5 0.0 collective-permute-done.12
  37.5 1.0 collective-permute-start.14
  38.5 0.0 collective-permute-done.7
  38.5 0.1 collective-permute-start.19
  38.6 6.5 %collective-permute-done.14 = bf16[96,1024]{1,0:T(8,128)(2,1)S(1)} collective-permute-done((bf16[96,1024]{1,0:T(8,128)(2,1)S(1)}, bf16[96,1024]{1,0:T(8,128)(2,1)S(1)}, u32[]{:S(2)}, u32[]{:S(2)}) %collective-permute-start.14) | collective-permute-done | bytes 196640 | tf_op jit(solution)/shard_map/ppermute | solution.py:55
  45.2 0.0 collective-permute-start.18
  45.2 0.1 collective-permute-done.15
  45.3 0.0 collective-permute-done.16
  45.4 0.5 collective-permute-start.20
  45.9 0.0 collective-permute-done.17.refs_4_
  45.9 0.0 collective-permute-done.19.refs_6_
  45.9 1.6 %collective-permute-done.18.refs_5_ = bf16[384,1024]{1,0:T(8,128)(2,1)S(1)} collective-permute-done((bf16[384,1024]{1,0:T(8,128)(2,1)S(1)}, bf16[384,1024]{1,0:T(8,128)(2,1)S(1)}, u32[]{:S(2)}, u32[]{:S(2)}) %collective-permute-start.18) | collective-permute-done | bytes 786464 | tf_op jit(solution)/shard_map/ppermute | solution.py:55
  47.5 0.0 copy-done.5
  47.5 0.9 copy-done.6
  48.4 0.4 collective-permute-done.20.refs_7_
  48.7 0.0 copy-done.2
  48.7 65.6 %shard_map.41 = (f32[1,128]{1,0:T(1,128)}, bf16[128,1024]{1,0:T(8,128)(2,1)}) custom-call(s32[1]{0:T(128)} %copy.15.size_ref, bf16[128,1024]{1,0:T(8,128)(2,1)} %own_ref.1, bf16[384,1024]{1,0:T(8,128)(2,1)} %copy-done, bf16[384,1024]{1,0:T(8,128)(2,1)} %copy-done.1, bf16[384,1024]{1,0:T(8,128)(2,1)} %copy-done.3, bf16[384,1024]{1,0:T(8,128)(2,1)} %copy-done.2, ...), custom_call_target="tpu_custom_call" | custom-call | tf_op jit(solution)/shard_map/pallas_call | solution.py:454
  (30 shorter events, 0.2 us)
Async XLA Ops:
  2.3 12.1 %collective-permute-start.8 = (bf16[96,1024]{1,0:T(8,128)(2,1)S(1)}, bf16[96,1024]{1,0:T(8,128)(2,1)S(1)}, u32[]{:S(2)}, u32[]{:S(2)}) collective-permute-start(bf16[96,1024]{1,0:T(8,128)(2,1)S(1)} %fusion), channel_id=1, source_target_pairs={{0,8},{1,9},{2,10},{3,11},{4,12},{5,13},{6,14},{7,15},{8,0},{9,1},... | collective-permute-start | bytes 589832 | tf_op jit(solution)/shard_map/ppermute | solution.py:55
  5.4 11.5 %collective-permute-start.3 = (bf16[96,1024]{1,0:T(8,128)(2,1)S(1)}, bf16[96,1024]{1,0:T(8,128)(2,1)S(1)}, u32[]{:S(2)}, u32[]{:S(2)}) collective-permute-start(bf16[96,1024]{1,0:T(8,128)(2,1)S(1)} %fusion), channel_id=1, source_target_pairs={{0,16},{1,17},{2,18},{3,19},{4,20},{5,21},{6,22},{7,23},{8,24},{9,... | collective-permute-start | bytes 589832 | tf_op jit(solution)/shard_map/ppermute | solution.py:55
  8.0 10.4 %collective-permute-start.2 = (bf16[96,1024]{1,0:T(8,128)(2,1)S(1)}, bf16[96,1024]{1,0:T(8,128)(2,1)S(1)}, u32[]{:S(2)}, u32[]{:S(2)}) collective-permute-start(bf16[96,1024]{1,0:T(8,128)(2,1)S(1)} %fusion), channel_id=1, source_target_pairs={{0,6},{1,7},{2,4},{3,5},{4,2},{5,3},{6,0},{7,1},{8,14},{9,15},{10,... | collective-permute-start | bytes 589832 | tf_op jit(solution)/shard_map/ppermute | solution.py:55
  10.4 9.2 %collective-permute-start.1 = (bf16[96,1024]{1,0:T(8,128)(2,1)S(1)}, bf16[96,1024]{1,0:T(8,128)(2,1)S(1)}, u32[]{:S(2)}, u32[]{:S(2)}) collective-permute-start(bf16[96,1024]{1,0:T(8,128)(2,1)S(1)} %fusion), channel_id=1, source_target_pairs={{0,4},{1,5},{2,6},{3,7},{4,0},{5,1},{6,2},{7,3},{8,12},{9,13},{10,... | collective-permute-start | bytes 589832 | tf_op jit(solution)/shard_map/ppermute | solution.py:55
  10.9 10.1 %collective-permute-start = (bf16[96,1024]{1,0:T(8,128)(2,1)S(1)}, bf16[96,1024]{1,0:T(8,128)(2,1)S(1)}, u32[]{:S(2)}, u32[]{:S(2)}) collective-permute-start(bf16[96,1024]{1,0:T(8,128)(2,1)S(1)} %fusion), channel_id=1, source_target_pairs={{0,2},{1,3},{2,0},{3,1},{4,6},{5,7},{6,4},{7,5},{8,10},{9,11},{10,... | collective-permute-start | bytes 589832 | tf_op jit(solution)/shard_map/ppermute | solution.py:55
  14.4 9.5 %collective-permute-start.10 = (bf16[96,1024]{1,0:T(8,128)(2,1)S(1)}, bf16[96,1024]{1,0:T(8,128)(2,1)S(1)}, u32[]{:S(2)}, u32[]{:S(2)}) collective-permute-start(bf16[96,1024]{1,0:T(8,128)(2,1)S(1)} %collective-permute-done.8), channel_id=1, source_target_pairs={{0,4},{1,5},{2,6},{3,7},{4,0},{5,1},{6,2},{7,3},{8,12},{9,13},{10,... | collective-permute-start | bytes 589832 | tf_op jit(solution)/shard_map/ppermute | solution.py:55
  16.9 7.2 %collective-permute-start.9 = (bf16[96,1024]{1,0:T(8,128)(2,1)S(1)}, bf16[96,1024]{1,0:T(8,128)(2,1)S(1)}, u32[]{:S(2)}, u32[]{:S(2)}) collective-permute-start(bf16[96,1024]{1,0:T(8,128)(2,1)S(1)} %collective-permute-done.8), channel_id=1, source_target_pairs={{0,2},{1,3},{2,0},{3,1},{4,6},{5,7},{6,4},{7,5},{8,10},{9,11},{10,... | collective-permute-start | bytes 589832 | tf_op jit(solution)/shard_map/ppermute | solution.py:55
  18.4 11.7 %collective-permute-start.13 = (bf16[96,1024]{1,0:T(8,128)(2,1)S(1)}, bf16[96,1024]{1,0:T(8,128)(2,1)S(1)}, u32[]{:S(2)}, u32[]{:S(2)}) collective-permute-start(bf16[96,1024]{1,0:T(8,128)(2,1)S(1)} %collective-permute-done.3), channel_id=1, source_target_pairs={{0,8},{1,9},{2,10},{3,11},{4,12},{5,13},{6,14},{7,15},{8,0},{9,1},... | collective-permute-start | bytes 589832 | tf_op jit(solution)/shard_map/ppermute | solution.py:55
  19.6 8.0 %collective-permute-start.5 = (bf16[96,1024]{1,0:T(8,128)(2,1)S(1)}, bf16[96,1024]{1,0:T(8,128)(2,1)S(1)}, u32[]{:S(2)}, u32[]{:S(2)}) collective-permute-start(bf16[96,1024]{1,0:T(8,128)(2,1)S(1)} %collective-permute-done.3), channel_id=1, source_target_pairs={{0,4},{1,5},{2,6},{3,7},{4,0},{5,1},{6,2},{7,3},{8,12},{9,13},{10,... | collective-permute-start | bytes 589832 | tf_op jit(solution)/shard_map/ppermute | solution.py:55
  21.0 8.1 %collective-permute-start.4 = (bf16[96,1024]{1,0:T(8,128)(2,1)S(1)}, bf16[96,1024]{1,0:T(8,128)(2,1)S(1)}, u32[]{:S(2)}, u32[]{:S(2)}) collective-permute-start(bf16[96,1024]{1,0:T(8,128)(2,1)S(1)} %collective-permute-done.3), channel_id=1, source_target_pairs={{0,2},{1,3},{2,0},{3,1},{4,6},{5,7},{6,4},{7,5},{8,10},{9,11},{10,... | collective-permute-start | bytes 589832 | tf_op jit(solution)/shard_map/ppermute | solution.py:55
  22.6 8.8 %copy-start = (bf16[384,1024]{1,0:T(8,128)(2,1)}, bf16[384,1024]{1,0:T(8,128)(2,1)S(1)}, u32[]{:S(2)}) copy-start(bf16[384,1024]{1,0:T(8,128)(2,1)S(1)} %pad_maximum_fusion.refs_0_) | copy-start | bytes 2359300
  23.9 22.0 %collective-permute-start.17 = (bf16[384,1024]{1,0:T(8,128)(2,1)S(1)}, bf16[384,1024]{1,0:T(8,128)(2,1)S(1)}, u32[]{:S(2)}, u32[]{:S(2)}) collective-permute-start(bf16[384,1024]{1,0:T(8,128)(2,1)S(1)} %pad_maximum_fusion.refs_0_), channel_id=1, source_target_pairs={{0,1},{1,0},{2,3},{3,2},{4,5},{5,4},{6,7},{7,6},{8,9},{9,8},{10,11... | collective-permute-start | bytes 2359304 | tf_op jit(solution)/shard_map/ppermute | solution.py:55
  24.1 13.4 %collective-permute-start.12 = (bf16[48,1024]{1,0:T(8,128)(2,1)S(1)}, bf16[48,1024]{1,0:T(8,128)(2,1)S(1)}, u32[]{:S(2)}, u32[]{:S(2)}) collective-permute-start(bf16[48,1024]{1,0:T(8,128)(2,1)S(1)} %slice.24), channel_id=1, source_target_pairs={{0,2},{1,3},{2,0},{3,1},{4,6},{5,7},{6,4},{7,5},{8,10},{9,11},{10,... | collective-permute-start | bytes 294920 | tf_op jit(solution)/shard_map/ppermute | solution.py:55
  27.6 8.5 %collective-permute-start.11 = (bf16[48,1024]{1,0:T(8,128)(2,1)S(1)}, bf16[48,1024]{1,0:T(8,128)(2,1)S(1)}, u32[]{:S(2)}, u32[]{:S(2)}) collective-permute-start(bf16[48,1024]{1,0:T(8,128)(2,1)S(1)} %slice.23), channel_id=1, source_target_pairs={{0,4},{1,5},{2,6},{3,7},{4,0},{5,1},{6,2},{7,3},{8,12},{9,13},{10,... | collective-permute-start | bytes 294920 | tf_op jit(solution)/shard_map/ppermute | solution.py:55
  29.1 9.4 %collective-permute-start.7 = (bf16[48,1024]{1,0:T(8,128)(2,1)S(1)}, bf16[48,1024]{1,0:T(8,128)(2,1)S(1)}, u32[]{:S(2)}, u32[]{:S(2)}) collective-permute-start(bf16[48,1024]{1,0:T(8,128)(2,1)S(1)} %slice.22), channel_id=1, source_target_pairs={{0,2},{1,3},{2,0},{3,1},{4,6},{5,7},{6,4},{7,5},{8,10},{9,11},{10,... | collective-permute-start | bytes 294920 | tf_op jit(solution)/shard_map/ppermute | solution.py:55
  30.2 4.7 %collective-permute-start.6 = (bf16[48,1024]{1,0:T(8,128)(2,1)S(1)}, bf16[48,1024]{1,0:T(8,128)(2,1)S(1)}, u32[]{:S(2)}, u32[]{:S(2)}) collective-permute-start(bf16[48,1024]{1,0:T(8,128)(2,1)S(1)} %slice.21), channel_id=1, source_target_pairs={{0,4},{1,5},{2,6},{3,7},{4,0},{5,1},{6,2},{7,3},{8,12},{9,13},{10,... | collective-permute-start | bytes 294920 | tf_op jit(solution)/shard_map/ppermute | solution.py:55
  34.9 10.5 %collective-permute-start.16 = (bf16[96,1024]{1,0:T(8,128)(2,1)S(1)}, bf16[96,1024]{1,0:T(8,128)(2,1)S(1)}, u32[]{:S(2)}, u32[]{:S(2)}) collective-permute-start(bf16[96,1024]{1,0:T(8,128)(2,1)S(1)} %collective-permute-done.13), channel_id=1, source_target_pairs={{0,6},{1,7},{2,4},{3,5},{4,2},{5,3},{6,0},{7,1},{8,14},{9,15},{10,... | collective-permute-start | bytes 589832 | tf_op jit(solution)/shard_map/ppermute | solution.py:55
  36.1 9.2 %collective-permute-start.15 = (bf16[96,1024]{1,0:T(8,128)(2,1)S(1)}, bf16[96,1024]{1,0:T(8,128)(2,1)S(1)}, u32[]{:S(2)}, u32[]{:S(2)}) collective-permute-start(bf16[96,1024]{1,0:T(8,128)(2,1)S(1)} %collective-permute-done.13), channel_id=1, source_target_pairs={{0,4},{1,5},{2,6},{3,7},{4,0},{5,1},{6,2},{7,3},{8,12},{9,13},{10,... | collective-permute-start | bytes 589832 | tf_op jit(solution)/shard_map/ppermute | solution.py:55
  37.5 7.7 %collective-permute-start.14 = (bf16[96,1024]{1,0:T(8,128)(2,1)S(1)}, bf16[96,1024]{1,0:T(8,128)(2,1)S(1)}, u32[]{:S(2)}, u32[]{:S(2)}) collective-permute-start(bf16[96,1024]{1,0:T(8,128)(2,1)S(1)} %collective-permute-done.13), channel_id=1, source_target_pairs={{0,2},{1,3},{2,0},{3,1},{4,6},{5,7},{6,4},{7,5},{8,10},{9,11},{10,... | collective-permute-start | bytes 589832 | tf_op jit(solution)/shard_map/ppermute | solution.py:55
  38.5 10.2 %copy-start.3 = (bf16[384,1024]{1,0:T(8,128)(2,1)}, bf16[384,1024]{1,0:T(8,128)(2,1)S(1)}, u32[]{:S(2)}) copy-start(bf16[384,1024]{1,0:T(8,128)(2,1)S(1)} %constant_dynamic-update-slice_fusion.5.refs_2_) | copy-start | bytes 2359300
  38.5 7.3 %collective-permute-start.19 = (bf16[384,1024]{1,0:T(8,128)(2,1)S(1)}, bf16[384,1024]{1,0:T(8,128)(2,1)S(1)}, u32[]{:S(2)}, u32[]{:S(2)}) collective-permute-start(bf16[384,1024]{1,0:T(8,128)(2,1)S(1)} %constant_dynamic-update-slice_fusion.5.refs_2_), channel_id=1, source_target_pairs={{0,1},{1,0},{2,3},{3,2},{4,5},{5,4},{6,7},{7,6},{8,9},{9,8},{10,11... | collective-permute-start | bytes 2359304 | tf_op jit(solution)/shard_map/ppermute | solution.py:55
  38.6 10.1 %copy-start.1 = (bf16[384,1024]{1,0:T(8,128)(2,1)}, bf16[384,1024]{1,0:T(8,128)(2,1)S(1)}, u32[]{:S(2)}) copy-start(bf16[384,1024]{1,0:T(8,128)(2,1)S(1)} %constant_dynamic-update-slice_fusion.refs_1_) | copy-start | bytes 2359300
  45.2 2.3 %collective-permute-start.18 = (bf16[384,1024]{1,0:T(8,128)(2,1)S(1)}, bf16[384,1024]{1,0:T(8,128)(2,1)S(1)}, u32[]{:S(2)}, u32[]{:S(2)}) collective-permute-start(bf16[384,1024]{1,0:T(8,128)(2,1)S(1)} %constant_dynamic-update-slice_fusion.refs_1_), channel_id=1, source_target_pairs={{0,1},{1,0},{2,3},{3,2},{4,5},{5,4},{6,7},{7,6},{8,9},{9,8},{10,11... | collective-permute-start | bytes 2359304 | tf_op jit(solution)/shard_map/ppermute | solution.py:55
  45.4 3.4 %copy-start.2 = (bf16[384,1024]{1,0:T(8,128)(2,1)}, bf16[384,1024]{1,0:T(8,128)(2,1)S(1)}, u32[]{:S(2)}) copy-start(bf16[384,1024]{1,0:T(8,128)(2,1)S(1)} %constant_dynamic-update-slice_fusion.10.refs_3_) | copy-start | bytes 2359300
  45.4 3.3 %collective-permute-start.20 = (bf16[384,1024]{1,0:T(8,128)(2,1)S(1)}, bf16[384,1024]{1,0:T(8,128)(2,1)}, u32[]{:S(2)}, u32[]{:S(2)}) collective-permute-start(bf16[384,1024]{1,0:T(8,128)(2,1)S(1)} %constant_dynamic-update-slice_fusion.10.refs_3_), channel_id=1, source_target_pairs={{0,1},{1,0},{2,3},{3,2},{4,5},{5,4},{6,7},{7,6},{8,9},{9,8},{10,11... | collective-permute-start | bytes 2359304 | tf_op jit(solution)/shard_map/ppermute | solution.py:55
  45.9 2.9 %copy-start.4 = (bf16[384,1024]{1,0:T(8,128)(2,1)}, bf16[384,1024]{1,0:T(8,128)(2,1)S(1)}, u32[]{:S(2)}) copy-start(bf16[384,1024]{1,0:T(8,128)(2,1)S(1)} %collective-permute-done.17.refs_4_) | copy-start | bytes 2359300
  45.9 1.6 %copy-start.5 = (bf16[384,1024]{1,0:T(8,128)(2,1)}, bf16[384,1024]{1,0:T(8,128)(2,1)S(1)}, u32[]{:S(2)}) copy-start(bf16[384,1024]{1,0:T(8,128)(2,1)S(1)} %collective-permute-done.19.refs_6_) | copy-start | bytes 2359300
  47.5 0.9 copy-start.6

commit v8 on v7

--- a/solution.py
+++ b/solution.py
@@ -69,9 +69,10 @@
     across, beside = flipped(rows, far), flipped(rows, near)
     groups = [rows, across, beside, flipped(across, near)]
     same_core = [
-        jnp.concatenate(plane_of(group, near, place in (0, 3)), axis=0)
-        for place, group in enumerate(groups)
+        jnp.concatenate(plane_of(group, near, place == 0), axis=0)
+        for place, group in enumerate(groups[:3])
     ]
+    same_core += plane_of(groups[3], near, True)
     return same_core + [flipped(group, 1) for group in same_core]
 
 

time: 115 us -> 119 us (1.035)
  waiting for transfers between devices: 19.3 us -> 22.8 us
    ppermute x21 -> x24, waiting for transfers between devices: 19.3 us -> 22.8 us  [flipped(): lax.ppermute(value, 'dev', [(source, source ^ mask) for source in range(s...]
    ppermute x21 -> x24, starting transfers between devices: 25.7 us -> 26 us  [flipped(): lax.ppermute(value, 'dev', [(source, source ^ mask) for source in range(s...]
  transfers between devices with their start and end apart: 21 -> 24, of which waited for: 12 -> 16; matrix products, arithmetic and copies ran while one was open for 0% -> 0% of each run, Pallas kernels for 0% -> 0%
where the time goes in v8:
time: 119 us
  Pallas kernels  65.5 us (55%)
  starting transfers between devices  26 us (22%)
  waiting for transfers between devices  22.8 us (19%)
  between operations  1.7 us (1%)
  local copies, waits for them, and re-layouts  1.67 us (1%)
    pallas_call x1, Pallas kernels, local_call(): pl.pallas_call(functools.partial(local_kernel, len(groups)), out_shape=[j...  65.5 us
    ppermute x24, starting transfers between devices, flipped(): lax.ppermute(value, 'dev', [(source, source ^ mask) for source in range(s...  26 us
    ppermute x24, waiting for transfers between devices, flipped(): lax.ppermute(value, 'dev', [(source, source ^ mask) for source in range(s...  22.8 us
  transfers between devices with their start and end apart: 24, of which 16 were waited for; matrix products, arithmetic and copies ran while one was open for 0% of the time, Pallas kernels for 0%

profile of v8, /device:TPU:0, one launch (start us, length us, event | category | flops | bytes accessed | tf_op | source)
XLA Modules:
  0.0 118.8 jit_solution(5756131756019809375)
XLA Ops:
  1.3 1.0 fusion
  2.3 4.0 %collective-permute-start.2 = (bf16[96,1024]{1,0:T(8,128)(2,1)S(1)}, bf16[96,1024]{1,0:T(8,128)(2,1)S(1)}, u32[]{:S(2)}, u32[]{:S(2)}) collective-permute-start(bf16[96,1024]{1,0:T(8,128)(2,1)S(1)} %fusion), channel_id=1, source_target_pairs={{0,6},{1,7},{2,4},{3,5},{4,2},{5,3},{6,0},{7,1},{8,14},{9,15},{10,... | collective-permute-start | bytes 589832 | tf_op jit(solution)/shard_map/ppermute | solution.py:55
  6.3 0.5 collective-permute-start.1
  6.8 0.1 collective-permute-start
  6.9 2.0 %collective-permute-start.8 = (bf16[96,1024]{1,0:T(8,128)(2,1)S(1)}, bf16[96,1024]{1,0:T(8,128)(2,1)S(1)}, u32[]{:S(2)}, u32[]{:S(2)}) collective-permute-start(bf16[96,1024]{1,0:T(8,128)(2,1)S(1)} %fusion), channel_id=1, source_target_pairs={{0,8},{1,9},{2,10},{3,11},{4,12},{5,13},{6,14},{7,15},{8,0},{9,1},... | collective-permute-start | bytes 589832 | tf_op jit(solution)/shard_map/ppermute | solution.py:55
  8.9 2.6 %collective-permute-start.3 = (bf16[96,1024]{1,0:T(8,128)(2,1)S(1)}, bf16[96,1024]{1,0:T(8,128)(2,1)S(1)}, u32[]{:S(2)}, u32[]{:S(2)}) collective-permute-start(bf16[96,1024]{1,0:T(8,128)(2,1)S(1)} %fusion), channel_id=1, source_target_pairs={{0,16},{1,17},{2,18},{3,19},{4,20},{5,21},{6,22},{7,23},{8,24},{9,... | collective-permute-start | bytes 589832 | tf_op jit(solution)/shard_map/ppermute | solution.py:55
  11.5 0.6 collective-permute-done.2
  12.0 3.3 %collective-permute-done.1 = bf16[96,1024]{1,0:T(8,128)(2,1)S(1)} collective-permute-done((bf16[96,1024]{1,0:T(8,128)(2,1)S(1)}, bf16[96,1024]{1,0:T(8,128)(2,1)S(1)}, u32[]{:S(2)}, u32[]{:S(2)}) %collective-permute-start.1) | collective-permute-done | bytes 196640 | tf_op jit(solution)/shard_map/ppermute | solution.py:55
  15.4 0.3 collective-permute-done
  15.7 0.1 pad_maximum_fusion.refs_0_
  15.7 0.1 collective-permute-start.17
  15.8 1.0 collective-permute-done.8
  16.8 1.8 %collective-permute-start.10 = (bf16[96,1024]{1,0:T(8,128)(2,1)S(1)}, bf16[96,1024]{1,0:T(8,128)(2,1)S(1)}, u32[]{:S(2)}, u32[]{:S(2)}) collective-permute-start(bf16[96,1024]{1,0:T(8,128)(2,1)S(1)} %collective-permute-done.8), channel_id=1, source_target_pairs={{0,4},{1,5},{2,6},{3,7},{4,0},{5,1},{6,2},{7,3},{8,12},{9,13},{10,... | collective-permute-start | bytes 589832 | tf_op jit(solution)/shard_map/ppermute | solution.py:55
  18.6 1.5 %collective-permute-start.9 = (bf16[96,1024]{1,0:T(8,128)(2,1)S(1)}, bf16[96,1024]{1,0:T(8,128)(2,1)S(1)}, u32[]{:S(2)}, u32[]{:S(2)}) collective-permute-start(bf16[96,1024]{1,0:T(8,128)(2,1)S(1)} %collective-permute-done.8), channel_id=1, source_target_pairs={{0,2},{1,3},{2,0},{3,1},{4,6},{5,7},{6,4},{7,5},{8,10},{9,11},{10,... | collective-permute-start | bytes 589832 | tf_op jit(solution)/shard_map/ppermute | solution.py:55
  20.1 1.0 collective-permute-start.5
  21.1 1.5 %collective-permute-start.4 = (bf16[96,1024]{1,0:T(8,128)(2,1)S(1)}, bf16[96,1024]{1,0:T(8,128)(2,1)S(1)}, u32[]{:S(2)}, u32[]{:S(2)}) collective-permute-start(bf16[96,1024]{1,0:T(8,128)(2,1)S(1)} %collective-permute-done.3), channel_id=1, source_target_pairs={{0,2},{1,3},{2,0},{3,1},{4,6},{5,7},{6,4},{7,5},{8,10},{9,11},{10,... | collective-permute-start | bytes 589832 | tf_op jit(solution)/shard_map/ppermute | solution.py:55
  22.6 2.0 %collective-permute-done.10 = bf16[96,1024]{1,0:T(8,128)(2,1)S(1)} collective-permute-done((bf16[96,1024]{1,0:T(8,128)(2,1)S(1)}, bf16[96,1024]{1,0:T(8,128)(2,1)S(1)}, u32[]{:S(2)}, u32[]{:S(2)}) %collective-permute-start.10) | collective-permute-done | bytes 196640 | tf_op jit(solution)/shard_map/ppermute | solution.py:55
  24.6 0.5 collective-permute-start.13
  25.2 1.2 %collective-permute-done.9 = bf16[96,1024]{1,0:T(8,128)(2,1)S(1)} collective-permute-done((bf16[96,1024]{1,0:T(8,128)(2,1)S(1)}, bf16[96,1024]{1,0:T(8,128)(2,1)S(1)}, u32[]{:S(2)}, u32[]{:S(2)}) %collective-permute-start.9) | collective-permute-done | bytes 196640 | tf_op jit(solution)/shard_map/ppermute | solution.py:55
  26.4 0.7 collective-permute-start.12
  27.1 0.3 collective-permute-done.5
  27.3 1.4 %collective-permute-start.11 = (bf16[48,1024]{1,0:T(8,128)(2,1)S(1)}, bf16[48,1024]{1,0:T(8,128)(2,1)S(1)}, u32[]{:S(2)}, u32[]{:S(2)}) collective-permute-start(bf16[48,1024]{1,0:T(8,128)(2,1)S(1)} %slice.23), channel_id=1, source_target_pairs={{0,4},{1,5},{2,6},{3,7},{4,0},{5,1},{6,2},{7,3},{8,12},{9,13},{10,... | collective-permute-start | bytes 294920 | tf_op jit(solution)/shard_map/ppermute | solution.py:55
  28.8 0.8 collective-permute-done.4
  29.6 0.4 collective-permute-start.7
  30.1 0.2 collective-permute-done.13.refs_3_
  30.3 1.8 %collective-permute-start.6 = (bf16[48,1024]{1,0:T(8,128)(2,1)S(1)}, bf16[48,1024]{1,0:T(8,128)(2,1)S(1)}, u32[]{:S(2)}, u32[]{:S(2)}) collective-permute-start(bf16[48,1024]{1,0:T(8,128)(2,1)S(1)} %slice.21), channel_id=1, source_target_pairs={{0,4},{1,5},{2,6},{3,7},{4,0},{5,1},{6,2},{7,3},{8,12},{9,13},{10,... | collective-permute-start | bytes 294920 | tf_op jit(solution)/shard_map/ppermute | solution.py:55
  32.1 0.1 collective-permute-done.11
  32.2 0.0 collective-permute-done.12
  32.2 0.6 collective-permute-start.19
  32.8 2.2 %collective-permute-done.6 = bf16[48,1024]{1,0:T(8,128)(2,1)S(1)} collective-permute-done((bf16[48,1024]{1,0:T(8,128)(2,1)S(1)}, bf16[48,1024]{1,0:T(8,128)(2,1)S(1)}, u32[]{:S(2)}, u32[]{:S(2)}) %collective-permute-start.6) | collective-permute-done | bytes 98336 | tf_op jit(solution)/shard_map/ppermute | solution.py:55
  35.0 0.1 collective-permute-start.18
  35.0 2.2 %collective-permute-start.16 = (bf16[96,1024]{1,0:T(8,128)(2,1)S(1)}, bf16[96,1024]{1,0:T(8,128)(2,1)S(1)}, u32[]{:S(2)}, u32[]{:S(2)}) collective-permute-start(bf16[96,1024]{1,0:T(8,128)(2,1)S(1)} %collective-permute-done.13.refs_3_), channel_id=1, source_target_pairs={{0,6},{1,7},{2,4},{3,5},{4,2},{5,3},{6,0},{7,1},{8,14},{9,15},{10,... | collective-permute-start | bytes 589832 | tf_op jit(solution)/shard_map/ppermute | solution.py:55
  37.3 1.1 collective-permute-start.15
  38.3 5.1 %collective-permute-done.16.refs_6_ = bf16[96,1024]{1,0:T(8,128)(2,1)S(1)} collective-permute-done((bf16[96,1024]{1,0:T(8,128)(2,1)S(1)}, bf16[96,1024]{1,0:T(8,128)(2,1)S(1)}, u32[]{:S(2)}, u32[]{:S(2)}) %collective-permute-start.16) | collective-permute-done | bytes 196640 | tf_op jit(solution)/shard_map/ppermute | solution.py:55
  43.4 1.7 %collective-permute-start.14 = (bf16[96,1024]{1,0:T(8,128)(2,1)S(1)}, bf16[96,1024]{1,0:T(8,128)(2,1)S(1)}, u32[]{:S(2)}, u32[]{:S(2)}) collective-permute-start(bf16[96,1024]{1,0:T(8,128)(2,1)S(1)} %collective-permute-done.13.refs_3_), channel_id=1, source_target_pairs={{0,2},{1,3},{2,0},{3,1},{4,6},{5,7},{6,4},{7,5},{8,10},{9,11},{10,... | collective-permute-start | bytes 589832 | tf_op jit(solution)/shard_map/ppermute | solution.py:55
  45.1 2.4 %collective-permute-done.15.refs_5_ = bf16[96,1024]{1,0:T(8,128)(2,1)S(1)} collective-permute-done((bf16[96,1024]{1,0:T(8,128)(2,1)S(1)}, bf16[96,1024]{1,0:T(8,128)(2,1)S(1)}, u32[]{:S(2)}, u32[]{:S(2)}) %collective-permute-start.15) | collective-permute-done | bytes 196640 | tf_op jit(solution)/shard_map/ppermute | solution.py:55
  47.5 0.0 collective-permute-start.23
  47.5 2.3 %collective-permute-done.14.refs_4_ = bf16[96,1024]{1,0:T(8,128)(2,1)S(1)} collective-permute-done((bf16[96,1024]{1,0:T(8,128)(2,1)S(1)}, bf16[96,1024]{1,0:T(8,128)(2,1)S(1)}, u32[]{:S(2)}, u32[]{:S(2)}) %collective-permute-start.14) | collective-permute-done | bytes 196640 | tf_op jit(solution)/shard_map/ppermute | solution.py:55
  49.8 0.5 collective-permute-start.21
  50.3 0.9 collective-permute-done.22.refs_12_
  51.2 0.3 collective-permute-done.21.refs_11_
  51.5 0.0 collective-permute-done.17.refs_7_
  51.5 0.0 collective-permute-done.19.refs_9_
  51.6 0.3 copy-done.11
  51.9 0.3 copy-done.12
  52.2 0.2 copy-done.3
  52.5 0.6 copy-done.4
  53.1 65.5 %shard_map.41 = (f32[1,128]{1,0:T(1,128)}, bf16[128,1024]{1,0:T(8,128)(2,1)}) custom-call(s32[1]{0:T(128)} %copy.12.size_ref, bf16[128,1024]{1,0:T(8,128)(2,1)} %own_ref.1, bf16[384,1024]{1,0:T(8,128)(2,1)} %copy-done, bf16[384,1024]{1,0:T(8,128)(2,1)} %copy-done.2, bf16[384,1024]{1,0:T(8,128)(2,1)} %copy-done.1, bf16[96,1024]{1,0:T(8,128)(2,1)} %copy-done.5, ...), custom_call_target="tpu_custom_call" | custom-call | tf_op jit(solution)/shard_map/pallas_call | solution.py:455
  (44 shorter events, 0.2 us)
Async XLA Ops:
  2.3 9.7 %collective-permute-start.2 = (bf16[96,1024]{1,0:T(8,128)(2,1)S(1)}, bf16[96,1024]{1,0:T(8,128)(2,1)S(1)}, u32[]{:S(2)}, u32[]{:S(2)}) collective-permute-start(bf16[96,1024]{1,0:T(8,128)(2,1)S(1)} %fusion), channel_id=1, source_target_pairs={{0,6},{1,7},{2,4},{3,5},{4,2},{5,3},{6,0},{7,1},{8,14},{9,15},{10,... | collective-permute-start | bytes 589832 | tf_op jit(solution)/shard_map/ppermute | solution.py:55
  6.3 9.1 %collective-permute-start.1 = (bf16[96,1024]{1,0:T(8,128)(2,1)S(1)}, bf16[96,1024]{1,0:T(8,128)(2,1)S(1)}, u32[]{:S(2)}, u32[]{:S(2)}) collective-permute-start(bf16[96,1024]{1,0:T(8,128)(2,1)S(1)} %fusion), channel_id=1, source_target_pairs={{0,4},{1,5},{2,6},{3,7},{4,0},{5,1},{6,2},{7,3},{8,12},{9,13},{10,... | collective-permute-start | bytes 589832 | tf_op jit(solution)/shard_map/ppermute | solution.py:55
  6.8 8.9 %collective-permute-start = (bf16[96,1024]{1,0:T(8,128)(2,1)S(1)}, bf16[96,1024]{1,0:T(8,128)(2,1)S(1)}, u32[]{:S(2)}, u32[]{:S(2)}) collective-permute-start(bf16[96,1024]{1,0:T(8,128)(2,1)S(1)} %fusion), channel_id=1, source_target_pairs={{0,2},{1,3},{2,0},{3,1},{4,6},{5,7},{6,4},{7,5},{8,10},{9,11},{10,... | collective-permute-start | bytes 589832 | tf_op jit(solution)/shard_map/ppermute | solution.py:55
  6.9 9.9 %collective-permute-start.8 = (bf16[96,1024]{1,0:T(8,128)(2,1)S(1)}, bf16[96,1024]{1,0:T(8,128)(2,1)S(1)}, u32[]{:S(2)}, u32[]{:S(2)}) collective-permute-start(bf16[96,1024]{1,0:T(8,128)(2,1)S(1)} %fusion), channel_id=1, source_target_pairs={{0,8},{1,9},{2,10},{3,11},{4,12},{5,13},{6,14},{7,15},{8,0},{9,1},... | collective-permute-start | bytes 589832 | tf_op jit(solution)/shard_map/ppermute | solution.py:55
  8.9 11.2 %collective-permute-start.3 = (bf16[96,1024]{1,0:T(8,128)(2,1)S(1)}, bf16[96,1024]{1,0:T(8,128)(2,1)S(1)}, u32[]{:S(2)}, u32[]{:S(2)}) collective-permute-start(bf16[96,1024]{1,0:T(8,128)(2,1)S(1)} %fusion), channel_id=1, source_target_pairs={{0,16},{1,17},{2,18},{3,19},{4,20},{5,21},{6,22},{7,23},{8,24},{9,... | collective-permute-start | bytes 589832 | tf_op jit(solution)/shard_map/ppermute | solution.py:55
  15.7 14.3 %copy-start = (bf16[384,1024]{1,0:T(8,128)(2,1)}, bf16[384,1024]{1,0:T(8,128)(2,1)S(1)}, u32[]{:S(2)}) copy-start(bf16[384,1024]{1,0:T(8,128)(2,1)S(1)} %pad_maximum_fusion.refs_0_) | copy-start | bytes 2359300
  15.7 35.8 %collective-permute-start.17 = (bf16[384,1024]{1,0:T(8,128)(2,1)S(1)}, bf16[384,1024]{1,0:T(8,128)(2,1)S(1)}, u32[]{:S(2)}, u32[]{:S(2)}) collective-permute-start(bf16[384,1024]{1,0:T(8,128)(2,1)S(1)} %pad_maximum_fusion.refs_0_), channel_id=1, source_target_pairs={{0,1},{1,0},{2,3},{3,2},{4,5},{5,4},{6,7},{7,6},{8,9},{9,8},{10,11... | collective-permute-start | bytes 2359304 | tf_op jit(solution)/shard_map/ppermute | solution.py:55
  16.8 7.8 %collective-permute-start.10 = (bf16[96,1024]{1,0:T(8,128)(2,1)S(1)}, bf16[96,1024]{1,0:T(8,128)(2,1)S(1)}, u32[]{:S(2)}, u32[]{:S(2)}) collective-permute-start(bf16[96,1024]{1,0:T(8,128)(2,1)S(1)} %collective-permute-done.8), channel_id=1, source_target_pairs={{0,4},{1,5},{2,6},{3,7},{4,0},{5,1},{6,2},{7,3},{8,12},{9,13},{10,... | collective-permute-start | bytes 589832 | tf_op jit(solution)/shard_map/ppermute | solution.py:55
  18.6 7.8 %collective-permute-start.9 = (bf16[96,1024]{1,0:T(8,128)(2,1)S(1)}, bf16[96,1024]{1,0:T(8,128)(2,1)S(1)}, u32[]{:S(2)}, u32[]{:S(2)}) collective-permute-start(bf16[96,1024]{1,0:T(8,128)(2,1)S(1)} %collective-permute-done.8), channel_id=1, source_target_pairs={{0,2},{1,3},{2,0},{3,1},{4,6},{5,7},{6,4},{7,5},{8,10},{9,11},{10,... | collective-permute-start | bytes 589832 | tf_op jit(solution)/shard_map/ppermute | solution.py:55
  20.1 7.3 %collective-permute-start.5 = (bf16[96,1024]{1,0:T(8,128)(2,1)S(1)}, bf16[96,1024]{1,0:T(8,128)(2,1)S(1)}, u32[]{:S(2)}, u32[]{:S(2)}) collective-permute-start(bf16[96,1024]{1,0:T(8,128)(2,1)S(1)} %collective-permute-done.3), channel_id=1, source_target_pairs={{0,4},{1,5},{2,6},{3,7},{4,0},{5,1},{6,2},{7,3},{8,12},{9,13},{10,... | collective-permute-start | bytes 589832 | tf_op jit(solution)/shard_map/ppermute | solution.py:55
  21.1 8.5 %collective-permute-start.4 = (bf16[96,1024]{1,0:T(8,128)(2,1)S(1)}, bf16[96,1024]{1,0:T(8,128)(2,1)S(1)}, u32[]{:S(2)}, u32[]{:S(2)}) collective-permute-start(bf16[96,1024]{1,0:T(8,128)(2,1)S(1)} %collective-permute-done.3), channel_id=1, source_target_pairs={{0,2},{1,3},{2,0},{3,1},{4,6},{5,7},{6,4},{7,5},{8,10},{9,11},{10,... | collective-permute-start | bytes 589832 | tf_op jit(solution)/shard_map/ppermute | solution.py:55
  24.6 5.7 %collective-permute-start.13 = (bf16[96,1024]{1,0:T(8,128)(2,1)S(1)}, bf16[96,1024]{1,0:T(8,128)(2,1)S(1)}, u32[]{:S(2)}, u32[]{:S(2)}) collective-permute-start(bf16[96,1024]{1,0:T(8,128)(2,1)S(1)} %collective-permute-done.3), channel_id=1, source_target_pairs={{0,8},{1,9},{2,10},{3,11},{4,12},{5,13},{6,14},{7,15},{8,0},{9,1},... | collective-permute-start | bytes 589832 | tf_op jit(solution)/shard_map/ppermute | solution.py:55
  26.4 5.8 %collective-permute-start.12 = (bf16[48,1024]{1,0:T(8,128)(2,1)S(1)}, bf16[48,1024]{1,0:T(8,128)(2,1)S(1)}, u32[]{:S(2)}, u32[]{:S(2)}) collective-permute-start(bf16[48,1024]{1,0:T(8,128)(2,1)S(1)} %slice.24), channel_id=1, source_target_pairs={{0,2},{1,3},{2,0},{3,1},{4,6},{5,7},{6,4},{7,5},{8,10},{9,11},{10,... | collective-permute-start | bytes 294920 | tf_op jit(solution)/shard_map/ppermute | solution.py:55
  27.3 4.8 %collective-permute-start.11 = (bf16[48,1024]{1,0:T(8,128)(2,1)S(1)}, bf16[48,1024]{1,0:T(8,128)(2,1)S(1)}, u32[]{:S(2)}, u32[]{:S(2)}) collective-permute-start(bf16[48,1024]{1,0:T(8,128)(2,1)S(1)} %slice.23), channel_id=1, source_target_pairs={{0,4},{1,5},{2,6},{3,7},{4,0},{5,1},{6,2},{7,3},{8,12},{9,13},{10,... | collective-permute-start | bytes 294920 | tf_op jit(solution)/shard_map/ppermute | solution.py:55
  29.6 5.4 %collective-permute-start.7 = (bf16[48,1024]{1,0:T(8,128)(2,1)S(1)}, bf16[48,1024]{1,0:T(8,128)(2,1)S(1)}, u32[]{:S(2)}, u32[]{:S(2)}) collective-permute-start(bf16[48,1024]{1,0:T(8,128)(2,1)S(1)} %slice.22), channel_id=1, source_target_pairs={{0,2},{1,3},{2,0},{3,1},{4,6},{5,7},{6,4},{7,5},{8,10},{9,11},{10,... | collective-permute-start | bytes 294920 | tf_op jit(solution)/shard_map/ppermute | solution.py:55
  30.3 21.9 %copy-start.5 = (bf16[96,1024]{1,0:T(8,128)(2,1)}, bf16[96,1024]{1,0:T(8,128)(2,1)S(1)}, u32[]{:S(2)}) copy-start(bf16[96,1024]{1,0:T(8,128)(2,1)S(1)} %collective-permute-done.13.refs_3_) | copy-start | bytes 589828
  30.3 4.6 %collective-permute-start.6 = (bf16[48,1024]{1,0:T(8,128)(2,1)S(1)}, bf16[48,1024]{1,0:T(8,128)(2,1)S(1)}, u32[]{:S(2)}, u32[]{:S(2)}) collective-permute-start(bf16[48,1024]{1,0:T(8,128)(2,1)S(1)} %slice.21), channel_id=1, source_target_pairs={{0,4},{1,5},{2,6},{3,7},{4,0},{5,1},{6,2},{7,3},{8,12},{9,13},{10,... | collective-permute-start | bytes 294920 | tf_op jit(solution)/shard_map/ppermute | solution.py:55
  32.1 5.1 %collective-permute-start.20 = (bf16[96,1024]{1,0:T(8,128)(2,1)S(1)}, bf16[96,1024]{1,0:T(8,128)(2,1)S(1)}, u32[]{:S(2)}, u32[]{:S(2)}) collective-permute-start(bf16[96,1024]{1,0:T(8,128)(2,1)S(1)} %collective-permute-done.13.refs_3_), channel_id=1, source_target_pairs={{0,1},{1,0},{2,3},{3,2},{4,5},{5,4},{6,7},{7,6},{8,9},{9,8},{10,11... | collective-permute-start | bytes 589832 | tf_op jit(solution)/shard_map/ppermute | solution.py:55
  32.2 20.0 %copy-start.1 = (bf16[384,1024]{1,0:T(8,128)(2,1)}, bf16[384,1024]{1,0:T(8,128)(2,1)S(1)}, u32[]{:S(2)}) copy-start(bf16[384,1024]{1,0:T(8,128)(2,1)S(1)} %constant_dynamic-update-slice_fusion.5.refs_2_) | copy-start | bytes 2359300
  32.2 19.3 %collective-permute-start.19 = (bf16[384,1024]{1,0:T(8,128)(2,1)S(1)}, bf16[384,1024]{1,0:T(8,128)(2,1)S(1)}, u32[]{:S(2)}, u32[]{:S(2)}) collective-permute-start(bf16[384,1024]{1,0:T(8,128)(2,1)S(1)} %constant_dynamic-update-slice_fusion.5.refs_2_), channel_id=1, source_target_pairs={{0,1},{1,0},{2,3},{3,2},{4,5},{5,4},{6,7},{7,6},{8,9},{9,8},{10,11... | collective-permute-start | bytes 2359304 | tf_op jit(solution)/shard_map/ppermute | solution.py:55
  35.0 17.2 %copy-start.2 = (bf16[384,1024]{1,0:T(8,128)(2,1)}, bf16[384,1024]{1,0:T(8,128)(2,1)S(1)}, u32[]{:S(2)}) copy-start(bf16[384,1024]{1,0:T(8,128)(2,1)S(1)} %constant_dynamic-update-slice_fusion.refs_1_) | copy-start | bytes 2359300
  35.0 17.2 %collective-permute-start.18 = (bf16[384,1024]{1,0:T(8,128)(2,1)S(1)}, bf16[384,1024]{1,0:T(8,128)(2,1)}, u32[]{:S(2)}, u32[]{:S(2)}) collective-permute-start(bf16[384,1024]{1,0:T(8,128)(2,1)S(1)} %constant_dynamic-update-slice_fusion.refs_1_), channel_id=1, source_target_pairs={{0,1},{1,0},{2,3},{3,2},{4,5},{5,4},{6,7},{7,6},{8,9},{9,8},{10,11... | collective-permute-start | bytes 2359304 | tf_op jit(solution)/shard_map/ppermute | solution.py:55
  35.0 8.3 %collective-permute-start.16 = (bf16[96,1024]{1,0:T(8,128)(2,1)S(1)}, bf16[96,1024]{1,0:T(8,128)(2,1)S(1)}, u32[]{:S(2)}, u32[]{:S(2)}) collective-permute-start(bf16[96,1024]{1,0:T(8,128)(2,1)S(1)} %collective-permute-done.13.refs_3_), channel_id=1, source_target_pairs={{0,6},{1,7},{2,4},{3,5},{4,2},{5,3},{6,0},{7,1},{8,14},{9,15},{10,... | collective-permute-start | bytes 589832 | tf_op jit(solution)/shard_map/ppermute | solution.py:55
  37.3 14.3 %copy-start.6 = (bf16[96,1024]{1,0:T(8,128)(2,1)}, bf16[96,1024]{1,0:T(8,128)(2,1)S(1)}, u32[]{:S(2)}) copy-start(bf16[96,1024]{1,0:T(8,128)(2,1)S(1)} %collective-permute-done.20.refs_10_) | copy-start | bytes 589828
  37.3 10.2 %collective-permute-start.15 = (bf16[96,1024]{1,0:T(8,128)(2,1)S(1)}, bf16[96,1024]{1,0:T(8,128)(2,1)S(1)}, u32[]{:S(2)}, u32[]{:S(2)}) collective-permute-start(bf16[96,1024]{1,0:T(8,128)(2,1)S(1)} %collective-permute-done.13.refs_3_), channel_id=1, source_target_pairs={{0,4},{1,5},{2,6},{3,7},{4,0},{5,1},{6,2},{7,3},{8,12},{9,13},{10,... | collective-permute-start | bytes 589832 | tf_op jit(solution)/shard_map/ppermute | solution.py:55
  43.4 8.2 %copy-start.7 = (bf16[96,1024]{1,0:T(8,128)(2,1)}, bf16[96,1024]{1,0:T(8,128)(2,1)S(1)}, u32[]{:S(2)}) copy-start(bf16[96,1024]{1,0:T(8,128)(2,1)S(1)} %collective-permute-done.16.refs_6_) | copy-start | bytes 589828
  43.4 6.4 %collective-permute-start.14 = (bf16[96,1024]{1,0:T(8,128)(2,1)S(1)}, bf16[96,1024]{1,0:T(8,128)(2,1)S(1)}, u32[]{:S(2)}, u32[]{:S(2)}) collective-permute-start(bf16[96,1024]{1,0:T(8,128)(2,1)S(1)} %collective-permute-done.13.refs_3_), channel_id=1, source_target_pairs={{0,2},{1,3},{2,0},{3,1},{4,6},{5,7},{6,4},{7,5},{8,10},{9,11},{10,... | collective-permute-start | bytes 589832 | tf_op jit(solution)/shard_map/ppermute | solution.py:55
  47.5 4.1 %copy-start.8 = (bf16[96,1024]{1,0:T(8,128)(2,1)}, bf16[96,1024]{1,0:T(8,128)(2,1)S(1)}, u32[]{:S(2)}) copy-start(bf16[96,1024]{1,0:T(8,128)(2,1)S(1)} %collective-permute-done.15.refs_5_) | copy-start | bytes 589828
  47.5 2.3 %collective-permute-start.23 = (bf16[96,1024]{1,0:T(8,128)(2,1)S(1)}, bf16[96,1024]{1,0:T(8,128)(2,1)S(1)}, u32[]{:S(2)}, u32[]{:S(2)}) collective-permute-start(bf16[96,1024]{1,0:T(8,128)(2,1)S(1)} %collective-permute-done.16.refs_6_), channel_id=1, source_target_pairs={{0,1},{1,0},{2,3},{3,2},{4,5},{5,4},{6,7},{7,6},{8,9},{9,8},{10,11... | collective-permute-start | bytes 589832 | tf_op jit(solution)/shard_map/ppermute | solution.py:55
  49.8 1.8 %copy-start.9 = (bf16[96,1024]{1,0:T(8,128)(2,1)}, bf16[96,1024]{1,0:T(8,128)(2,1)S(1)}, u32[]{:S(2)}) copy-start(bf16[96,1024]{1,0:T(8,128)(2,1)S(1)} %collective-permute-done.14.refs_4_) | copy-start | bytes 589828
  49.8 1.4 %collective-permute-start.22 = (bf16[96,1024]{1,0:T(8,128)(2,1)S(1)}, bf16[96,1024]{1,0:T(8,128)(2,1)S(1)}, u32[]{:S(2)}, u32[]{:S(2)}) collective-permute-start(bf16[96,1024]{1,0:T(8,128)(2,1)S(1)} %collective-permute-done.15.refs_5_), channel_id=1, source_target_pairs={{0,1},{1,0},{2,3},{3,2},{4,5},{5,4},{6,7},{7,6},{8,9},{9,8},{10,11... | collective-permute-start | bytes 589832 | tf_op jit(solution)/shard_map/ppermute | solution.py:55
  49.8 1.8 %copy-start.10 = (bf16[96,1024]{1,0:T(8,128)(2,1)}, bf16[96,1024]{1,0:T(8,128)(2,1)S(1)}, u32[]{:S(2)}) copy-start(bf16[96,1024]{1,0:T(8,128)(2,1)S(1)} %collective-permute-done.23.refs_13_) | copy-start | bytes 589828
  49.8 1.7 %collective-permute-start.21 = (bf16[96,1024]{1,0:T(8,128)(2,1)S(1)}, bf16[96,1024]{1,0:T(8,128)(2,1)S(1)}, u32[]{:S(2)}, u32[]{:S(2)}) collective-permute-start(bf16[96,1024]{1,0:T(8,128)(2,1)S(1)} %collective-permute-done.14.refs_4_), channel_id=1, source_target_pairs={{0,1},{1,0},{2,3},{3,2},{4,5},{5,4},{6,7},{7,6},{8,9},{9,8},{10,11... | collective-permute-start | bytes 589832 | tf_op jit(solution)/shard_map/ppermute | solution.py:55
  51.2 0.7 copy-start.11
  51.5 0.7 copy-start.12
  51.5 0.9 copy-start.3
  52.2 0.9 copy-start.4
